TPU v7x, 32 devices: a whole 2x2x4 slice. The times are simulated.
32 devices in a mesh: rows: 8 (over z, y), cols: 4 (over x, core).
Axes of the slice: x: 2, y: 2, z: 4, core: 2. Of those that a mesh axis runs over, the one named last changes fastest.
Arguments:
- tokens: bfloat16 [8192, 2048], P('rows', 'cols'), may hold values from -6 to 6
- gain_attn: bfloat16 [2048], P('cols'), may hold values from -0.5 to 0.5
- gain_mlp: bfloat16 [2048], P('cols'), may hold values from -0.5 to 0.5
- w_q: bfloat16 [2048, 2048], P('rows', 'cols'), may hold values from -0.125 to 0.125
- w_kv: bfloat16 [2048, 512], P('rows', 'cols'), may hold values from -0.125 to 0.125
- a_qkv: bfloat16 [2048, 256], P('rows'), may hold values from -0.125 to 0.125
- b_q: bfloat16 [256, 2048], P('rows', 'cols'), may hold values from -0.1875 to 0.1875
- b_kv: bfloat16 [256, 512], P('rows', 'cols'), may hold values from -0.1875 to 0.1875
- w_o: bfloat16 [2048, 2048], P('cols', 'rows'), may hold values from -1.5 to 1.5
- a_o: bfloat16 [2048, 256], P('cols', 'rows'), may hold values from -1.5 to 1.5
- b_o: bfloat16 [256, 2048], P('rows', 'cols'), may hold values from -0.1875 to 0.1875
- w_gate: bfloat16 [2048, 16384], P('rows', 'cols'), may hold values from -0.125 to 0.125
- w_up: bfloat16 [2048, 16384], P('rows', 'cols'), may hold values from -0.125 to 0.125
- a_gu: bfloat16 [2048, 256], P('rows'), may hold values from -0.125 to 0.125
- b_gate: bfloat16 [256, 16384], P('rows', 'cols'), may hold values from -0.1875 to 0.1875
- b_up: bfloat16 [256, 16384], P('rows', 'cols'), may hold values from -0.1875 to 0.1875
- w_down: bfloat16 [16384, 2048], P('cols', 'rows'), may hold values from -0.09375 to 0.09375
- a_down: bfloat16 [16384, 256], P('cols', 'rows'), may hold values from -0.09375 to 0.09375
- b_down: bfloat16 [256, 2048], P('rows', 'cols'), may hold values from -0.1875 to 0.1875
- lengths: int32 [8], replicated, may hold values from 256 to 1024, as said below
- teacher: bfloat16 [8192, 2048], P('rows', 'cols'), may hold values from -6 to 6
- out_grad: bfloat16 [8192, 2048], P('rows', 'cols'), may hold values from -6 to 6
Outputs:
- output: bfloat16 [8192, 2048], P('rows', 'cols')
- loss: float32 [1], replicated
- grad_tokens: float32 [8192, 2048], P('rows', 'cols')
- grad_gain_attn: float32 [2048], P('cols')
- grad_gain_mlp: float32 [2048], P('cols')
- grad_w_q: float32 [2048, 2048], P('rows', 'cols')
- grad_w_kv: float32 [2048, 512], P('rows', 'cols')
- grad_a_qkv: float32 [2048, 256], P('rows')
- grad_b_q: float32 [256, 2048], P('rows', 'cols')
- grad_b_kv: float32 [256, 512], P('rows', 'cols')
- grad_w_o: float32 [2048, 2048], P('cols', 'rows')
- grad_a_o: float32 [2048, 256], P('cols', 'rows')
- grad_b_o: float32 [256, 2048], P('rows', 'cols')
- grad_w_gate: float32 [2048, 16384], P('rows', 'cols')
- grad_w_up: float32 [2048, 16384], P('rows', 'cols')
- grad_a_gu: float32 [2048, 256], P('rows')
- grad_b_gate: float32 [256, 16384], P('rows', 'cols')
- grad_b_up: float32 [256, 16384], P('rows', 'cols')
- grad_w_down: float32 [16384, 2048], P('cols', 'rows')
- grad_a_down: float32 [16384, 256], P('cols', 'rows')
- grad_b_down: float32 [256, 2048], P('rows', 'cols')
Inputs may be any that keep to these rules, and one draw needn't show every extreme that they name: `lengths`: each sequence's valid tokens stand at its start; some sequence is valid in all 1024 slots.
All inputs are finite; a program needn't handle non-finite values.
Results may differ from a plain program's by a relative error of at most 0.02.
Values may be sent and summed in bfloat16 or wider, within the bound.
No kernel may reach another device: no remote copies, remote signals or barrier semaphores. Data moves between devices by JAX's collectives and lax.ppermute only.
A program may use at most 320 MiB of HBM per device.

v0:
```python
import jax
import jax.numpy as jnp
from jax import lax
from jax.sharding import PartitionSpec as P

LEN = 1024


NORM_EPS = 1e-06


def product(former, latter):
    return jnp.dot(former, latter, preferred_element_type=jnp.float32)


def left_trans(former, latter):
    return lax.dot_general(
        former, latter, (((0,), (0,)), ((), ())), preferred_element_type=jnp.float32
    )


def right_trans(former, latter):
    return lax.dot_general(
        former, latter, (((1,), (1,)), ((), ())), preferred_element_type=jnp.float32
    )


def angles(length, head_size):
    half_size = head_size // 2
    inverse = 10000.0 ** (-(jnp.arange(half_size, dtype=jnp.float32) * 2.0 / head_size))
    theta = jnp.arange(length, dtype=jnp.float32)[:, None] * inverse[None, :]
    return (jnp.cos(theta), jnp.sin(theta))


def rotate(values_in, cosine_table, sine_table):
    half_size = values_in.shape[-1] // 2
    first_half = values_in[..., :half_size]
    second_half = values_in[..., half_size:]
    return jnp.concatenate(
        [
            first_half * cosine_table - second_half * sine_table,
            second_half * cosine_table + first_half * sine_table,
        ],
        axis=-1,
    )


def allowed_mask(key_count, length):
    row_place = jnp.arange(key_count)[:, None]
    col_place = jnp.arange(key_count)[None, :]
    return ((col_place <= row_place) & (col_place < length))[None]


def attend_forward(packed):
    query_rows, key_rows, value_rows, length = packed
    allowed = allowed_mask(key_rows.shape[0], length)
    scores = jnp.einsum("hqd,kd->hqk", query_rows, key_rows, preferred_element_type=jnp.float32)
    masked = jnp.where(allowed, scores, -1e30)
    largest = jnp.max(masked, axis=-1, keepdims=True)
    exponent = jnp.exp(masked - largest)
    totals = jnp.sum(exponent, axis=-1, keepdims=True)
    probability = (exponent / totals).astype(jnp.bfloat16)
    attended = jnp.einsum(
        "hqk,kd->hqd", probability, value_rows, preferred_element_type=jnp.float32
    )
    return (attended.astype(jnp.bfloat16), (largest + jnp.log(totals))[..., 0])


def attend_backward(packed):
    query_rows, key_rows, value_rows, length, log_total, grad_out = packed
    allowed = allowed_mask(key_rows.shape[0], length)
    scores = jnp.einsum("hqd,kd->hqk", query_rows, key_rows, preferred_element_type=jnp.float32)
    probability = jnp.where(allowed, jnp.exp(scores - log_total[..., None]), 0.0)
    grad_prob = jnp.einsum("hqd,kd->hqk", grad_out, value_rows, preferred_element_type=jnp.float32)
    row_terms = jnp.sum(probability * grad_prob, axis=-1, keepdims=True)
    grad_scores = (probability * (grad_prob - row_terms)).astype(jnp.bfloat16)
    grad_query = jnp.einsum(
        "hqk,kd->hqd", grad_scores, key_rows, preferred_element_type=jnp.float32
    )
    grad_key = jnp.einsum(
        "hqk,hqd->kd", grad_scores, query_rows, preferred_element_type=jnp.float32
    )
    grad_value = jnp.einsum(
        "hqk,hqd->kd",
        probability.astype(jnp.bfloat16),
        grad_out,
        preferred_element_type=jnp.float32,
    )
    return (grad_query, grad_key, grad_value)


def gather_norm(local_rows, gain_local):
    return (
        lax.all_gather(local_rows, "cols", axis=1, tiled=True),
        lax.all_gather(gain_local, "cols", axis=0, tiled=True),
    )


def gather_grads(local_grad):
    return lax.all_gather(local_grad, "cols", axis=1, tiled=True)


def gather_weights(first_w, second_w, third_w, fourth_w, fifth_w, sixth_w, seventh_w, eighth_w):
    return (
        lax.all_gather(first_w, "rows", axis=0, tiled=True),
        lax.all_gather(second_w, "rows", axis=0, tiled=True),
        lax.all_gather(third_w, "rows", axis=0, tiled=True),
        lax.all_gather(fourth_w, "rows", axis=0, tiled=True),
        lax.all_gather(fifth_w, "rows", axis=0, tiled=True),
        lax.all_gather(sixth_w, "rows", axis=1, tiled=True),
        lax.all_gather(seventh_w, "rows", axis=1, tiled=True),
        lax.all_gather(eighth_w, "rows", axis=0, tiled=True),
    )


def scatter_grads(first_g, second_g, third_g, fourth_g, fifth_g, sixth_g, seventh_g, eighth_g):
    return (
        lax.psum_scatter(
            first_g.astype(jnp.bfloat16), "rows", scatter_dimension=0, tiled=True
        ).astype(jnp.float32),
        lax.psum_scatter(
            second_g.astype(jnp.bfloat16), "rows", scatter_dimension=0, tiled=True
        ).astype(jnp.float32),
        lax.psum_scatter(
            third_g.astype(jnp.bfloat16), "rows", scatter_dimension=0, tiled=True
        ).astype(jnp.float32),
        lax.psum_scatter(
            fourth_g.astype(jnp.bfloat16), "rows", scatter_dimension=0, tiled=True
        ).astype(jnp.float32),
        lax.psum_scatter(
            fifth_g.astype(jnp.bfloat16), "rows", scatter_dimension=0, tiled=True
        ).astype(jnp.float32),
        lax.psum_scatter(
            sixth_g.astype(jnp.bfloat16), "rows", scatter_dimension=1, tiled=True
        ).astype(jnp.float32),
        lax.psum_scatter(
            seventh_g.astype(jnp.bfloat16), "rows", scatter_dimension=1, tiled=True
        ).astype(jnp.float32),
        lax.psum_scatter(
            eighth_g.astype(jnp.bfloat16), "rows", scatter_dimension=0, tiled=True
        ).astype(jnp.float32),
    )


def low_rank_sum(partial_sum):
    return lax.psum(partial_sum.astype(jnp.bfloat16), "cols").astype(jnp.float32)


def branch_sum(partial_sum):
    return lax.psum_scatter(
        partial_sum.astype(jnp.bfloat16), "cols", scatter_dimension=1, tiled=True
    ).astype(jnp.float32)


def norm_forward(full_rows, gain_full):
    values_in = full_rows.astype(jnp.float32)
    row_scale = lax.rsqrt(jnp.mean(values_in * values_in, axis=-1, keepdims=True) + NORM_EPS)
    return (
        (values_in * row_scale * (1.0 + gain_full.astype(jnp.float32))).astype(jnp.bfloat16),
        row_scale,
    )


def norm_backward(
    partial_sum, low_grad, low_map, full_rows, local_rows, gain_full, gain_local, row_scale
):
    features = full_rows.shape[1]
    piece_cols = local_rows.shape[1]
    offset = lax.axis_index("cols") * piece_cols
    rows_here = local_rows.astype(jnp.float32)
    factor_here = 1.0 + gain_local.astype(jnp.float32)
    grad_all = lax.psum(partial_sum.astype(jnp.bfloat16), "cols").astype(jnp.float32) + right_trans(
        low_grad, low_map
    )
    rows_all = full_rows.astype(jnp.float32)
    row_dots = jnp.sum(
        grad_all * (1.0 + gain_full.astype(jnp.float32)) * rows_all, axis=-1, keepdims=True
    )
    grad_rows = lax.dynamic_slice_in_dim(grad_all, offset, piece_cols, 1)
    grad_input = (
        row_scale * factor_here * grad_rows
        - rows_here * (row_scale * row_scale * row_scale) * row_dots / features
    )
    grad_gain = jnp.sum(grad_rows * rows_here * row_scale, axis=0)
    return (grad_input, grad_gain)


def geglu(gate_lin, up_lin):
    return jax.nn.gelu(gate_lin, approximate=True) * up_lin


def shards(
    tokens,
    gain_attn,
    gain_mlp,
    w_q,
    w_kv,
    a_qkv,
    b_q,
    b_kv,
    w_o,
    a_o,
    b_o,
    w_gate,
    w_up,
    a_gu,
    b_gate,
    b_up,
    w_down,
    a_down,
    b_down,
    lengths,
    teacher,
    out_grad,
):
    row_count = tokens.shape[0]
    seqs_here = row_count // LEN
    lens_here = lax.dynamic_slice_in_dim(lengths, lax.axis_index("rows") * seqs_here, seqs_here)
    full_x, gain_one_full = gather_norm(tokens, gain_attn)
    normed, scale_one = norm_forward(full_x, gain_one_full)
    full_w_q, full_w_kv, full_a_qkv, full_b_q, full_b_kv, full_w_o, full_a_o, full_b_o = (
        gather_weights(w_q, w_kv, a_qkv, b_q, b_kv, w_o, a_o, b_o)
    )
    lowrank = product(normed, full_a_qkv).astype(jnp.bfloat16)
    q_lin = product(normed, full_w_q) + product(lowrank, full_b_q)
    kv_piece = product(normed, full_w_kv) + product(lowrank, full_b_kv)
    kv_lin = lax.all_gather(kv_piece, "cols", axis=1, tiled=True)
    head_size = kv_lin.shape[1] // 2
    heads_here = q_lin.shape[1] // head_size
    query_scale = head_size ** (-0.5)
    cosine_table, sine_table = angles(LEN, head_size)
    queries = q_lin.reshape(seqs_here, LEN, heads_here, head_size).transpose(0, 2, 1, 3)
    queries = (rotate(queries, cosine_table, sine_table) * query_scale).astype(jnp.bfloat16)
    keys = rotate(
        kv_lin[:, :head_size].reshape(seqs_here, LEN, head_size), cosine_table, sine_table
    ).astype(jnp.bfloat16)
    values = kv_lin[:, head_size:].reshape(seqs_here, LEN, head_size).astype(jnp.bfloat16)
    attended, log_total = lax.map(attend_forward, (queries, keys, values, lens_here))
    attn_rows = attended.transpose(0, 2, 1, 3).reshape(row_count, heads_here * head_size)
    low_o = low_rank_sum(product(attn_rows, full_a_o)).astype(jnp.bfloat16)
    branch_one = branch_sum(product(attn_rows, full_w_o)) + product(low_o, full_b_o)
    middle = tokens.astype(jnp.float32) + branch_one
    middle_low = middle.astype(jnp.bfloat16)
    full_mid, gain_two_full = gather_norm(middle_low, gain_mlp)
    normed_two, scale_two = norm_forward(full_mid, gain_two_full)
    (
        full_w_gate,
        full_w_up,
        full_a_gu,
        full_b_gate,
        full_b_up,
        full_w_down,
        full_a_down,
        full_b_down,
    ) = gather_weights(w_gate, w_up, a_gu, b_gate, b_up, w_down, a_down, b_down)
    low_g = product(normed_two, full_a_gu).astype(jnp.bfloat16)
    gate_lin = product(normed_two, full_w_gate) + product(low_g, full_b_gate)
    up_lin = product(normed_two, full_w_up) + product(low_g, full_b_up)
    hidden = geglu(gate_lin, up_lin).astype(jnp.bfloat16)
    low_d = low_rank_sum(product(hidden, full_a_down)).astype(jnp.bfloat16)
    branch_two = branch_sum(product(hidden, full_w_down)) + product(low_d, full_b_down)
    result = middle + branch_two
    positions = jnp.arange(LEN)
    valid_rows = (positions[None, :] < lens_here[:, None]).reshape(row_count, 1).astype(jnp.float32)
    valid_count = jnp.sum(lengths).astype(jnp.float32)
    error_rows = result - teacher.astype(jnp.float32)
    total_square = lax.psum(jnp.sum(error_rows * error_rows * valid_rows), ("rows", "cols"))
    loss_value = (total_square / (2.0 * valid_count)).reshape(1)
    seed_grad = (
        out_grad.astype(jnp.float32)
        + row_count * lax.axis_size("rows") / valid_count * error_rows * valid_rows
    )
    (
        full_w_gate,
        full_w_up,
        full_a_gu,
        full_b_gate,
        full_b_up,
        full_w_down,
        full_a_down,
        full_b_down,
    ) = gather_weights(w_gate, w_up, a_gu, b_gate, b_up, w_down, a_down, b_down)
    grad_two = seed_grad.astype(jnp.bfloat16)
    grad_two_full = gather_grads(grad_two)
    grad_low_d = low_rank_sum(right_trans(grad_two, full_b_down)).astype(jnp.bfloat16)
    d_hidden = right_trans(grad_two_full, full_w_down) + right_trans(grad_low_d, full_a_down)
    grad_w_down = left_trans(hidden, grad_two_full)
    grad_a_down = left_trans(hidden, grad_low_d)
    grad_b_down = left_trans(low_d, grad_two)
    geglu_value, geglu_back = jax.vjp(geglu, gate_lin, up_lin)
    d_gate, d_up = geglu_back(d_hidden)
    d_gate = d_gate.astype(jnp.bfloat16)
    d_up = d_up.astype(jnp.bfloat16)
    grad_w_gate = left_trans(normed_two, d_gate)
    grad_w_up = left_trans(normed_two, d_up)
    grad_b_gate = left_trans(low_g, d_gate)
    grad_b_up = left_trans(low_g, d_up)
    grad_low_g = low_rank_sum(
        right_trans(d_gate, full_b_gate) + right_trans(d_up, full_b_up)
    ).astype(jnp.bfloat16)
    grad_a_gu = left_trans(normed_two, grad_low_g)
    part_two = right_trans(d_gate, full_w_gate) + right_trans(d_up, full_w_up)
    mlp_grads = scatter_grads(
        grad_w_gate,
        grad_w_up,
        grad_a_gu,
        grad_b_gate,
        grad_b_up,
        grad_w_down,
        grad_a_down,
        grad_b_down,
    )
    d_norm_two, gain_two_grad = norm_backward(
        part_two, grad_low_g, full_a_gu, full_mid, middle_low, gain_two_full, gain_mlp, scale_two
    )
    d_middle = seed_grad + d_norm_two
    full_w_q, full_w_kv, full_a_qkv, full_b_q, full_b_kv, full_w_o, full_a_o, full_b_o = (
        gather_weights(w_q, w_kv, a_qkv, b_q, b_kv, w_o, a_o, b_o)
    )
    grad_one = d_middle.astype(jnp.bfloat16)
    grad_one_full = gather_grads(grad_one)
    grad_low_o = low_rank_sum(right_trans(grad_one, full_b_o)).astype(jnp.bfloat16)
    d_attended = (right_trans(grad_one_full, full_w_o) + right_trans(grad_low_o, full_a_o)).astype(
        jnp.bfloat16
    )
    grad_w_o = left_trans(attn_rows, grad_one_full)
    grad_a_o = left_trans(attn_rows, grad_low_o)
    grad_b_o = left_trans(low_o, grad_one)
    d_heads = d_attended.reshape(seqs_here, LEN, heads_here, head_size).transpose(0, 2, 1, 3)
    d_queries, d_keys, d_values = lax.map(
        attend_backward, (queries, keys, values, lens_here, log_total, d_heads)
    )
    d_q_lin = rotate(d_queries * query_scale, cosine_table, -sine_table)
    d_q_lin = (
        d_q_lin.transpose(0, 2, 1, 3)
        .reshape(row_count, heads_here * head_size)
        .astype(jnp.bfloat16)
    )
    d_key_rows = rotate(d_keys, cosine_table, -sine_table).reshape(row_count, head_size)
    d_kv_part = jnp.concatenate([d_key_rows, d_values.reshape(row_count, head_size)], axis=1)
    d_kv_lin = lax.psum_scatter(
        d_kv_part.astype(jnp.bfloat16), "cols", scatter_dimension=1, tiled=True
    )
    grad_w_q = left_trans(normed, d_q_lin)
    grad_b_q = left_trans(lowrank, d_q_lin)
    grad_w_kv = left_trans(normed, d_kv_lin)
    grad_b_kv = left_trans(lowrank, d_kv_lin)
    grad_low = low_rank_sum(
        right_trans(d_q_lin, full_b_q) + right_trans(d_kv_lin, full_b_kv)
    ).astype(jnp.bfloat16)
    grad_a_qkv = left_trans(normed, grad_low)
    part_one = right_trans(d_q_lin, full_w_q) + right_trans(d_kv_lin, full_w_kv)
    attn_grads = scatter_grads(
        grad_w_q, grad_w_kv, grad_a_qkv, grad_b_q, grad_b_kv, grad_w_o, grad_a_o, grad_b_o
    )
    d_norm_one, gain_one_grad = norm_backward(
        part_one, grad_low, full_a_qkv, full_x, tokens, gain_one_full, gain_attn, scale_one
    )
    grad_tokens = d_middle + d_norm_one
    gain_one_sum, gain_two_sum = lax.psum((gain_one_grad, gain_two_grad), "rows")
    return (
        result.astype(jnp.bfloat16),
        loss_value,
        grad_tokens,
        gain_one_sum,
        gain_two_sum,
        attn_grads[0],
        attn_grads[1],
        attn_grads[2],
        attn_grads[3],
        attn_grads[4],
        attn_grads[5],
        attn_grads[6],
        attn_grads[7],
        mlp_grads[0],
        mlp_grads[1],
        mlp_grads[2],
        mlp_grads[3],
        mlp_grads[4],
        mlp_grads[5],
        mlp_grads[6],
        mlp_grads[7],
    )


def solution(mesh):
    in_specs = (
        P("rows", "cols"),
        P("cols"),
        P("cols"),
        P("rows", "cols"),
        P("rows", "cols"),
        P("rows", None),
        P("rows", "cols"),
        P("rows", "cols"),
        P("cols", "rows"),
        P("cols", "rows"),
        P("rows", "cols"),
        P("rows", "cols"),
        P("rows", "cols"),
        P("rows", None),
        P("rows", "cols"),
        P("rows", "cols"),
        P("cols", "rows"),
        P("cols", "rows"),
        P("rows", "cols"),
        P(),
        P("rows", "cols"),
        P("rows", "cols"),
    )
    out_specs = (
        P("rows", "cols"),
        P(),
        P("rows", "cols"),
        P("cols"),
        P("cols"),
        P("rows", "cols"),
        P("rows", "cols"),
        P("rows", None),
        P("rows", "cols"),
        P("rows", "cols"),
        P("cols", "rows"),
        P("cols", "rows"),
        P("rows", "cols"),
        P("rows", "cols"),
        P("rows", "cols"),
        P("rows", None),
        P("rows", "cols"),
        P("rows", "cols"),
        P("cols", "rows"),
        P("cols", "rows"),
        P("rows", "cols"),
    )
    return jax.shard_map(shards, mesh=mesh, in_specs=in_specs, out_specs=out_specs, check_vma=False)
```

profile of v0, /device:TPU:0, one launch (start us, length us, event | category | flops | bytes accessed | tf_op | source)
XLA Modules:
  0.0 3529.8 jit_solution(9620337408967872411)
XLA Ops:
  10.1 6.2 all-gather
  16.3 31.6 all_gather.91
  47.9 31.9 all_gather.90
  98.2 31.7 all_gather.89
  129.9 31.6 all_gather.94
  191.1 28.8 all-gather.26.cloned.1.call-done
  219.9 6.0 convolution_convert_fusion.7
  226.6 31.0 all_gather.95
  257.7 44.1 %reduce-scatter.22.cloned.1.call-done = bf16[1024,512]{1,0:T(8,128)(2,1)} async-done(((bf16[1024,2048]{1,0:T(8,128)(2,1)}), bf16[1024,512]{1,0:T(8,128)(2,1)}) %reduce-scatter.22.cloned.1.call-update) | async-done | bytes 1048592 | tf_op jit(solution)/shard_map/reduce_scatter | solution.py:150
  315.3 24.8 all-gather.28.cloned.1.call-done
  343.7 38.8 %all-gather.32.cloned.1.call-done = bf16[2048,256]{1,0:T(8,128)(2,1)} async-done(((bf16[256,256]{1,0:T(8,128)(2,1)}), bf16[2048,256]{1,0:T(8,128)(2,1)}) %all-gather.32.cloned.1.call-update) | async-done | bytes 1048592 | tf_op jit(solution)/shard_map/all_gather | solution.py:107
  386.3 46.0 %all-gather.38.cloned.1.call-done = bf16[256,4096]{1,0:T(8,128)(2,1)} async-done(((bf16[32,4096]{1,0:T(8,128)(2,1)}), bf16[256,4096]{1,0:T(8,128)(2,1)}) %all-gather.38.cloned.1.call-update) | async-done | bytes 2097168 | tf_op jit(solution)/shard_map/all_gather | solution.py:109
  432.3 9.8 fusion.87
  442.1 40.0 %all-gather.34.cloned.1.call-done = bf16[256,4096]{1,0:T(8,128)(2,1)} async-done(((bf16[32,4096]{1,0:T(8,128)(2,1)}), bf16[256,4096]{1,0:T(8,128)(2,1)}) %all-gather.34.cloned.1.call-update) | async-done | bytes 2097168 | tf_op jit(solution)/shard_map/all_gather | solution.py:108
  482.1 11.0 fusion.86
  493.1 216.8 %all-gather.30.cloned.1.call-done = bf16[2048,4096]{1,0:T(8,128)(2,1)} async-done(((bf16[256,4096]{1,0:T(8,128)(2,1)}), bf16[2048,4096]{1,0:T(8,128)(2,1)}) %all-gather.30.cloned.1.call-update) | async-done | bytes 16777232 | tf_op jit(solution)/shard_map/all_gather | solution.py:105
  709.9 28.5 convolution_add_fusion.2
  738.4 199.1 %all-gather.36.cloned.1.call-done = bf16[2048,4096]{1,0:T(8,128)(2,1)} async-done(((bf16[256,4096]{1,0:T(8,128)(2,1)}), bf16[2048,4096]{1,0:T(8,128)(2,1)}) %all-gather.36.cloned.1.call-update) | async-done | bytes 16777232 | tf_op jit(solution)/shard_map/all_gather | solution.py:106
  937.5 35.0 multiply_convert_fusion.1
  972.5 14.3 all-gather.42.cloned.1.call-done
  986.8 7.1 convolution_convert_fusion.15
  994.0 220.5 %all-gather.40.cloned.1.call-done = bf16[4096,2048]{1,0:T(8,128)(2,1)} async-done(((bf16[4096,256]{1,0:T(8,128)(2,1)}), bf16[4096,2048]{1,0:T(8,128)(2,1)}) %all-gather.40.cloned.1.call-update) | async-done | bytes 16777232 | tf_op jit(solution)/shard_map/all_gather | solution.py:110
  1214.5 23.6 convolution_convert_fusion.6
  1240.8 30.8 all_gather.105
  1271.7 24.9 reduce-scatter.24.cloned.1.call-done
  1302.8 32.8 all-reduce.14.cloned.1.call-done
  1335.6 9.7 fusion.88
  1345.3 26.4 all-gather.44.cloned.1.call-done
  1371.7 39.7 %multiply_convert_fusion = (bf16[1024,4096]{1,0:T(8,128)(2,1)}, bf16[1024,4096]{1,0:T(8,128)(2,1)}) fusion(f32[1024,4096]{1,0:T(8,128)} %convolution_add_fusion.2, f32[1024,4096]{1,0:T(8,128)} %get-tuple-element.107, f32[1024,4096]{1,0:T(8,128)} %fusion.88, bf16[1024,2048]{1,0:T(8,128)(2,1)} %all-gather.44.cloned.1.call-done, ...), kind=kOutput, calls=%fused_computation.9 | convolution fusion | flops 17284726784 | bytes 88080384 | tf_op jit(solution)/shard_map/dot_general | solution.py:23
  1411.4 24.7 fusion.89
  1439.5 22.2 add_convert_fusion.1
  1465.5 93.5 %all-reduce.20.cloned.1.call-done = (bf16[1024,2048]{1,0:T(8,128)(2,1)}, bf16[1024,256]{1,0:T(8,128)(2,1)}) async-done(((bf16[1024,2048]{1,0:T(8,128)(2,1)}, bf16[1024,256]{1,0:T(8,128)(2,1)}), (bf16[1024,2048]{1,0:T(8,128)(2,1)}, bf16[1024,256]{1,0:T(8,128)(2,1)})) %all-reduce.20.cloned.1.call-update) | async-done | bytes 4718608 | tf_op jit(solution)/shard_map/psum | solution.py:172
  1559.1 5.8 fusion.14
  1572.1 31.9 all-gather.46.cloned.1.call-done
  1609.2 31.1 all-reduce.16.cloned.1.call-done
  1663.8 7.4 fusion.92
  1671.2 12.2 reduce-scatter.58.cloned.1.call-done
  1685.5 6.8 add_convert_fusion
  1694.9 7.9 convolution_convert_fusion.3
  1708.1 7.1 convolution_convert_fusion.4
  1715.3 7.3 convolution_convert_fusion.5
  1734.4 5.8 convolution_convert_fusion.8
  1740.5 5.9 convolution_convert_fusion.9
  1746.5 40.0 %all-reduce.18.cloned.1.call-done = (bf16[1024,2048]{1,0:T(8,128)(2,1)}, bf16[1024,256]{1,0:T(8,128)(2,1)}) async-done(((bf16[1024,2048]{1,0:T(8,128)(2,1)}, bf16[1024,256]{1,0:T(8,128)(2,1)}), (bf16[1024,2048]{1,0:T(8,128)(2,1)}, bf16[1024,256]{1,0:T(8,128)(2,1)})) %all-reduce.18.cloned.1.call-update) | async-done | bytes 4718608 | tf_op jit(solution)/shard_map/psum | solution.py:172
  1791.2 24.7 convolution_convert_fusion
  1816.2 25.6 convolution_convert_fusion.2
  1842.1 25.7 convolution_convert_fusion.1
  1869.9 53.6 %reduce-scatter.54.cloned.1.call-done = bf16[4096,32]{0,1:T(8,128)(2,1)} async-done(((bf16[4096,256]{0,1:T(8,128)(2,1)}), bf16[4096,32]{0,1:T(8,128)(2,1)}) %reduce-scatter.54.cloned.1.call-update) | async-done | bytes 262160 | tf_op jit(solution)/shard_map/reduce_scatter | solution.py:136
  1925.3 40.0 %psum.79 = f32[]{:T(128)} all-reduce(f32[]{:T(128)} %get-tuple-element.85), channel_id=1, replica_groups=mesh['rows'=8,'cols'=4] {'rows','cols'}, use_global_device_ids=true, to_apply=%region_9.10 | all-reduce | flops 1 | bytes 8 | tf_op jit(solution)/shard_map/psum | solution.py:267
  1966.0 22.5 reduce-scatter.40.cloned.1.call-done
  1989.9 63.6 %reduce-scatter.38.cloned.1.call-done = bf16[512,32]{0,1:T(8,128)(2,1)} async-done(((bf16[512,256]{0,1:T(8,128)(2,1)}), bf16[512,32]{0,1:T(8,128)(2,1)}) %reduce-scatter.38.cloned.1.call-update) | async-done | bytes 32784 | tf_op jit(solution)/shard_map/reduce_scatter | solution.py:136
  2054.9 69.6 %reduce-scatter.50.cloned.1.call-done = bf16[32,4096]{1,0:T(8,128)(2,1)} async-done(((bf16[256,4096]{1,0:T(8,128)(2,1)}), bf16[32,4096]{1,0:T(8,128)(2,1)}) %reduce-scatter.50.cloned.1.call-update) | async-done | bytes 262160 | tf_op jit(solution)/shard_map/reduce_scatter | solution.py:130
  2126.3 69.2 %reduce-scatter.48.cloned.1.call-done = bf16[32,4096]{1,0:T(8,128)(2,1)} async-done(((bf16[256,4096]{1,0:T(8,128)(2,1)}), bf16[32,4096]{1,0:T(8,128)(2,1)}) %reduce-scatter.48.cloned.1.call-update) | async-done | bytes 262160 | tf_op jit(solution)/shard_map/reduce_scatter | solution.py:127
  2197.2 64.9 %reduce-scatter.46.cloned.1.call-done = bf16[256,256]{1,0:T(8,128)(2,1)} async-done(((bf16[2048,256]{1,0:T(8,128)(2,1)}), bf16[256,256]{1,0:T(8,128)(2,1)}) %reduce-scatter.46.cloned.1.call-update) | async-done | bytes 131088 | tf_op jit(solution)/shard_map/reduce_scatter | solution.py:124
  2263.7 63.4 %reduce-scatter.32.cloned.1.call-done = bf16[32,512]{1,0:T(8,128)(2,1)} async-done(((bf16[256,512]{1,0:T(8,128)(2,1)}), bf16[32,512]{1,0:T(8,128)(2,1)}) %reduce-scatter.32.cloned.1.call-update) | async-done | bytes 32784 | tf_op jit(solution)/shard_map/reduce_scatter | solution.py:127
  2328.5 64.0 %reduce-scatter.34.cloned.1.call-done = bf16[32,128]{1,0:T(8,128)(2,1)} async-done(((bf16[256,128]{1,0:T(8,128)(2,1)}), bf16[32,128]{1,0:T(8,128)(2,1)}) %reduce-scatter.34.cloned.1.call-update) | async-done | bytes 8208 | tf_op jit(solution)/shard_map/reduce_scatter | solution.py:130
  2393.8 64.4 %reduce-scatter.28.cloned.1.call-done = bf16[256,128]{1,0:T(8,128)(2,1)} async-done(((bf16[2048,128]{1,0:T(8,128)(2,1)}), bf16[256,128]{1,0:T(8,128)(2,1)}) %reduce-scatter.28.cloned.1.call-update) | async-done | bytes 65552 | tf_op jit(solution)/shard_map/reduce_scatter | solution.py:121
  2459.8 69.9 %reduce-scatter.36.cloned.1.call-done = bf16[512,256]{1,0:T(8,128)(2,1)} async-done(((bf16[512,2048]{1,0:T(8,128)(2,1)}), bf16[512,256]{1,0:T(8,128)(2,1)}) %reduce-scatter.36.cloned.1.call-update) | async-done | bytes 262160 | tf_op jit(solution)/shard_map/reduce_scatter | solution.py:133
  2531.5 69.5 %reduce-scatter.26.cloned.1.call-done = bf16[256,512]{1,0:T(8,128)(2,1)} async-done(((bf16[2048,512]{1,0:T(8,128)(2,1)}), bf16[256,512]{1,0:T(8,128)(2,1)}) %reduce-scatter.26.cloned.1.call-update) | async-done | bytes 262160 | tf_op jit(solution)/shard_map/reduce_scatter | solution.py:118
  2610.5 19.7 all-reduce
  2630.2 37.9 %reduce-scatter.30.cloned.1.call-done = bf16[256,256]{1,0:T(8,128)(2,1)} async-done(((bf16[2048,256]{1,0:T(8,128)(2,1)}), bf16[256,256]{1,0:T(8,128)(2,1)}) %reduce-scatter.30.cloned.1.call-update) | async-done | bytes 131088 | tf_op jit(solution)/shard_map/reduce_scatter | solution.py:124
  2669.8 281.4 %reduce-scatter.52.cloned.1.call-done = bf16[4096,256]{1,0:T(8,128)(2,1)} async-done(((bf16[4096,2048]{1,0:T(8,128)(2,1)}), bf16[4096,256]{1,0:T(8,128)(2,1)}) %reduce-scatter.52.cloned.1.call-update) | async-done | bytes 2097168 | tf_op jit(solution)/shard_map/reduce_scatter | solution.py:133
  2955.1 279.0 %reduce-scatter.42.cloned.1.call-done = bf16[256,4096]{1,0:T(8,128)(2,1)} async-done(((bf16[2048,4096]{1,0:T(8,128)(2,1)}), bf16[256,4096]{1,0:T(8,128)(2,1)}) %reduce-scatter.42.cloned.1.call-update) | async-done | bytes 2097168 | tf_op jit(solution)/shard_map/reduce_scatter | solution.py:118
  3238.2 279.0 %reduce-scatter.44.cloned.1.call-done = bf16[256,4096]{1,0:T(8,128)(2,1)} async-done(((bf16[2048,4096]{1,0:T(8,128)(2,1)}), bf16[256,4096]{1,0:T(8,128)(2,1)}) %reduce-scatter.44.cloned.1.call-update) | async-done | bytes 2097168 | tf_op jit(solution)/shard_map/reduce_scatter | solution.py:121
  (339 shorter events, 191.1 us)
Async XLA Ops:
  7.2 72.6 %all-gather.18.cloned.1.call-start = ((), (), s32[]{:S(2)}) async-start(), calls=%async_computation.19 | async-start | bytes 5242880 | tf_op jit(solution)/shard_map/all_gather | solution.py:94
  7.9 81.9 %all-gather.22.cloned.1.call-start = ((), (), s32[]{:S(2)}) async-start(), calls=%async_computation.21 | async-start | bytes 1179648 | tf_op jit(solution)/shard_map/all_gather | solution.py:107
  8.7 156.1 %all-gather.20.cloned.1.call-start = ((), (), s32[]{:S(2)}) async-start(), calls=%async_computation.20 | async-start | bytes 2359296 | tf_op jit(solution)/shard_map/all_gather | solution.py:105
  9.4 167.2 %all-gather.24.cloned.1.call-start = ((), (), s32[]{:S(2)}) async-start(), calls=%async_computation.22 | async-start | bytes 2621440 | tf_op jit(solution)/shard_map/all_gather | solution.py:227
  47.9 45.9 %copy-start.46 = (bf16[256,128]{1,0:T(8,128)(2,1)}, bf16[256,128]{1,0:T(8,128)(2,1)S(1)}, u32[]{:S(2)}) copy-start(bf16[256,128]{1,0:T(8,128)(2,1)S(1)} %all_gather.91) | copy-start | bytes 196612
  47.9 38.9 %copy-start.54 = (f32[4,1,512]{2,1,0:T(1,128)}, f32[4,1,512]{2,1,0:T(1,128)S(1)}, u32[]{:S(2)}) copy-start(f32[4,1,512]{2,1,0:T(1,128)S(1)} %convert_add_fusion.4) | copy-start | bytes 24580
  93.7 76.4 %copy-start.15 = (bf16[1024,256]{1,0:T(8,128)(2,1)}, bf16[1024,256]{1,0:T(8,128)(2,1)S(1)}, u32[]{:S(2)}) copy-start(bf16[1024,256]{1,0:T(8,128)(2,1)S(1)} %convolution_convert_fusion.18) | copy-start | bytes 1572868
  94.1 35.8 %copy-start.67 = (bf16[512,32]{0,1:T(8,128)(2,1)S(1)}, bf16[512,32]{0,1:T(8,128)(2,1)}, u32[]{:S(2)}) copy-start(bf16[512,32]{0,1:T(8,128)(2,1)} %param.31) | copy-start | bytes 98308
  96.2 123.6 %all-gather.26.cloned.1.call-start = ((), (), s32[]{:S(2)}) async-start(), calls=%async_computation.23 | async-start | bytes 2359296 | tf_op jit(solution)/shard_map/all_gather | solution.py:110
  96.8 160.8 %all-reduce.10.cloned.1.call-start = ((), (), s32[]{:S(2)}) async-start(), calls=%async_computation.25 | async-start | bytes 1048576 | tf_op jit(solution)/shard_map/psum | solution.py:146
  96.9 81.1 %copy-start.75 = (f32[128]{0:T(128)}, f32[128]{0:T(128)S(1)}, u32[]{:S(2)}) copy-start(f32[128]{0:T(128)S(1)} %negate_power_fusion) | copy-start | bytes 1540
  129.9 40.2 %copy-start.28 = (bf16[256,512]{1,0:T(8,128)(2,1)}, bf16[256,512]{1,0:T(8,128)(2,1)S(1)}, u32[]{:S(2)}) copy-start(bf16[256,512]{1,0:T(8,128)(2,1)S(1)} %all_gather.89) | copy-start | bytes 786436
  161.5 28.2 copy-start.33
  189.7 36.2 %copy-start.25 = (bf16[2,1024,256]{1,2,0:T(8,128)(2,1)}, bf16[2,1024,256]{1,2,0:T(8,128)(2,1)S(1)}, u32[]{:S(2)}) copy-start(bf16[2,1024,256]{1,2,0:T(8,128)(2,1)S(1)} %fusion.37) | copy-start | bytes 3145732
  191.0 110.8 %reduce-scatter.22.cloned.1.call-start = ((), (), s32[]{:S(2)}) async-start(), calls=%async_computation.24 | async-start | bytes 5242880 | tf_op jit(solution)/shard_map/reduce_scatter | solution.py:150
  225.9 76.0 %copy-start.13 = (bf16[1024,512]{1,0:T(8,128)(2,1)S(1)}, bf16[1024,512]{1,0:T(8,128)(2,1)}, u32[]{:S(2)}) copy-start(bf16[1024,512]{1,0:T(8,128)(2,1)} %param.22) | copy-start | bytes 3145732
  225.9 114.1 %all-gather.28.cloned.1.call-start = ((), (), s32[]{:S(2)}) async-start(), calls=%async_computation.26 | async-start | bytes 5242880 | tf_op jit(solution)/shard_map/all_gather | solution.py:94
  257.7 50.4 %copy-start.30 = (bf16[256,512]{1,0:T(8,128)(2,1)}, bf16[256,512]{1,0:T(8,128)(2,1)S(1)}, u32[]{:S(2)}) copy-start(bf16[256,512]{1,0:T(8,128)(2,1)S(1)} %all_gather.95) | copy-start | bytes 786436
  305.4 77.1 %all-gather.32.cloned.1.call-start = ((), (), s32[]{:S(2)}) async-start(), calls=%async_computation.28 | async-start | bytes 1179648 | tf_op jit(solution)/shard_map/all_gather | solution.py:107
  306.2 126.1 %all-gather.38.cloned.1.call-start = ((), (), s32[]{:S(2)}) async-start(), calls=%async_computation.31 | async-start | bytes 2359296 | tf_op jit(solution)/shard_map/all_gather | solution.py:109
  306.7 175.3 %all-gather.34.cloned.1.call-start = ((), (), s32[]{:S(2)}) async-start(), calls=%async_computation.29 | async-start | bytes 2359296 | tf_op jit(solution)/shard_map/all_gather | solution.py:108
  307.5 402.4 %all-gather.30.cloned.1.call-start = ((), (), s32[]{:S(2)}) async-start(), calls=%async_computation.27 | async-start | bytes 18874368 | tf_op jit(solution)/shard_map/all_gather | solution.py:105
  308.1 629.4 %all-gather.36.cloned.1.call-start = ((), (), s32[]{:S(2)}) async-start(), calls=%async_computation.30 | async-start | bytes 18874368 | tf_op jit(solution)/shard_map/all_gather | solution.py:106
  308.8 678.0 %all-gather.42.cloned.1.call-start = ((), (), s32[]{:S(2)}) async-start(), calls=%async_computation.34 | async-start | bytes 2359296 | tf_op jit(solution)/shard_map/all_gather | solution.py:111
  309.4 905.2 %all-gather.40.cloned.1.call-start = ((), (), s32[]{:S(2)}) async-start(), calls=%async_computation.32 | async-start | bytes 18874368 | tf_op jit(solution)/shard_map/all_gather | solution.py:110
  310.0 961.7 %all-reduce.12.cloned.1.call-start = ((), (), s32[]{:S(2)}) async-start(), calls=%async_computation.35 | async-start | bytes 1048576 | tf_op jit(solution)/shard_map/psum | solution.py:146
  315.3 622.3 %copy-start.64 = (f32[4,1,512]{2,1,0:T(1,128)}, f32[4,1,512]{2,1,0:T(1,128)S(1)}, u32[]{:S(2)}) copy-start(f32[4,1,512]{2,1,0:T(1,128)S(1)} %convert_add_fusion.3) | copy-start | bytes 24580
  343.7 593.8 %copy-start.71 = (f32[1024]{0:T(1024)}, f32[1024]{0:T(1024)S(1)}, u32[]{:S(2)}) copy-start(f32[1024]{0:T(1024)S(1)} %get-tuple-element.98) | copy-start | bytes 12292
  386.3 95.8 %copy-start.7 = (bf16[1024,256]{1,0:T(8,128)(2,1)}, bf16[1024,256]{1,0:T(8,128)(2,1)S(1)}, u32[]{:S(2)}) copy-start(bf16[1024,256]{1,0:T(8,128)(2,1)S(1)} %convolution_convert_fusion.17) | copy-start | bytes 1572868
  994.0 302.6 %reduce-scatter.24.cloned.1.call-start = ((), (), s32[]{:S(2)}) async-start(), calls=%async_computation.33 | async-start | bytes 5242880 | tf_op jit(solution)/shard_map/reduce_scatter | solution.py:150
  1238.2 58.4 %copy-start.17 = (f32[1024,512]{1,0:T(8,128)S(1)}, f32[1024,512]{1,0:T(8,128)}, u32[]{:S(2)}) copy-start(f32[1024,512]{1,0:T(8,128)} %get-tuple-element.105) | copy-start | bytes 6291460
  1238.2 97.4 %all-reduce.14.cloned.1.call-start = ((), (), s32[]{:S(2)}) async-start(), calls=%async_computation.37 | async-start | bytes 1048576 | tf_op jit(solution)/shard_map/psum | solution.py:146
  1240.8 59.9 %copy-start.58 = (f32[1024]{0:T(1024)}, f32[1024]{0:T(1024)S(1)}, u32[]{:S(2)}) copy-start(f32[1024]{0:T(1024)S(1)} %fusion.66) | copy-start | bytes 12292
  1300.7 34.9 copy-start.41
  1302.0 69.7 %all-gather.44.cloned.1.call-start = ((), (), s32[]{:S(2)}) async-start(), calls=%async_computation.36 | async-start | bytes 5242880 | tf_op jit(solution)/shard_map/all_gather | solution.py:100
  1302.7 256.3 %all-reduce.20.cloned.1.call-start = ((), (), s32[]{:S(2)}) async-start(), calls=%async_computation.58 | async-start | bytes 9437184 | tf_op jit(solution)/shard_map/psum | solution.py:172
  1411.4 24.7 copy-start.40
  1464.8 94.2 %copy-start.45 = (bf16[2048,256]{1,0:T(8,128)(2,1)S(1)}, bf16[2048,256]{1,0:T(8,128)(2,1)}, u32[]{:S(2)}) copy-start(bf16[2048,256]{1,0:T(8,128)(2,1)} %all-gather.32.cloned.1.call-done) | copy-start | bytes 3145732
  1464.8 94.2 %copy-start.65 = (f32[4,1,512]{2,1,0:T(1,128)S(1)}, f32[4,1,512]{2,1,0:T(1,128)}, u32[]{:S(2)}) copy-start(f32[4,1,512]{2,1,0:T(1,128)} %copy-done.64) | copy-start | bytes 24580
  1464.8 139.1 %all-gather.46.cloned.1.call-start = ((), (), s32[]{:S(2)}) async-start(), calls=%async_computation.38 | async-start | bytes 5242880 | tf_op jit(solution)/shard_map/all_gather | solution.py:100
  1569.2 71.1 %all-reduce.16.cloned.1.call-start = ((), (), s32[]{:S(2)}) async-start(), calls=%async_computation.39 | async-start | bytes 1048576 | tf_op jit(solution)/shard_map/psum | solution.py:146
  1572.0 68.3 %copy-start.34 = (bf16[512,256]{0,1:T(8,128)(2,1)S(1)}, bf16[512,256]{0,1:T(8,128)(2,1)}, u32[]{:S(2)}) copy-start(bf16[512,256]{0,1:T(8,128)(2,1)} %copy-done.33) | copy-start | bytes 786436
  1572.0 70.0 %copy-start.3 = (pred[1024,1024]{0,1:T(8,128)(4,1)S(1)}, pred[1024,1024]{0,1:T(8,128)(4,1)}, u32[]{:S(2)}) copy-start(pred[1024,1024]{0,1:T(8,128)(4,1)} %copy-done.2) | copy-start | bytes 3145732
  1572.0 111.4 %reduce-scatter.58.cloned.1.call-start = ((), (), s32[]{:S(2)}) async-start(), calls=%async_computation.56 | async-start | bytes 1310720
  1658.4 128.1 %all-reduce.18.cloned.1.call-start = ((), (), s32[]{:S(2)}) async-start(), calls=%async_computation.57 | async-start | bytes 9437184 | tf_op jit(solution)/shard_map/psum | solution.py:172
  1692.3 176.2 %reduce-scatter.56.cloned.1.call-start = ((), (), s32[]{:S(2)}) async-start(), calls=%async_computation.55 | async-start | bytes 294912 | tf_op jit(solution)/shard_map/reduce_scatter | solution.py:139
  1694.8 228.7 %reduce-scatter.54.cloned.1.call-start = ((), (), s32[]{:S(2)}) async-start(), calls=%async_computation.54 | async-start | bytes 2359296 | tf_op jit(solution)/shard_map/reduce_scatter | solution.py:136
  1702.8 285.7 %reduce-scatter.40.cloned.1.call-start = ((), (), s32[]{:S(2)}) async-start(), calls=%async_computation.47 | async-start | bytes 294912 | tf_op jit(solution)/shard_map/reduce_scatter | solution.py:139
  1705.1 348.4 %reduce-scatter.38.cloned.1.call-start = ((), (), s32[]{:S(2)}) async-start(), calls=%async_computation.46 | async-start | bytes 294912 | tf_op jit(solution)/shard_map/reduce_scatter | solution.py:136
  1707.7 416.9 %reduce-scatter.50.cloned.1.call-start = ((), (), s32[]{:S(2)}) async-start(), calls=%async_computation.52 | async-start | bytes 2359296 | tf_op jit(solution)/shard_map/reduce_scatter | solution.py:130
  1715.2 480.2 %reduce-scatter.48.cloned.1.call-start = ((), (), s32[]{:S(2)}) async-start(), calls=%async_computation.51 | async-start | bytes 2359296 | tf_op jit(solution)/shard_map/reduce_scatter | solution.py:127
  1722.6 539.5 %reduce-scatter.46.cloned.1.call-start = ((), (), s32[]{:S(2)}) async-start(), calls=%async_computation.50 | async-start | bytes 1179648 | tf_op jit(solution)/shard_map/reduce_scatter | solution.py:124
  1727.6 599.5 %reduce-scatter.32.cloned.1.call-start = ((), (), s32[]{:S(2)}) async-start(), calls=%async_computation.43 | async-start | bytes 294912 | tf_op jit(solution)/shard_map/reduce_scatter | solution.py:127
  1728.9 663.6 %reduce-scatter.34.cloned.1.call-start = ((), (), s32[]{:S(2)}) async-start(), calls=%async_computation.44 | async-start | bytes 73728 | tf_op jit(solution)/shard_map/reduce_scatter | solution.py:130
  1730.0 728.3 %reduce-scatter.28.cloned.1.call-start = ((), (), s32[]{:S(2)}) async-start(), calls=%async_computation.41 | async-start | bytes 589824 | tf_op jit(solution)/shard_map/reduce_scatter | solution.py:121
  1734.3 795.3 %reduce-scatter.36.cloned.1.call-start = ((), (), s32[]{:S(2)}) async-start(), calls=%async_computation.45 | async-start | bytes 2359296 | tf_op jit(solution)/shard_map/reduce_scatter | solution.py:133
  1740.3 860.7 %reduce-scatter.26.cloned.1.call-start = ((), (), s32[]{:S(2)}) async-start(), calls=%async_computation.40 | async-start | bytes 2359296 | tf_op jit(solution)/shard_map/reduce_scatter | solution.py:118
  1746.4 921.7 %reduce-scatter.30.cloned.1.call-start = ((), (), s32[]{:S(2)}) async-start(), calls=%async_computation.42 | async-start | bytes 1179648 | tf_op jit(solution)/shard_map/reduce_scatter | solution.py:124
  1791.1 1160.0 %reduce-scatter.52.cloned.1.call-start = ((), (), s32[]{:S(2)}) async-start(), calls=%async_computation.53 | async-start | bytes 18874368 | tf_op jit(solution)/shard_map/reduce_scatter | solution.py:133
  1815.9 1418.2 %reduce-scatter.42.cloned.1.call-start = ((), (), s32[]{:S(2)}) async-start(), calls=%async_computation.48 | async-start | bytes 18874368 | tf_op jit(solution)/shard_map/reduce_scatter | solution.py:118
  1841.8 1675.4 %reduce-scatter.44.cloned.1.call-start = ((), (), s32[]{:S(2)}) async-start(), calls=%async_computation.49 | async-start | bytes 18874368 | tf_op jit(solution)/shard_map/reduce_scatter | solution.py:121
  1867.8 734.9 %copy-start.42 = (bf16[2048,256]{1,0:T(8,128)(2,1)S(1)}, bf16[2048,256]{1,0:T(8,128)(2,1)}, u32[]{:S(2)}) copy-start(bf16[2048,256]{1,0:T(8,128)(2,1)} %all-gather.22.cloned.1.call-done) | copy-start | bytes 3145732
  1867.9 734.9 %copy-start.48 = (bf16[1024,256]{1,0:T(8,128)(2,1)S(1)}, bf16[1024,256]{1,0:T(8,128)(2,1)}, u32[]{:S(2)}) copy-start(bf16[1024,256]{1,0:T(8,128)(2,1)} %get-tuple-element.75) | copy-start | bytes 1572868
  1867.9 734.9 %copy-start.55 = (f32[4,1,512]{2,1,0:T(1,128)S(1)}, f32[4,1,512]{2,1,0:T(1,128)}, u32[]{:S(2)}) copy-start(f32[4,1,512]{2,1,0:T(1,128)} %copy-done.54) | copy-start | bytes 24580
  (60 other events, 341.2 us)
Sparse Core Ops, SparseCore 0:
  9.6 37.1 all-gather.17
  48.9 40.9 all-gather.21
  92.0 52.0 all-gather.19
  146.1 21.4 all-gather.23
  169.5 50.3 all-gather.25
  222.6 31.5 all-reduce.9
  257.4 44.3 reduce-scatter.21
  305.5 34.4 all-gather.27
  342.2 40.2 all-gather.31
  384.4 47.7 all-gather.37
  434.4 47.6 all-gather.33
  484.0 225.7 all-gather.29
  712.0 225.4 all-gather.35
  939.5 47.2 all-gather.41
  988.7 225.8 all-gather.39
  1217.3 31.5 all-reduce.11
  1251.9 44.6 reduce-scatter.23
  1302.1 33.4 all-reduce.13
  1337.1 34.5 all-gather.43
  1465.0 94.0 all-reduce.19
  1569.3 34.5 all-gather.45
  1606.9 33.3 all-reduce.15
  1658.5 24.8 reduce-scatter.57
  1692.4 94.0 all-reduce.17
  1790.4 62.2 reduce-scatter.55
  1856.0 67.4 reduce-scatter.53
  1927.3 61.1 reduce-scatter.39
  1992.4 61.0 reduce-scatter.37
  2057.0 67.4 reduce-scatter.49
  2127.9 67.5 reduce-scatter.47
  2198.9 63.1 reduce-scatter.45
  2266.0 61.0 reduce-scatter.31
  2331.0 61.5 reduce-scatter.33
  2396.4 61.7 reduce-scatter.27
  2461.8 67.8 reduce-scatter.35
  2533.6 67.3 reduce-scatter.25
  2604.8 63.2 reduce-scatter.29
  2671.9 279.1 reduce-scatter.51
  2954.8 279.2 reduce-scatter.41
  3237.9 279.2 reduce-scatter.43
where the time goes:
time: 3540 us; the launch traced here: 3530 us
  waiting for transfers between devices  2730 us (77%)
  matrix products  438 us (12%)
  blocking collectives  260 us (7%)
  other arithmetic  66.9 us (2%)
    reduce_scatter x2, waiting for transfers between devices, scatter_grads(): lax.psum_scatter(sixth_g.astype(jnp.bfloat16), 'rows', scatter_dimension=...  351 us
    reduce_scatter x2, waiting for transfers between devices, scatter_grads(): lax.psum_scatter(first_g.astype(jnp.bfloat16), 'rows', scatter_dimension=...  349 us
    reduce_scatter x2, waiting for transfers between devices, scatter_grads(): lax.psum_scatter(second_g.astype(jnp.bfloat16), 'rows', scatter_dimension...  343 us
    all_gather x2, waiting for transfers between devices, gather_weights(): lax.all_gather(sixth_w, 'rows', axis=1, tiled=True)  249 us
    all_gather x2, waiting for transfers between devices, gather_weights(): lax.all_gather(first_w, 'rows', axis=0, tiled=True)  217 us
    all_gather x1, waiting for transfers between devices, gather_weights(): lax.all_gather(second_w, 'rows', axis=0, tiled=True)  199 us
    dot_general x16, matrix products, product(): return jnp.dot(former, latter, preferred_element_type=jnp.float32)  147 us
    dot_general x16, matrix products, right_trans(): lax.dot_general(former, latter, (((1,), (1,)), ((), ())), preferred_eleme...  140 us
  transfers between devices with their start and end apart: 40, of which 34 were waited for; matrix products, arithmetic and copies ran while one was open for 10% of the time, Pallas kernels for 0%

commit v1 on v0

v1 whole, which is shorter than its diff:
```python
import jax
import jax.numpy as jnp
from jax import lax
from jax.sharding import PartitionSpec as P

NORM_EPS = 1e-06
BF = jnp.bfloat16
F32 = jnp.float32


def product(former, latter):
    return jnp.dot(former, latter, preferred_element_type=F32)


def left_trans(former, latter):
    return lax.dot_general(
        former, latter, (((0,), (0,)), ((), ())), preferred_element_type=F32
    )


def right_trans(former, latter):
    return lax.dot_general(
        former, latter, (((1,), (1,)), ((), ())), preferred_element_type=F32
    )


def angles(length, head_size):
    half_size = head_size // 2
    inverse = 10000.0 ** (-(jnp.arange(half_size, dtype=F32) * 2.0 / head_size))
    theta = jnp.arange(length, dtype=F32)[:, None] * inverse[None, :]
    return (jnp.cos(theta), jnp.sin(theta))


def rotate(values_in, cosine_table, sine_table):
    half_size = values_in.shape[-1] // 2
    first_half = values_in[..., :half_size]
    second_half = values_in[..., half_size:]
    return jnp.concatenate(
        [
            first_half * cosine_table - second_half * sine_table,
            second_half * cosine_table + first_half * sine_table,
        ],
        axis=-1,
    )


def allowed_mask(key_count, length):
    row_place = jnp.arange(key_count)[:, None]
    col_place = jnp.arange(key_count)[None, :]
    return ((col_place <= row_place) & (col_place < length))[None]


def attend_forward(query_rows, key_rows, value_rows, length):
    allowed = allowed_mask(key_rows.shape[0], length)
    scores = jnp.einsum("hqd,kd->hqk", query_rows, key_rows, preferred_element_type=F32)
    masked = jnp.where(allowed, scores, -1e30)
    largest = jnp.max(masked, axis=-1, keepdims=True)
    exponent = jnp.exp(masked - largest)
    totals = jnp.sum(exponent, axis=-1, keepdims=True)
    probability = (exponent / totals).astype(BF)
    attended = jnp.einsum("hqk,kd->hqd", probability, value_rows, preferred_element_type=F32)
    return (attended.astype(BF), (largest + jnp.log(totals))[..., 0])


def attend_backward(query_rows, key_rows, value_rows, length, log_total, grad_out):
    allowed = allowed_mask(key_rows.shape[0], length)
    scores = jnp.einsum("hqd,kd->hqk", query_rows, key_rows, preferred_element_type=F32)
    probability = jnp.where(allowed, jnp.exp(scores - log_total[..., None]), 0.0)
    grad_prob = jnp.einsum("hqd,kd->hqk", grad_out, value_rows, preferred_element_type=F32)
    row_terms = jnp.sum(probability * grad_prob, axis=-1, keepdims=True)
    grad_scores = (probability * (grad_prob - row_terms)).astype(BF)
    grad_query = jnp.einsum("hqk,kd->hqd", grad_scores, key_rows, preferred_element_type=F32)
    grad_key = jnp.einsum("hqk,hqd->kd", grad_scores, query_rows, preferred_element_type=F32)
    grad_value = jnp.einsum(
        "hqk,hqd->kd", probability.astype(BF), grad_out, preferred_element_type=F32
    )
    return (grad_query, grad_key, grad_value)


def norm_scale(values_in):
    return lax.rsqrt(jnp.mean(values_in * values_in, axis=-1, keepdims=True) + NORM_EPS)


def norm_forward(values_in, gain_row):
    row_scale = norm_scale(values_in)
    return ((values_in * row_scale * (1.0 + gain_row)).astype(BF), row_scale)


def norm_backward(grad_rows, rows_in, gain_row, row_scale):
    factor = 1.0 + gain_row
    row_dots = jnp.sum(grad_rows * factor * rows_in, axis=-1, keepdims=True)
    grad_input = (
        row_scale * factor * grad_rows
        - rows_in * (row_scale * row_scale * row_scale) * row_dots / rows_in.shape[1]
    )
    return (grad_input, jnp.sum(grad_rows * rows_in * row_scale, axis=0))


def geglu(gate_lin, up_lin):
    return jax.nn.gelu(gate_lin, approximate=True) * up_lin


def solution(mesh):
    row_devices = mesh.shape["rows"]
    col_devices = mesh.shape["cols"]
    nk = 2
    nx = col_devices // nk
    nz = 4 if row_devices % 4 == 0 else row_devices
    ny = row_devices // nz
    BOTH = ("rows", "cols")

    def permute(value, move):
        pairs = []
        for z in range(nz):
            for y in range(ny):
                for x in range(nx):
                    for k in range(nk):
                        tz, ty, tx, tk = move(z, y, x, k)
                        source = (z * ny + y) * col_devices + x * nk + k
                        target = (tz * ny + ty) * col_devices + tx * nk + tk
                        pairs.append((source, target))
        return lax.ppermute(value, BOTH, pairs)

    def swap_z(value, mask):
        return permute(value, lambda z, y, x, k: (z ^ mask, y, x, k))

    def swap_y(value, mask):
        return permute(value, lambda z, y, x, k: (z, y ^ mask, x, k))

    def swap_x(value, mask):
        return permute(value, lambda z, y, x, k: (z, y, x ^ mask, k))

    def swap_k(value):
        return permute(value, lambda z, y, x, k: (z, y, x, k ^ 1))

    def ring(value):
        return permute(
            value, lambda z, y, x, k: ((z + 1) % nz if k == 0 else (z - 1) % nz, y, x, k)
        )

    def natural(parts, place):
        count = len(parts)
        arrays = list(parts)
        bit = 1
        while bit < count:
            hot = (place & bit) != 0
            arrays = [
                jnp.where(hot, arrays[slot ^ bit], arrays[slot]) for slot in range(count)
            ]
            bit *= 2
        return arrays

    def gather_cols(value, place):
        parts = [None] * col_devices
        for mask in range(nx):
            near = value if mask == 0 else swap_x(value, mask)
            parts[mask * nk] = near
            parts[mask * nk + 1] = swap_k(near)
        return natural(parts, place)

    def scatter_rest(kept, place_x):
        near = lax.dynamic_index_in_dim(kept, place_x, 0, keepdims=False)
        for mask in range(1, nx):
            away = lax.dynamic_index_in_dim(kept, place_x ^ mask, 0, keepdims=False)
            near = near + swap_x(away.astype(BF), mask).astype(F32)
        return near

    def scatter_cols(blocks, place_x, place_k, make):
        hot = place_k == 0
        away = jnp.where(hot, blocks[:, 1], blocks[:, 0])
        near = jnp.where(hot, blocks[:, 0], blocks[:, 1])
        got = swap_k(make(away).astype(BF))
        kept = make(near) + got.astype(F32)
        return scatter_rest(kept, place_x)

    def sum_all(value):
        for mask_count, swap in ((nx, swap_x), (ny, swap_y), (nz, swap_z)):
            bit = 1
            while bit < mask_count:
                value = value + swap(value, bit)
                bit *= 2
        return value + swap_k(value)

    def sum_cols(value):
        value = value + swap_k(value.astype(BF)).astype(F32)
        bit = 1
        while bit < nx:
            value = value + swap_x(value.astype(BF), bit).astype(F32)
            bit *= 2
        return value

    MASKS = [(mx, my) for mx in range(nx) for my in range(ny)]

    def spread_weight(own, x_first):
        parts = {(0, 0): own}
        if x_first:
            for mx in range(1, nx):
                parts[(mx, 0)] = swap_x(own, mx)
            for mx in range(nx):
                for my in range(1, ny):
                    parts[(mx, my)] = swap_y(parts[(mx, 0)], my)
        else:
            for my in range(1, ny):
                parts[(0, my)] = swap_y(own, my)
            for my in range(ny):
                for mx in range(1, nx):
                    parts[(mx, my)] = swap_x(parts[(0, my)], mx)
        return [parts[mask] for mask in MASKS]

    def reduce_weight(parts, x_first):
        sums = dict(zip(MASKS, parts))
        if x_first:
            for my in reversed(range(ny)):
                total = sums[(0, my)].astype(F32)
                for mx in range(1, nx):
                    total = total + swap_x(sums[(mx, my)], mx).astype(F32)
                sums[(0, my)] = total.astype(BF)
            total = sums[(0, 0)].astype(F32)
            for my in range(1, ny):
                total = total + swap_y(sums[(0, my)], my).astype(F32)
        else:
            for mx in reversed(range(nx)):
                total = sums[(mx, 0)].astype(F32)
                for my in range(1, ny):
                    total = total + swap_y(sums[(mx, my)], my).astype(F32)
                sums[(mx, 0)] = total.astype(BF)
            total = sums[(0, 0)].astype(F32)
            for mx in range(1, nx):
                total = total + swap_x(sums[(mx, 0)], mx).astype(F32)
        return total.astype(BF)

    def exchange(value, axis):
        return lax.all_to_all(value, axis, 0, 0, tiled=True)

    def shards(
        tokens,
        gain_attn,
        gain_mlp,
        w_q,
        w_kv,
        a_qkv,
        b_q,
        b_kv,
        w_o,
        a_o,
        b_o,
        w_gate,
        w_up,
        a_gu,
        b_gate,
        b_up,
        w_down,
        a_down,
        b_down,
        lengths,
        teacher,
        out_grad,
    ):
        row_place = lax.axis_index("rows")
        col_place = lax.axis_index("cols")
        place_x = col_place // nk
        place_k = col_place % nk
        row_count, local_features = tokens.shape
        features = local_features * col_devices
        seq_len = row_count * row_devices // lengths.shape[0]
        seqs_here = row_count // seq_len
        own_rows = row_count // col_devices
        rank = a_qkv.shape[1]
        block_d = w_q.shape[0]
        block_r = b_q.shape[0]
        block_e = block_d + block_r
        q_width = w_q.shape[1]
        kv_width = w_kv.shape[1]
        head_size = kv_width * col_devices // 2
        heads_here = q_width // head_size
        hidden_part = w_gate.shape[1] // row_devices
        lens_here = lax.dynamic_slice_in_dim(lengths, row_place * seqs_here, seqs_here)

        gain_rows = jnp.concatenate(
            [gain_attn[None], gain_mlp[None], jnp.zeros((14, local_features), BF)], axis=0
        )
        small_parts = gather_cols(jnp.concatenate([b_o, b_down, gain_rows], axis=0), col_place)
        small_full = jnp.concatenate(small_parts, axis=1)
        gain_one = small_full[2 * block_r].astype(F32)[None]
        gain_two = small_full[2 * block_r + 1].astype(F32)[None]
        full_x = jnp.concatenate(gather_cols(tokens, col_place), axis=1)

        pack_one = jnp.concatenate(
            [
                jnp.concatenate([w_q, w_kv, a_qkv], axis=1),
                jnp.concatenate([b_q, b_kv, jnp.zeros((block_r, rank), BF)], axis=1),
            ],
            axis=0,
        )
        got_one = lax.all_gather(pack_one, "rows", axis=0, tiled=False)
        full_a_qkv = got_one[:, :block_d, q_width + kv_width :].reshape(features, rank)
        qkv_base = got_one[:, :block_d, : q_width + kv_width].reshape(
            features, q_width + kv_width
        )
        full_b_qkv = got_one[:, block_d:, : q_width + kv_width].reshape(rank, q_width + kv_width)
        w_qkv = (qkv_base.astype(F32) + product(full_a_qkv, full_b_qkv)).astype(BF)

        pack_two = jnp.concatenate(
            [
                jnp.concatenate([w_o.T, a_o.T], axis=0),
                jnp.concatenate(
                    [
                        small_full[: 2 * block_r].reshape(-1, q_width),
                        a_gu.reshape(-1, q_width),
                    ],
                    axis=0,
                ),
            ],
            axis=0,
        )
        got_two = lax.all_gather(pack_two, "rows", axis=0, tiled=False)
        o_base = got_two[:, :block_d].reshape(features, q_width)
        full_a_o_t = got_two[:, block_d:block_e].reshape(rank, q_width)
        b_rows = 2 * block_r * features // q_width
        b_pair = got_two[:, block_e : block_e + b_rows].reshape(
            row_devices, 2, block_r, features
        )
        full_b_o = b_pair[:, 0].reshape(rank, features)
        full_b_down = b_pair[:, 1].reshape(rank, features)
        full_a_gu = got_two[:, block_e + b_rows :].reshape(features, rank)
        w_o_t = (o_base.astype(F32) + left_trans(full_b_o, full_a_o_t)).astype(BF)

        def hidden_slices(weight, adapter, x_first):
            block = jnp.concatenate([weight, adapter], axis=0)
            block = block.reshape(block_e, row_devices, hidden_part).transpose(1, 0, 2)
            return spread_weight(exchange(block, "rows"), x_first)

        def joined(parts, factor):
            whole = jnp.concatenate(parts, axis=2)
            width = whole.shape[2]
            base = whole[:, :block_d].reshape(features, width)
            side = whole[:, block_d:].reshape(rank, width)
            return ((base.astype(F32) + product(factor, side)).astype(BF), side)

        full_b_down_t = full_b_down.T
        gate_w, gate_side = joined(hidden_slices(w_gate, b_gate, False), full_a_gu)
        up_w, up_side = joined(hidden_slices(w_up, b_up, True), full_a_gu)
        down_w, down_side = joined(hidden_slices(w_down.T, a_down.T, False), full_b_down_t)

        pair = jnp.stack([teacher, out_grad]).reshape(
            2, col_devices, own_rows, local_features
        )
        pair = exchange(pair.transpose(1, 0, 2, 3), "cols")
        pair = pair.transpose(1, 2, 0, 3).reshape(2, own_rows, features)
        teacher_own = pair[0].astype(F32)
        out_grad_own = pair[1].astype(F32)

        normed, scale_one = norm_forward(full_x.astype(F32), gain_one)
        kv_piece = product(normed, w_qkv[:, q_width:])
        kv_parts = gather_cols(kv_piece, col_place)
        q_lin = product(normed, w_qkv[:, :q_width])
        kv_lin = jnp.concatenate(kv_parts, axis=1)
        query_scale = head_size ** (-0.5)
        cosine_table, sine_table = angles(seq_len, head_size)
        queries = q_lin.reshape(seqs_here, seq_len, heads_here, head_size).transpose(0, 2, 1, 3)
        queries = (rotate(queries, cosine_table, sine_table) * query_scale).astype(BF)
        keys = rotate(
            kv_lin[:, :head_size].reshape(seqs_here, seq_len, head_size),
            cosine_table,
            sine_table,
        ).astype(BF)
        values = kv_lin[:, head_size:].reshape(seqs_here, seq_len, head_size).astype(BF)
        forward_parts = [
            attend_forward(queries[s], keys[s], values[s], lens_here[s])
            for s in range(seqs_here)
        ]
        attn_rows = jnp.concatenate(
            [part[0].transpose(1, 0, 2).reshape(seq_len, q_width) for part in forward_parts],
            axis=0,
        )
        branch_one = scatter_cols(
            attn_rows.reshape(nx, nk, own_rows, q_width),
            place_x,
            place_k,
            lambda block: right_trans(block.reshape(nx * own_rows, q_width), w_o_t).reshape(
                nx, own_rows, features
            ),
        )
        own_x = lax.dynamic_slice_in_dim(full_x, col_place * own_rows, own_rows, 0).astype(F32)
        own_scale = lax.dynamic_slice_in_dim(scale_one, col_place * own_rows, own_rows, 0)
        middle = own_x + branch_one
        middle_low = middle.astype(BF).astype(F32)
        normed_two, scale_two = norm_forward(middle_low, gain_two)

        def gather_ring(value):
            chunks = []
            for step in range(nz):
                chunks.append(jnp.concatenate([value, swap_k(value)], axis=0))
                if step + 1 < nz:
                    value = ring(value)
            return chunks

        def scatter_ring(parts):
            def chip_sum(part):
                return part[:own_rows] + swap_k(part[own_rows:].astype(BF)).astype(F32)

            total = None
            for step in list(range(1, nz)) + [0]:
                mine = chip_sum(parts[step])
                if total is not None:
                    mine = mine + ring(total.astype(BF)).astype(F32)
                total = mine
            return total

        normed_chunks = gather_ring(normed_two)
        gates, ups, hiddens, parts = [], [], [], []
        for chunk in normed_chunks:
            gate_lin = product(chunk, gate_w)
            up_lin = product(chunk, up_w)
            hidden = geglu(gate_lin, up_lin).astype(BF)
            gates.append(gate_lin)
            ups.append(up_lin)
            hiddens.append(hidden)
            parts.append(right_trans(hidden, down_w))
        result = middle + scatter_ring(parts)

        spots = col_place * own_rows + jnp.arange(own_rows)
        limits = jnp.take(lens_here, spots // seq_len) if seqs_here > 1 else lens_here[0]
        valid_rows = ((spots % seq_len) < limits).astype(F32)[:, None]
        valid_count = jnp.sum(lengths).astype(F32)
        error_rows = result - teacher_own
        square = jnp.sum(error_rows * error_rows * valid_rows)
        total_tokens = row_count * row_devices
        seed_grad = out_grad_own + total_tokens / valid_count * error_rows * valid_rows
        grad_two = seed_grad.astype(BF)

        def to_columns(value):
            blocks = value.reshape(own_rows, col_devices, local_features).transpose(1, 0, 2)
            return exchange(blocks, "cols").reshape(row_count, local_features)

        output = to_columns(result.astype(BF))

        grad_chunks = gather_ring(grad_two)
        d_gates, d_ups, back_parts = [], [], []
        for chunk, gate_lin, up_lin in zip(grad_chunks, gates, ups):
            d_hidden = product(chunk, down_w)
            _, geglu_back = jax.vjp(geglu, gate_lin, up_lin)
            d_gate, d_up = geglu_back(d_hidden)
            d_gate = d_gate.astype(BF)
            d_up = d_up.astype(BF)
            d_gates.append(d_gate)
            d_ups.append(d_up)
            back_parts.append(right_trans(d_gate, gate_w) + right_trans(d_up, up_w))
        d_normed_two = scatter_ring(back_parts)

        def weight_grads(left_chunks, right_chunks, factor, x_first):
            left = jnp.concatenate(left_chunks, axis=0)
            right = jnp.concatenate(right_chunks, axis=0)
            whole = left_trans(left, right).astype(BF)
            side = left_trans(factor, whole).astype(BF)
            packed = jnp.concatenate(
                [
                    whole.reshape(row_devices, block_d, -1),
                    side.reshape(row_devices, block_r, -1),
                ],
                axis=1,
            )
            split = [
                packed[:, :, i * hidden_part : (i + 1) * hidden_part] for i in range(len(MASKS))
            ]
            own = exchange(reduce_weight(split, x_first), "rows")
            block = own.transpose(1, 0, 2).reshape(block_e, row_devices * hidden_part)
            return (block[:block_d], block[block_d:], whole)

        down_g, down_s, down_all = weight_grads(grad_chunks, hiddens, full_b_down_t, False)
        gate_g, gate_s, gate_all = weight_grads(normed_chunks, d_gates, full_a_gu, True)
        up_g, up_s, up_all = weight_grads(normed_chunks, d_ups, full_a_gu, False)
        a_gu_part = right_trans(gate_all, gate_side) + right_trans(up_all, up_side)
        b_down_part = right_trans(down_side, down_all)

        d_norm_two, gain_two_part = norm_backward(d_normed_two, middle_low, gain_two, scale_two)
        d_middle = seed_grad + d_norm_two

        grad_one = d_middle.astype(BF)
        grad_one_full = jnp.concatenate(gather_cols(grad_one, col_place), axis=0)
        d_attended = product(grad_one_full, w_o_t).astype(BF)
        o_grad_t = left_trans(grad_one_full, attn_rows).astype(BF)
        a_o_grad_t = product(full_b_o, o_grad_t).astype(BF)
        b_o_part = right_trans(full_a_o_t, o_grad_t)

        def split_features(value):
            blocks = value.reshape(rank, nx, nk, local_features).transpose(1, 2, 0, 3)
            own = scatter_cols(blocks, place_x, place_k, lambda block: block)
            return own.astype(BF).reshape(row_devices, block_r, local_features)

        rows_pack = jnp.concatenate(
            [
                o_grad_t.reshape(row_devices, block_d, q_width),
                a_o_grad_t.reshape(row_devices, block_r, q_width),
                split_features(b_o_part),
                split_features(b_down_part),
                a_gu_part.astype(BF).reshape(row_devices, -1, q_width),
            ],
            axis=1,
        )
        rows_sum = lax.psum_scatter(rows_pack, "rows", scatter_dimension=0, tiled=True)[0]
        grad_w_o = rows_sum[:block_d].T.astype(F32)
        grad_a_o = rows_sum[block_d:block_e].T.astype(F32)
        grad_b_o = rows_sum[block_e : block_e + block_r].astype(F32)
        grad_b_down = rows_sum[block_e + block_r : block_e + 2 * block_r].astype(F32)
        grad_a_gu = sum_cols(
            rows_sum[block_e + 2 * block_r :].reshape(block_d, rank).astype(F32)
        )

        d_heads = d_attended.reshape(seqs_here, seq_len, heads_here, head_size)
        d_heads = d_heads.transpose(0, 2, 1, 3)
        q_pieces, kv_pieces = [], []
        for s in range(seqs_here):
            d_query, d_key, d_value = attend_backward(
                queries[s], keys[s], values[s], lens_here[s], forward_parts[s][1], d_heads[s]
            )
            d_query = rotate(d_query * query_scale, cosine_table, -sine_table)
            q_pieces.append(d_query.transpose(1, 0, 2).reshape(seq_len, q_width).astype(BF))
            d_key = rotate(d_key, cosine_table, -sine_table)
            kv_pieces.append(jnp.concatenate([d_key, d_value], axis=1))
        d_q_lin = jnp.concatenate(q_pieces, axis=0)
        kv_blocks = jnp.concatenate(kv_pieces, axis=0).reshape(row_count, nx, nk, kv_width)
        d_kv_lin = scatter_cols(
            kv_blocks.transpose(1, 2, 0, 3), place_x, place_k, lambda block: block
        ).astype(BF)
        d_qkv = jnp.concatenate([d_q_lin, d_kv_lin], axis=1)
        d_normed = scatter_cols(
            d_qkv.reshape(nx, nk, own_rows, q_width + kv_width),
            place_x,
            place_k,
            lambda block: right_trans(
                block.reshape(nx * own_rows, q_width + kv_width), w_qkv
            ).reshape(nx, own_rows, features),
        )
        qkv_grad = left_trans(normed, d_qkv).astype(BF)
        b_qkv_grad = left_trans(full_a_qkv, qkv_grad).astype(BF)
        a_qkv_part = right_trans(qkv_grad, full_b_qkv).astype(BF)
        last_pack = jnp.concatenate(
            [
                jnp.concatenate(
                    [
                        qkv_grad.reshape(row_devices, block_d, -1),
                        a_qkv_part.reshape(row_devices, block_d, rank),
                    ],
                    axis=2,
                ),
                jnp.concatenate(
                    [
                        b_qkv_grad.reshape(row_devices, block_r, -1),
                        jnp.zeros((row_devices, block_r, rank), BF),
                    ],
                    axis=2,
                ),
            ],
            axis=1,
        )
        last_sum = lax.psum_scatter(last_pack, "rows", scatter_dimension=0, tiled=True)[0]
        grad_a_qkv = sum_cols(last_sum[:block_d, q_width + kv_width :].astype(F32))
        grad_w_q = last_sum[:block_d, :q_width].astype(F32)
        grad_w_kv = last_sum[:block_d, q_width : q_width + kv_width].astype(F32)
        grad_b_q = last_sum[block_d:, :q_width].astype(F32)
        grad_b_kv = last_sum[block_d:, q_width : q_width + kv_width].astype(F32)

        d_norm_one, gain_one_part = norm_backward(d_normed, own_x, gain_one, own_scale)
        grad_tokens = to_columns((d_middle + d_norm_one).astype(BF)).astype(F32)
        vectors = jnp.concatenate(
            [
                gain_one_part[None],
                gain_two_part[None],
                jnp.full((1, features), square, F32),
            ],
            axis=0,
        )
        sums = sum_all(vectors)
        gains = lax.dynamic_slice_in_dim(sums, col_place * local_features, local_features, 1)
        loss_value = (sums[2, 0] / (2.0 * valid_count)).reshape(1)
        return (
            output,
            loss_value,
            grad_tokens,
            gains[0],
            gains[1],
            grad_w_q,
            grad_w_kv,
            grad_a_qkv,
            grad_b_q,
            grad_b_kv,
            grad_w_o,
            grad_a_o,
            grad_b_o,
            gate_g.astype(F32),
            up_g.astype(F32),
            grad_a_gu,
            gate_s.astype(F32),
            up_s.astype(F32),
            down_g.T.astype(F32),
            down_s.T.astype(F32),
            grad_b_down,
        )

    in_specs = (
        P("rows", "cols"),
        P("cols"),
        P("cols"),
        P("rows", "cols"),
        P("rows", "cols"),
        P("rows", None),
        P("rows", "cols"),
        P("rows", "cols"),
        P("cols", "rows"),
        P("cols", "rows"),
        P("rows", "cols"),
        P("rows", "cols"),
        P("rows", "cols"),
        P("rows", None),
        P("rows", "cols"),
        P("rows", "cols"),
        P("cols", "rows"),
        P("cols", "rows"),
        P("rows", "cols"),
        P(),
        P("rows", "cols"),
        P("rows", "cols"),
    )
    out_specs = (
        P("rows", "cols"),
        P(),
        P("rows", "cols"),
        P("cols"),
        P("cols"),
        P("rows", "cols"),
        P("rows", "cols"),
        P("rows", None),
        P("rows", "cols"),
        P("rows", "cols"),
        P("cols", "rows"),
        P("cols", "rows"),
        P("rows", "cols"),
        P("rows", "cols"),
        P("rows", "cols"),
        P("rows", None),
        P("rows", "cols"),
        P("rows", "cols"),
        P("cols", "rows"),
        P("cols", "rows"),
        P("rows", "cols"),
    )
    return jax.shard_map(shards, mesh=mesh, in_specs=in_specs, out_specs=out_specs, check_vma=False)
```

time: 3540 us -> 1580 us (0.45)
  waiting for transfers between devices: 2730 us -> 708 us
  blocking collectives: 260 us -> 0 us
  local copies, waits for them, and re-layouts: 14.2 us -> 196 us
  starting transfers between devices: 3.05 us -> 120 us
  other arithmetic: 66.9 us -> 156 us
  matrix products: 438 us -> 370 us
    reduce_scatter x18 -> x2, waiting for transfers between devices: 1620 us -> 0.01 us  [the longest x1 0.01 us: shards(): lax.psum_scatter(rows_pack, 'rows', scatter_dimension=0, tiled=True)[0]]
    all_gather x15 -> x2, waiting for transfers between devices: 890 us -> 0.01 us  [the longest x1 0.01 us: shards(): got_one = lax.all_gather(pack_one, 'rows', axis=0, tiled=False)]
    ppermute x0 -> x77, waiting for transfers between devices: none -> 452 us  [permute(): return lax.ppermute(value, BOTH, pairs)]
    all_to_all x0 -> x9, waiting for transfers between devices: none -> 256 us  [exchange(): return lax.all_to_all(value, axis, 0, 0, tiled=True)]
    all_gather x8 -> x0, blocking collectives: 200 us -> none  [the longest x2 61.9 us: gather_weights(): lax.all_gather(eighth_w, 'rows', axis=0, tiled=True)]
    psum x6 -> x0, waiting for transfers between devices: 197 us -> none  [the longest x2 134 us: norm_backward(): lax.psum(partial_sum.astype(jnp.bfloat16), 'cols').astype(jnp.float32)]
    ppermute x0 -> x77, starting transfers between devices: none -> 72.8 us  [permute(): return lax.ppermute(value, BOTH, pairs)]
    slice x0 -> x27, local copies, waits for them, and re-layouts: none -> 61.3 us  [the longest x3 25.5 us: joined(): base = whole[:, :block_d].reshape(features, width)]
  transfers between devices with their start and end apart: 40 -> 90, of which waited for: 34 -> 31; matrix products, arithmetic and copies ran while one was open for 10% -> 44% of each run, Pallas kernels for 0% -> 0%
where the time goes in v1:
time: 1580 us; the launch traced here: 1570 us
  waiting for transfers between devices  708 us (45%)
  matrix products  370 us (23%)
  local copies, waits for them, and re-layouts  196 us (12%)
  other arithmetic  156 us (10%)
  starting transfers between devices  120 us (8%)
  between operations  19.1 us (1%)
    ppermute x77, waiting for transfers between devices, permute(): return lax.ppermute(value, BOTH, pairs)  452 us
    all_to_all x9, waiting for transfers between devices, exchange(): return lax.all_to_all(value, axis, 0, 0, tiled=True)  256 us
    dot_general x20, matrix products, product(): return jnp.dot(former, latter, preferred_element_type=F32)  141 us
    dot_general x21, matrix products, right_trans(): lax.dot_general(former, latter, (((1,), (1,)), ((), ())), preferred_eleme...  120 us
    dot_general x10, matrix products, left_trans(): lax.dot_general(former, latter, (((0,), (0,)), ((), ())), preferred_eleme...  86.3 us
    ppermute x77, starting transfers between devices, permute(): return lax.ppermute(value, BOTH, pairs)  72.8 us
    unnamed x326, local copies, waits for them, and re-layouts  70.7 us
    all_to_all x9, starting transfers between devices, exchange(): return lax.all_to_all(value, axis, 0, 0, tiled=True)  47.2 us
  transfers between devices with their start and end apart: 90, of which 31 were waited for; matrix products, arithmetic and copies ran while one was open for 44% of the time, Pallas kernels for 0%

profile of v1, /device:TPU:0, one launch (start us, length us, event | category | flops | bytes accessed | tf_op | source)
XLA Modules:
  0.0 1570.6 jit_solution(11316765899007259465)
XLA Ops:
  12.8 7.3 all-to-all-start
  23.8 96.7 %all-to-all-done = bf16[8,288,512]{2,1,0:T(8,128)(2,1)S(1)} async-done(((bf16[8,288,512]{2,1,0:T(8,128)(2,1)}), bf16[8,288,512]{2,1,0:T(8,128)(2,1)S(1)}, u32[]{:S(2)}, u32[]{:S(2)}) %all-to-all-start) | async-done | bytes 2359328 | tf_op jit(solution)/shard_map/all_to_all | solution.py:233
  136.0 19.5 %collective-permute-done = bf16[1024,512]{1,0:T(8,128)(2,1)} collective-permute-done((bf16[1024,512]{1,0:T(8,128)(2,1)}, bf16[1024,512]{1,0:T(8,128)(2,1)}, u32[]{:S(2)}, u32[]{:S(2)}) %collective-permute-start) | collective-permute-done | bytes 1048608 | tf_op jit(solution)/shard_map/ppermute | solution.py:122
  162.9 36.2 %all-to-all-done.1 = bf16[8,288,512]{2,1,0:T(8,128)(2,1)} async-done(((bf16[8,288,512]{2,1,0:T(8,128)(2,1)}), bf16[8,288,512]{2,1,0:T(8,128)(2,1)}, u32[]{:S(2)}, u32[]{:S(2)}) %all-to-all-start.1) | async-done | bytes 2359328 | tf_op jit(solution)/shard_map/all_to_all | solution.py:233
  234.0 6.7 fusion.128
  248.9 49.0 %all-to-all-done.2 = bf16[8,288,512]{2,1,0:T(8,128)(2,1)} async-done(((bf16[8,288,512]{2,1,0:T(8,128)(2,1)}), bf16[8,288,512]{2,1,0:T(8,128)(2,1)}, u32[]{:S(2)}, u32[]{:S(2)}) %all-to-all-start.2) | async-done | bytes 2359328 | tf_op jit(solution)/shard_map/all_to_all | solution.py:233
  349.4 9.0 collective-permute-done.12
  361.8 47.1 %collective-permute-done.18 = bf16[8,288,512]{2,1,0:T(8,128)(2,1)} collective-permute-done((bf16[8,288,512]{2,1,0:T(8,128)(2,1)}, bf16[8,288,512]{2,1,0:T(8,128)(2,1)}, u32[]{:S(2)}, u32[]{:S(2)}) %collective-permute-start.18) | collective-permute-done | bytes 2359328 | tf_op jit(solution)/shard_map/ppermute | solution.py:122
  426.3 32.8 %collective-permute-done.17 = bf16[8,288,512]{2,1,0:T(8,128)(2,1)} collective-permute-done((bf16[8,288,512]{2,1,0:T(8,128)(2,1)}, bf16[8,288,512]{2,1,0:T(8,128)(2,1)}, u32[]{:S(2)}, u32[]{:S(2)}) %collective-permute-start.17) | collective-permute-done | bytes 2359328 | tf_op jit(solution)/shard_map/ppermute | solution.py:122
  465.7 8.4 slice.402
  486.3 8.8 slice.399
  495.1 20.5 %collective-permute-done.20 = bf16[8,288,512]{2,1,0:T(8,128)(2,1)} collective-permute-done((bf16[8,288,512]{2,1,0:T(8,128)(2,1)}, bf16[8,288,512]{2,1,0:T(8,128)(2,1)}, u32[]{:S(2)}, u32[]{:S(2)}) %collective-permute-start.20) | collective-permute-done | bytes 2359328 | tf_op jit(solution)/shard_map/ppermute | solution.py:122
  521.1 8.3 slice.404
  533.2 9.7 fusion.1
  548.2 5.7 fusion.2
  553.9 6.9 fusion
  560.8 9.9 collective-permute-done.22
  577.4 7.7 fusion.160
  585.1 10.3 multiply_convert_fusion.8
  601.1 7.2 multiply_convert_fusion.5
  610.5 7.6 fusion.251
  628.6 7.1 multiply_convert_fusion.6
  635.7 10.9 collective-permute-done.24
  646.6 7.6 fusion.249
  668.9 6.7 multiply_convert_fusion.7
  705.0 17.2 %collective-permute-done.33 = bf16[256,2048]{1,0:T(8,128)(2,1)} collective-permute-done((bf16[256,2048]{1,0:T(8,128)(2,1)}, bf16[256,2048]{1,0:T(8,128)(2,1)}, u32[]{:S(2)}, u32[]{:S(2)}) %collective-permute-start.33) | collective-permute-done | bytes 1048608 | tf_op jit(solution)/shard_map/ppermute | solution.py:122
  722.2 6.2 constant_dynamic-update-slice_fusion.25
  739.1 11.3 fusion.53
  750.4 8.5 fusion.252
  760.7 7.0 convolution_add_fusion.3
  777.2 12.9 fusion.74
  790.1 6.1 fusion.255
  797.8 8.4 convolution_add_fusion
  813.1 13.1 fusion.67
  826.1 6.1 fusion.254
  832.2 8.4 convolution_add_fusion.1
  852.9 22.8 %fusion.39 = bf16[2048,2048]{1,0:T(8,128)(2,1)S(1)} fusion(bf16[2048,2048]{1,0:T(8,128)(2,1)} %constant_dynamic-update-slice_fusion.18, bf16[512,2048]{1,0:T(8,128)(2,1)} %copy-done.113, bf16[512,2048]{1,0:T(8,128)(2,1)} %get-tuple-element.176, bf16[512,2048]{1,0:T(8,128)(2,1)} %get-tuple-element.178, bf16[512,2048]{1,0:T(8,128)(2,1)} %get-tuple-element.180), kind=kOutput, calls=%fused_computation.65 | convolution fusion | flops 17217617920 | bytes 25165824 | tf_op jit(solution)/shard_map/dot_general | solution.py:16
  875.7 5.8 fusion.152
  886.0 11.2 fusion.60
  897.2 7.8 fusion.253
  905.0 21.7 %fusion.33 = bf16[2048,2048]{1,0:T(8,128)(2,1)S(1)} fusion(bf16[2048,2048]{1,0:T(8,128)(2,1)} %get-tuple-element.142, bf16[512,2048]{1,0:T(8,128)(2,1)S(1)} %copy-done.120, bf16[512,2048]{1,0:T(8,128)(2,1)S(1)} %copy-done.119, bf16[512,2048]{1,0:T(8,128)(2,1)S(1)} %copy-done.117, bf16[512,2048]{1,0:T(8,128)(2,1)S(1)} %copy-done.115), kind=kOutput, calls=%fused_computation.63 | convolution fusion | flops 17217617920 | bytes 25165824 | tf_op jit(solution)/shard_map/dot_general | solution.py:16
  926.8 25.4 %fusion.36 = bf16[2048,2048]{1,0:T(8,128)(2,1)S(1)} fusion(bf16[2048,2048]{1,0:T(8,128)(2,1)} %get-tuple-element.142, bf16[512,2048]{1,0:T(8,128)(2,1)} %get-tuple-element.112, bf16[512,2048]{1,0:T(8,128)(2,1)} %get-tuple-element.110, bf16[512,2048]{1,0:T(8,128)(2,1)} %get-tuple-element.108, bf16[512,2048]{1,0:T(8,128)(2,1)S(1)} %copy-done.122), kind=kOutput, calls=%fused_computation.64 | convolution fusion | flops 17217617920 | bytes 25165824 | tf_op jit(solution)/shard_map/dot_general | solution.py:16
  952.3 14.8 convolution_add_fusion.2
  986.0 15.4 collective-permute-done.46
  1009.5 17.9 %collective-permute-done.47 = bf16[256,2048]{1,0:T(8,128)(2,1)S(1)} collective-permute-done((bf16[256,2048]{1,0:T(8,128)(2,1)S(1)}, bf16[256,2048]{1,0:T(8,128)(2,1)S(1)}, u32[]{:S(2)}, u32[]{:S(2)}) %collective-permute-start.47) | collective-permute-done | bytes 1048608 | tf_op jit(solution)/shard_map/ppermute | solution.py:122
  1041.4 21.5 %collective-permute-done.65 = bf16[256,512]{1,0:T(8,128)(2,1)} collective-permute-done((bf16[256,512]{1,0:T(8,128)(2,1)S(1)}, bf16[256,512]{1,0:T(8,128)(2,1)}, u32[]{:S(2)}, u32[]{:S(2)}) %collective-permute-start.65) | collective-permute-done | bytes 262176 | tf_op jit(solution)/shard_map/ppermute | solution.py:122
  1066.6 4.9 add_convert_fusion.7
  1076.8 12.6 collective-permute-done.75
  1102.7 6.4 convolution_convert_fusion.8
  1114.8 4.9 collective-permute-done.63
  1124.1 9.4 multiply_reduce_fusion
  1133.8 133.6 %collective-permute-done.68 = bf16[8,288,512]{2,1,0:T(8,128)(2,1)} collective-permute-done((bf16[8,288,512]{2,1,0:T(8,128)(2,1)}, bf16[8,288,512]{2,1,0:T(8,128)(2,1)}, u32[]{:S(2)}, u32[]{:S(2)}) %collective-permute-start.68) | collective-permute-done | bytes 2359328 | tf_op jit(solution)/shard_map/ppermute | solution.py:122
  1276.0 7.3 multiply_convert_fusion
  1287.0 5.5 fusion.156
  1310.6 20.3 %all-to-all-done.6 = bf16[8,288,512]{2,1,0:T(8,128)(2,1)} async-done(((bf16[8,288,512]{2,1,0:T(8,128)(2,1)}), bf16[8,288,512]{2,1,0:T(8,128)(2,1)}, u32[]{:S(2)}, u32[]{:S(2)}) %all-to-all-start.6) | async-done | bytes 2359328 | tf_op jit(solution)/shard_map/all_to_all | solution.py:233
  1334.6 5.4 convolution_convert_fusion.3
  1357.6 4.9 add_convert_fusion
  1362.5 53.5 %all-to-all-done.7 = bf16[8,288,512]{2,1,0:T(8,128)(2,1)S(1)} async-done(((bf16[8,288,512]{2,1,0:T(8,128)(2,1)}), bf16[8,288,512]{2,1,0:T(8,128)(2,1)S(1)}, u32[]{:S(2)}, u32[]{:S(2)}) %all-to-all-start.7) | async-done | bytes 2359328 | tf_op jit(solution)/shard_map/all_to_all | solution.py:233
  1416.0 7.5 all-to-all-start.8
  1435.5 16.4 %collective-permute-done.56 = f32[3,2048]{1,0:T(4,128)S(1)} collective-permute-done((f32[3,2048]{1,0:T(4,128)S(1)}, f32[3,2048]{1,0:T(4,128)S(1)}, u32[]{:S(2)}, u32[]{:S(2)}) %collective-permute-start.56) | collective-permute-done | bytes 24608 | tf_op jit(solution)/shard_map/ppermute | solution.py:122
  1452.0 11.6 collective-permute-done.57
  1467.2 28.1 %collective-permute-done.58 = f32[3,2048]{1,0:T(4,128)S(1)} collective-permute-done((f32[3,2048]{1,0:T(4,128)S(1)}, f32[3,2048]{1,0:T(4,128)S(1)}, u32[]{:S(2)}, u32[]{:S(2)}) %collective-permute-start.58) | collective-permute-done | bytes 24608 | tf_op jit(solution)/shard_map/ppermute | solution.py:122
  1510.9 6.2 all-to-all-start.5
  1528.9 5.3 copy.166
  (680 shorter events, 490.9 us)
Async XLA Ops:
  7.2 201.6 %all-gather.5.cloned.1.call-start = ((), (), s32[]{:S(2)}) async-start(), calls=%async_computation.13 | async-start | bytes 4644864 | tf_op jit(solution)/shard_map/all_gather | solution.py:295
  12.8 107.7 %all-to-all-start = ((bf16[8,288,512]{2,1,0:T(8,128)(2,1)}), bf16[8,288,512]{2,1,0:T(8,128)(2,1)S(1)}, u32[]{:S(2)}, u32[]{:S(2)}) async-start(bf16[8,288,512]{2,1,0:T(8,128)(2,1)} %bitcast.431), calls=%async_computation | async-start | bytes 4718592 | tf_op jit(solution)/shard_map/all_to_all | solution.py:233
  120.5 78.7 %all-to-all-start.1 = ((bf16[8,288,512]{2,1,0:T(8,128)(2,1)}), bf16[8,288,512]{2,1,0:T(8,128)(2,1)}, u32[]{:S(2)}, u32[]{:S(2)}) async-start(bf16[8,288,512]{2,1,0:T(8,128)(2,1)} %bitcast.430), calls=%async_computation.1 | async-start | bytes 4718592 | tf_op jit(solution)/shard_map/all_to_all | solution.py:233
  124.8 199.8 %all-gather.7.cloned.1.call-start = ((), (), s32[]{:S(2)}) async-start(), calls=%async_computation.14 | async-start | bytes 6193152 | tf_op jit(solution)/shard_map/all_gather | solution.py:316
  129.6 25.9 %collective-permute-start = (bf16[1024,512]{1,0:T(8,128)(2,1)}, bf16[1024,512]{1,0:T(8,128)(2,1)}, u32[]{:S(2)}, u32[]{:S(2)}) collective-permute-start(bf16[1024,512]{1,0:T(8,128)(2,1)} %param.22), channel_id=1, source_target_pairs={{0,2},{1,3},{2,0},{3,1},{4,6},{5,7},{6,4},{7,5},{8,10},{9,11},{10,... | collective-permute-start | bytes 3145736 | tf_op jit(solution)/shard_map/ppermute | solution.py:122
  135.7 68.0 %collective-permute-start.2 = (bf16[1024,512]{1,0:T(8,128)(2,1)}, bf16[1024,512]{1,0:T(8,128)(2,1)}, u32[]{:S(2)}, u32[]{:S(2)}) collective-permute-start(bf16[1024,512]{1,0:T(8,128)(2,1)} %param.22), channel_id=1, source_target_pairs={{0,1},{1,0},{2,3},{3,2},{4,5},{5,4},{6,7},{7,6},{8,9},{9,8},{10,11... | collective-permute-start | bytes 3145736 | tf_op jit(solution)/shard_map/ppermute | solution.py:122
  155.5 48.2 %collective-permute-start.1 = (bf16[1024,512]{1,0:T(8,128)(2,1)}, bf16[1024,512]{1,0:T(8,128)(2,1)}, u32[]{:S(2)}, u32[]{:S(2)}) collective-permute-start(bf16[1024,512]{1,0:T(8,128)(2,1)} %collective-permute-done), channel_id=1, source_target_pairs={{0,1},{1,0},{2,3},{3,2},{4,5},{5,4},{6,7},{7,6},{8,9},{9,8},{10,11... | collective-permute-start | bytes 3145736 | tf_op jit(solution)/shard_map/ppermute | solution.py:122
  199.1 98.7 %all-to-all-start.2 = ((bf16[8,288,512]{2,1,0:T(8,128)(2,1)}), bf16[8,288,512]{2,1,0:T(8,128)(2,1)}, u32[]{:S(2)}, u32[]{:S(2)}) async-start(bf16[8,288,512]{2,1,0:T(8,128)(2,1)} %bitcast.434), calls=%async_computation.2 | async-start | bytes 4718592 | tf_op jit(solution)/shard_map/all_to_all | solution.py:233
  227.0 110.6 %collective-permute-start.16 = (bf16[8,288,512]{2,1,0:T(8,128)(2,1)}, bf16[8,288,512]{2,1,0:T(8,128)(2,1)}, u32[]{:S(2)}, u32[]{:S(2)}) collective-permute-start(bf16[8,288,512]{2,1,0:T(8,128)(2,1)} %all-to-all-done.1), channel_id=1, source_target_pairs={{0,2},{1,3},{2,0},{3,1},{4,6},{5,7},{6,4},{7,5},{8,10},{9,11},{10,... | collective-permute-start | bytes 7077896 | tf_op jit(solution)/shard_map/ppermute | solution.py:122
  227.5 111.5 %collective-permute-start.15 = (bf16[8,288,512]{2,1,0:T(8,128)(2,1)}, bf16[8,288,512]{2,1,0:T(8,128)(2,1)}, u32[]{:S(2)}, u32[]{:S(2)}) collective-permute-start(bf16[8,288,512]{2,1,0:T(8,128)(2,1)} %all-to-all-done.1), channel_id=1, source_target_pairs={{0,4},{1,5},{2,6},{3,7},{4,0},{5,1},{6,2},{7,3},{8,12},{9,13},{10,... | collective-permute-start | bytes 7077896 | tf_op jit(solution)/shard_map/ppermute | solution.py:122
  229.5 113.5 %collective-permute-start.13 = (bf16[8,288,512]{2,1,0:T(8,128)(2,1)S(1)}, bf16[8,288,512]{2,1,0:T(8,128)(2,1)}, u32[]{:S(2)}, u32[]{:S(2)}) collective-permute-start(bf16[8,288,512]{2,1,0:T(8,128)(2,1)S(1)} %copy-done.22), channel_id=1, source_target_pairs={{0,2},{1,3},{2,0},{3,1},{4,6},{5,7},{6,4},{7,5},{8,10},{9,11},{10,... | collective-permute-start | bytes 7077896 | tf_op jit(solution)/shard_map/ppermute | solution.py:122
  234.0 63.9 %collective-permute-start.7 = (f32[1024,128]{0,1:T(8,128)}, f32[1024,128]{0,1:T(8,128)}, u32[]{:S(2)}, u32[]{:S(2)}) collective-permute-start(f32[1024,128]{0,1:T(8,128)} %collective-permute-done.6), channel_id=1, source_target_pairs={{0,1},{1,0},{2,3},{3,2},{4,5},{5,4},{6,7},{7,6},{8,9},{9,8},{10,11... | collective-permute-start | bytes 1572872 | tf_op jit(solution)/shard_map/ppermute | solution.py:122
  246.9 111.5 %collective-permute-start.12 = (bf16[8,288,512]{2,1,0:T(8,128)(2,1)S(1)}, bf16[8,288,512]{2,1,0:T(8,128)(2,1)}, u32[]{:S(2)}, u32[]{:S(2)}) collective-permute-start(bf16[8,288,512]{2,1,0:T(8,128)(2,1)S(1)} %copy-done.22), channel_id=1, source_target_pairs={{0,4},{1,5},{2,6},{3,7},{4,0},{5,1},{6,2},{7,3},{8,12},{9,13},{10,... | collective-permute-start | bytes 7077896 | tf_op jit(solution)/shard_map/ppermute | solution.py:122
  297.9 111.1 %collective-permute-start.18 = (bf16[8,288,512]{2,1,0:T(8,128)(2,1)}, bf16[8,288,512]{2,1,0:T(8,128)(2,1)}, u32[]{:S(2)}, u32[]{:S(2)}) collective-permute-start(bf16[8,288,512]{2,1,0:T(8,128)(2,1)} %all-to-all-done.2), channel_id=1, source_target_pairs={{0,4},{1,5},{2,6},{3,7},{4,0},{5,1},{6,2},{7,3},{8,12},{9,13},{10,... | collective-permute-start | bytes 7077896 | tf_op jit(solution)/shard_map/ppermute | solution.py:122
  337.5 85.0 %collective-permute-start.19 = (bf16[8,288,512]{2,1,0:T(8,128)(2,1)}, bf16[8,288,512]{2,1,0:T(8,128)(2,1)}, u32[]{:S(2)}, u32[]{:S(2)}) collective-permute-start(bf16[8,288,512]{2,1,0:T(8,128)(2,1)} %all-to-all-done.2), channel_id=1, source_target_pairs={{0,2},{1,3},{2,0},{3,1},{4,6},{5,7},{6,4},{7,5},{8,10},{9,11},{10,... | collective-permute-start | bytes 7077896 | tf_op jit(solution)/shard_map/ppermute | solution.py:122
  339.0 120.1 %collective-permute-start.17 = (bf16[8,288,512]{2,1,0:T(8,128)(2,1)}, bf16[8,288,512]{2,1,0:T(8,128)(2,1)}, u32[]{:S(2)}, u32[]{:S(2)}) collective-permute-start(bf16[8,288,512]{2,1,0:T(8,128)(2,1)} %collective-permute-done.16), channel_id=1, source_target_pairs={{0,4},{1,5},{2,6},{3,7},{4,0},{5,1},{6,2},{7,3},{8,12},{9,13},{10,... | collective-permute-start | bytes 7077896 | tf_op jit(solution)/shard_map/ppermute | solution.py:122
  343.0 131.2 %collective-permute-start.9 = (bf16[2,256,2048]{2,1,0:T(8,128)(2,1)}, bf16[2,256,2048]{2,1,0:T(8,128)(2,1)}, u32[]{:S(2)}, u32[]{:S(2)}) collective-permute-start(bf16[2,256,2048]{2,1,0:T(8,128)(2,1)} %convolution_convert_fusion.2), channel_id=1, source_target_pairs={{0,1},{1,0},{2,3},{3,2},{4,5},{5,4},{6,7},{7,6},{8,9},{9,8},{10,11... | collective-permute-start | bytes 6291464 | tf_op jit(solution)/shard_map/ppermute | solution.py:122
  344.5 353.7 %all-to-all-start.4 = ((bf16[4,2,256,512]{3,2,1,0:T(8,128)(2,1)}), bf16[4,2,256,512]{3,2,1,0:T(8,128)(2,1)}, u32[]{:S(2)}, u32[]{:S(2)}) async-start(bf16[4,2,256,512]{3,2,1,0:T(8,128)(2,1)} %maximum_bitcast_fusion), calls=%async_computation.4 | async-start | bytes 4194304 | tf_op jit(solution)/shard_map/all_to_all | solution.py:233
  358.4 123.3 %collective-permute-start.14 = (bf16[8,288,512]{2,1,0:T(8,128)(2,1)}, bf16[8,288,512]{2,1,0:T(8,128)(2,1)}, u32[]{:S(2)}, u32[]{:S(2)}) collective-permute-start(bf16[8,288,512]{2,1,0:T(8,128)(2,1)} %collective-permute-done.12), channel_id=1, source_target_pairs={{0,2},{1,3},{2,0},{3,1},{4,6},{5,7},{6,4},{7,5},{8,10},{9,11},{10,... | collective-permute-start | bytes 7077896 | tf_op jit(solution)/shard_map/ppermute | solution.py:122
  409.0 106.6 %collective-permute-start.20 = (bf16[8,288,512]{2,1,0:T(8,128)(2,1)}, bf16[8,288,512]{2,1,0:T(8,128)(2,1)}, u32[]{:S(2)}, u32[]{:S(2)}) collective-permute-start(bf16[8,288,512]{2,1,0:T(8,128)(2,1)} %collective-permute-done.18), channel_id=1, source_target_pairs={{0,2},{1,3},{2,0},{3,1},{4,6},{5,7},{6,4},{7,5},{8,10},{9,11},{10,... | collective-permute-start | bytes 7077896 | tf_op jit(solution)/shard_map/ppermute | solution.py:122
  480.2 62.6 %collective-permute-start.10 = (bf16[256,2048]{1,0:T(8,128)(2,1)}, bf16[256,2048]{1,0:T(8,128)(2,1)S(1)}, u32[]{:S(2)}, u32[]{:S(2)}) collective-permute-start(bf16[256,2048]{1,0:T(8,128)(2,1)} %fusion.161), channel_id=1, source_target_pairs={{0,2},{1,3},{2,0},{3,1},{4,6},{5,7},{6,4},{7,5},{8,10},{9,11},{10,... | collective-permute-start | bytes 3145736 | tf_op jit(solution)/shard_map/ppermute | solution.py:122
  547.8 22.9 %collective-permute-start.22 = (bf16[256,2048]{1,0:T(8,128)(2,1)}, bf16[256,2048]{1,0:T(8,128)(2,1)}, u32[]{:S(2)}, u32[]{:S(2)}) collective-permute-start(bf16[256,2048]{1,0:T(8,128)(2,1)} %get-tuple-element.89), channel_id=1, source_target_pairs={{0,8},{1,25},{2,10},{3,27},{4,12},{5,29},{6,14},{7,31},{8,16},{9,1... | collective-permute-start | bytes 3145736 | tf_op jit(solution)/shard_map/ppermute | solution.py:122
  548.0 24.5 %collective-permute-start.11 = (bf16[256,2048]{1,0:T(8,128)(2,1)}, bf16[256,2048]{1,0:T(8,128)(2,1)}, u32[]{:S(2)}, u32[]{:S(2)}) collective-permute-start(bf16[256,2048]{1,0:T(8,128)(2,1)} %get-tuple-element.89), channel_id=1, source_target_pairs={{0,1},{1,0},{2,3},{3,2},{4,5},{5,4},{6,7},{7,6},{8,9},{9,8},{10,11... | collective-permute-start | bytes 3145736 | tf_op jit(solution)/shard_map/ppermute | solution.py:122
  570.8 24.6 %collective-permute-start.29 = (bf16[256,2048]{1,0:T(8,128)(2,1)}, bf16[256,2048]{1,0:T(8,128)(2,1)S(1)}, u32[]{:S(2)}, u32[]{:S(2)}) collective-permute-start(bf16[256,2048]{1,0:T(8,128)(2,1)} %collective-permute-done.22), channel_id=1, source_target_pairs={{0,1},{1,0},{2,3},{3,2},{4,5},{5,4},{6,7},{7,6},{8,9},{9,8},{10,11... | collective-permute-start | bytes 3145736 | tf_op jit(solution)/shard_map/ppermute | solution.py:122
  570.8 37.6 %collective-permute-start.23 = (bf16[256,2048]{1,0:T(8,128)(2,1)}, bf16[256,2048]{1,0:T(8,128)(2,1)S(1)}, u32[]{:S(2)}, u32[]{:S(2)}) collective-permute-start(bf16[256,2048]{1,0:T(8,128)(2,1)} %collective-permute-done.22), channel_id=1, source_target_pairs={{0,8},{1,25},{2,10},{3,27},{4,12},{5,29},{6,14},{7,31},{8,16},{9,1... | collective-permute-start | bytes 3145736 | tf_op jit(solution)/shard_map/ppermute | solution.py:122
  618.3 28.3 %collective-permute-start.24 = (bf16[256,2048]{1,0:T(8,128)(2,1)S(1)}, bf16[256,2048]{1,0:T(8,128)(2,1)S(1)}, u32[]{:S(2)}, u32[]{:S(2)}) collective-permute-start(bf16[256,2048]{1,0:T(8,128)(2,1)S(1)} %collective-permute-done.23), channel_id=1, source_target_pairs={{0,8},{1,25},{2,10},{3,27},{4,12},{5,29},{6,14},{7,31},{8,16},{9,1... | collective-permute-start | bytes 3145736 | tf_op jit(solution)/shard_map/ppermute | solution.py:122
  627.2 39.4 %collective-permute-start.31 = (bf16[256,2048]{1,0:T(8,128)(2,1)}, bf16[256,2048]{1,0:T(8,128)(2,1)S(1)}, u32[]{:S(2)}, u32[]{:S(2)}) collective-permute-start(bf16[256,2048]{1,0:T(8,128)(2,1)} %fusion.121), channel_id=1, source_target_pairs={{0,8},{1,25},{2,10},{3,27},{4,12},{5,29},{6,14},{7,31},{8,16},{9,1... | collective-permute-start | bytes 3145736 | tf_op jit(solution)/shard_map/ppermute | solution.py:122
  668.1 25.9 %collective-permute-start.32 = (bf16[256,2048]{1,0:T(8,128)(2,1)}, bf16[256,2048]{1,0:T(8,128)(2,1)S(1)}, u32[]{:S(2)}, u32[]{:S(2)}) collective-permute-start(bf16[256,2048]{1,0:T(8,128)(2,1)} %fusion.123), channel_id=1, source_target_pairs={{0,8},{1,25},{2,10},{3,27},{4,12},{5,29},{6,14},{7,31},{8,16},{9,1... | collective-permute-start | bytes 3145736 | tf_op jit(solution)/shard_map/ppermute | solution.py:122
  695.6 26.6 %collective-permute-start.33 = (bf16[256,2048]{1,0:T(8,128)(2,1)}, bf16[256,2048]{1,0:T(8,128)(2,1)}, u32[]{:S(2)}, u32[]{:S(2)}) collective-permute-start(bf16[256,2048]{1,0:T(8,128)(2,1)} %fusion.125), channel_id=1, source_target_pairs={{0,8},{1,25},{2,10},{3,27},{4,12},{5,29},{6,14},{7,31},{8,16},{9,1... | collective-permute-start | bytes 3145736 | tf_op jit(solution)/shard_map/ppermute | solution.py:122
  730.0 28.9 %collective-permute-start.36 = (bf16[256,2048]{1,0:T(8,128)(2,1)}, bf16[256,2048]{1,0:T(8,128)(2,1)}, u32[]{:S(2)}, u32[]{:S(2)}) collective-permute-start(bf16[256,2048]{1,0:T(8,128)(2,1)} %get-tuple-element.91), channel_id=1, source_target_pairs={{0,8},{1,25},{2,10},{3,27},{4,12},{5,29},{6,14},{7,31},{8,16},{9,1... | collective-permute-start | bytes 3145736 | tf_op jit(solution)/shard_map/ppermute | solution.py:122
  734.5 536.9 %all-to-all-start.3 = ((bf16[4,256,512]{2,1,0:T(8,128)(2,1)}), bf16[4,256,512]{2,1,0:T(8,128)(2,1)}, u32[]{:S(2)}, u32[]{:S(2)}) async-start(bf16[4,256,512]{2,1,0:T(8,128)(2,1)} %bitcast.378), calls=%async_computation.3 | async-start | bytes 2097152 | tf_op jit(solution)/shard_map/all_to_all | solution.py:233
  738.8 797.1 %reduce-scatter.5.cloned.1.call-start = ((), (), s32[]{:S(2)}) async-start(), calls=%async_computation.12 | async-start | bytes 4423680 | tf_op jit(solution)/shard_map/reduce_scatter | solution.py:501
  758.9 18.3 %collective-permute-start.43 = (bf16[256,2048]{1,0:T(8,128)(2,1)}, bf16[256,2048]{1,0:T(8,128)(2,1)S(1)}, u32[]{:S(2)}, u32[]{:S(2)}) collective-permute-start(bf16[256,2048]{1,0:T(8,128)(2,1)} %collective-permute-done.36), channel_id=1, source_target_pairs={{0,1},{1,0},{2,3},{3,2},{4,5},{5,4},{6,7},{7,6},{8,9},{9,8},{10,11... | collective-permute-start | bytes 3145736 | tf_op jit(solution)/shard_map/ppermute | solution.py:122
  770.8 238.7 %collective-permute-start.35 = (bf16[256,2048]{1,0:T(8,128)(2,1)}, bf16[256,2048]{1,0:T(8,128)(2,1)}, u32[]{:S(2)}, u32[]{:S(2)}) collective-permute-start(bf16[256,2048]{1,0:T(8,128)(2,1)} %slice.683), channel_id=1, source_target_pairs={{0,1},{1,0},{2,3},{3,2},{4,5},{5,4},{6,7},{7,6},{8,9},{9,8},{10,11... | collective-permute-start | bytes 3145736 | tf_op jit(solution)/shard_map/ppermute | solution.py:122
  770.9 26.9 %collective-permute-start.37 = (bf16[256,2048]{1,0:T(8,128)(2,1)}, bf16[256,2048]{1,0:T(8,128)(2,1)S(1)}, u32[]{:S(2)}, u32[]{:S(2)}) collective-permute-start(bf16[256,2048]{1,0:T(8,128)(2,1)} %collective-permute-done.36), channel_id=1, source_target_pairs={{0,8},{1,25},{2,10},{3,27},{4,12},{5,29},{6,14},{7,31},{8,16},{9,1... | collective-permute-start | bytes 3145736 | tf_op jit(solution)/shard_map/ppermute | solution.py:122
  809.1 36.3 %collective-permute-start.44 = (bf16[256,2048]{1,0:T(8,128)(2,1)}, bf16[256,2048]{1,0:T(8,128)(2,1)}, u32[]{:S(2)}, u32[]{:S(2)}) collective-permute-start(bf16[256,2048]{1,0:T(8,128)(2,1)} %slice.680), channel_id=1, source_target_pairs={{0,1},{1,0},{2,3},{3,2},{4,5},{5,4},{6,7},{7,6},{8,9},{9,8},{10,11... | collective-permute-start | bytes 3145736 | tf_op jit(solution)/shard_map/ppermute | solution.py:122
  809.6 35.7 %collective-permute-start.38 = (bf16[256,2048]{1,0:T(8,128)(2,1)S(1)}, bf16[256,2048]{1,0:T(8,128)(2,1)S(1)}, u32[]{:S(2)}, u32[]{:S(2)}) collective-permute-start(bf16[256,2048]{1,0:T(8,128)(2,1)S(1)} %collective-permute-done.37), channel_id=1, source_target_pairs={{0,8},{1,25},{2,10},{3,27},{4,12},{5,29},{6,14},{7,31},{8,16},{9,1... | collective-permute-start | bytes 3145736 | tf_op jit(solution)/shard_map/ppermute | solution.py:122
  843.3 130.3 %collective-permute-start.42 = (bf16[256,2048]{1,0:T(8,128)(2,1)}, bf16[256,2048]{1,0:T(8,128)(2,1)}, u32[]{:S(2)}, u32[]{:S(2)}) collective-permute-start(bf16[256,2048]{1,0:T(8,128)(2,1)} %slice.681), channel_id=1, source_target_pairs={{0,1},{1,0},{2,3},{3,2},{4,5},{5,4},{6,7},{7,6},{8,9},{9,8},{10,11... | collective-permute-start | bytes 3145736 | tf_op jit(solution)/shard_map/ppermute | solution.py:122
  848.8 124.8 %collective-permute-start.45 = (bf16[256,2048]{1,0:T(8,128)(2,1)}, bf16[256,2048]{1,0:T(8,128)(2,1)}, u32[]{:S(2)}, u32[]{:S(2)}) collective-permute-start(bf16[256,2048]{1,0:T(8,128)(2,1)} %fusion.115), channel_id=1, source_target_pairs={{0,8},{1,25},{2,10},{3,27},{4,12},{5,29},{6,14},{7,31},{8,16},{9,1... | collective-permute-start | bytes 3145736 | tf_op jit(solution)/shard_map/ppermute | solution.py:122
  883.9 123.3 %collective-permute-start.64 = (bf16[2,256,512]{2,1,0:T(8,128)(2,1)}, bf16[2,256,512]{2,1,0:T(8,128)(2,1)}, u32[]{:S(2)}, u32[]{:S(2)}) collective-permute-start(bf16[2,256,512]{2,1,0:T(8,128)(2,1)} %fusion.178), channel_id=1, source_target_pairs={{0,1},{1,0},{2,3},{3,2},{4,5},{5,4},{6,7},{7,6},{8,9},{9,8},{10,11... | collective-permute-start | bytes 1572872 | tf_op jit(solution)/shard_map/ppermute | solution.py:122
  968.8 16.3 %collective-permute-start.40 = (bf16[256,2048]{1,0:T(8,128)(2,1)S(1)}, bf16[256,2048]{1,0:T(8,128)(2,1)S(1)}, u32[]{:S(2)}, u32[]{:S(2)}) collective-permute-start(bf16[256,2048]{1,0:T(8,128)(2,1)S(1)} %slice.682), channel_id=1, source_target_pairs={{0,1},{1,0},{2,3},{3,2},{4,5},{5,4},{6,7},{7,6},{8,9},{9,8},{10,11... | collective-permute-start | bytes 3145736 | tf_op jit(solution)/shard_map/ppermute | solution.py:122
  975.7 25.7 %collective-permute-start.46 = (bf16[256,2048]{1,0:T(8,128)(2,1)S(1)}, bf16[256,2048]{1,0:T(8,128)(2,1)S(1)}, u32[]{:S(2)}, u32[]{:S(2)}) collective-permute-start(bf16[256,2048]{1,0:T(8,128)(2,1)S(1)} %fusion.117), channel_id=1, source_target_pairs={{0,8},{1,25},{2,10},{3,27},{4,12},{5,29},{6,14},{7,31},{8,16},{9,1... | collective-permute-start | bytes 3145736 | tf_op jit(solution)/shard_map/ppermute | solution.py:122
  978.5 87.5 %collective-permute-start.67 = (bf16[8,288,512]{2,1,0:T(8,128)(2,1)}, bf16[8,288,512]{2,1,0:T(8,128)(2,1)}, u32[]{:S(2)}, u32[]{:S(2)}) collective-permute-start(bf16[8,288,512]{2,1,0:T(8,128)(2,1)} %get-tuple-element.105), channel_id=1, source_target_pairs={{0,2},{1,3},{2,0},{3,1},{4,6},{5,7},{6,4},{7,5},{8,10},{9,11},{10,... | collective-permute-start | bytes 7077896 | tf_op jit(solution)/shard_map/ppermute | solution.py:122
  985.1 86.4 %collective-permute-start.70 = (bf16[8,288,512]{2,1,0:T(8,128)(2,1)}, bf16[8,288,512]{2,1,0:T(8,128)(2,1)}, u32[]{:S(2)}, u32[]{:S(2)}) collective-permute-start(bf16[8,288,512]{2,1,0:T(8,128)(2,1)} %get-tuple-element.103), channel_id=1, source_target_pairs={{0,4},{1,5},{2,6},{3,7},{4,0},{5,1},{6,2},{7,3},{8,12},{9,13},{10,... | collective-permute-start | bytes 7077896 | tf_op jit(solution)/shard_map/ppermute | solution.py:122
  1001.8 25.5 %collective-permute-start.47 = (bf16[256,2048]{1,0:T(8,128)(2,1)S(1)}, bf16[256,2048]{1,0:T(8,128)(2,1)S(1)}, u32[]{:S(2)}, u32[]{:S(2)}) collective-permute-start(bf16[256,2048]{1,0:T(8,128)(2,1)S(1)} %fusion.119), channel_id=1, source_target_pairs={{0,8},{1,25},{2,10},{3,27},{4,12},{5,29},{6,14},{7,31},{8,16},{9,1... | collective-permute-start | bytes 3145736 | tf_op jit(solution)/shard_map/ppermute | solution.py:122
  1007.3 82.1 %collective-permute-start.75 = (bf16[8,288,512]{2,1,0:T(8,128)(2,1)}, bf16[8,288,512]{2,1,0:T(8,128)(2,1)}, u32[]{:S(2)}, u32[]{:S(2)}) collective-permute-start(bf16[8,288,512]{2,1,0:T(8,128)(2,1)} %get-tuple-element.101), channel_id=1, source_target_pairs={{0,4},{1,5},{2,6},{3,7},{4,0},{5,1},{6,2},{7,3},{8,12},{9,13},{10,... | collective-permute-start | bytes 7077896 | tf_op jit(solution)/shard_map/ppermute | solution.py:122
  1033.5 32.6 %collective-permute-start.48 = (bf16[256,2048]{1,0:T(8,128)(2,1)}, bf16[256,2048]{1,0:T(8,128)(2,1)}, u32[]{:S(2)}, u32[]{:S(2)}) collective-permute-start(bf16[256,2048]{1,0:T(8,128)(2,1)} %get-tuple-element.94), channel_id=1, source_target_pairs={{0,2},{1,3},{2,0},{3,1},{4,6},{5,7},{6,4},{7,5},{8,10},{9,11},{10,... | collective-permute-start | bytes 3145736 | tf_op jit(solution)/shard_map/ppermute | solution.py:122
  1035.4 27.5 %collective-permute-start.65 = (bf16[256,512]{1,0:T(8,128)(2,1)S(1)}, bf16[256,512]{1,0:T(8,128)(2,1)}, u32[]{:S(2)}, u32[]{:S(2)}) collective-permute-start(bf16[256,512]{1,0:T(8,128)(2,1)S(1)} %fusion.198), channel_id=1, source_target_pairs={{0,2},{1,3},{2,0},{3,1},{4,6},{5,7},{6,4},{7,5},{8,10},{9,11},{10,... | collective-permute-start | bytes 786440 | tf_op jit(solution)/shard_map/ppermute | solution.py:122
  1062.9 70.6 %collective-permute-start.66 = (bf16[8,288,512]{2,1,0:T(8,128)(2,1)}, bf16[8,288,512]{2,1,0:T(8,128)(2,1)}, u32[]{:S(2)}, u32[]{:S(2)}) collective-permute-start(bf16[8,288,512]{2,1,0:T(8,128)(2,1)} %get-tuple-element.104), channel_id=1, source_target_pairs={{0,2},{1,3},{2,0},{3,1},{4,6},{5,7},{6,4},{7,5},{8,10},{9,11},{10,... | collective-permute-start | bytes 7077896 | tf_op jit(solution)/shard_map/ppermute | solution.py:122
  1066.0 28.3 %collective-permute-start.50 = (bf16[256,2048]{1,0:T(8,128)(2,1)}, bf16[256,2048]{1,0:T(8,128)(2,1)S(1)}, u32[]{:S(2)}, u32[]{:S(2)}) collective-permute-start(bf16[256,2048]{1,0:T(8,128)(2,1)} %get-tuple-element.94), channel_id=1, source_target_pairs={{0,1},{1,0},{2,3},{3,2},{4,5},{5,4},{6,7},{7,6},{8,9},{9,8},{10,11... | collective-permute-start | bytes 3145736 | tf_op jit(solution)/shard_map/ppermute | solution.py:122
  1066.1 29.5 %collective-permute-start.49 = (bf16[256,2048]{1,0:T(8,128)(2,1)}, bf16[256,2048]{1,0:T(8,128)(2,1)S(1)}, u32[]{:S(2)}, u32[]{:S(2)}) collective-permute-start(bf16[256,2048]{1,0:T(8,128)(2,1)} %collective-permute-done.48), channel_id=1, source_target_pairs={{0,1},{1,0},{2,3},{3,2},{4,5},{5,4},{6,7},{7,6},{8,9},{9,8},{10,11... | collective-permute-start | bytes 3145736 | tf_op jit(solution)/shard_map/ppermute | solution.py:122
  1071.5 231.0 %collective-permute-start.69 = (bf16[8,288,512]{2,1,0:T(8,128)(2,1)}, bf16[8,288,512]{2,1,0:T(8,128)(2,1)}, u32[]{:S(2)}, u32[]{:S(2)}) collective-permute-start(bf16[8,288,512]{2,1,0:T(8,128)(2,1)} %get-tuple-element.102), channel_id=1, source_target_pairs={{0,4},{1,5},{2,6},{3,7},{4,0},{5,1},{6,2},{7,3},{8,12},{9,13},{10,... | collective-permute-start | bytes 7077896 | tf_op jit(solution)/shard_map/ppermute | solution.py:122
  1089.4 268.2 %collective-permute-start.74 = (bf16[8,288,512]{2,1,0:T(8,128)(2,1)}, bf16[8,288,512]{2,1,0:T(8,128)(2,1)}, u32[]{:S(2)}, u32[]{:S(2)}) collective-permute-start(bf16[8,288,512]{2,1,0:T(8,128)(2,1)} %get-tuple-element.100), channel_id=1, source_target_pairs={{0,4},{1,5},{2,6},{3,7},{4,0},{5,1},{6,2},{7,3},{8,12},{9,13},{10,... | collective-permute-start | bytes 7077896 | tf_op jit(solution)/shard_map/ppermute | solution.py:122
  1094.3 173.1 %collective-permute-start.68 = (bf16[8,288,512]{2,1,0:T(8,128)(2,1)}, bf16[8,288,512]{2,1,0:T(8,128)(2,1)}, u32[]{:S(2)}, u32[]{:S(2)}) collective-permute-start(bf16[8,288,512]{2,1,0:T(8,128)(2,1)} %add_convert_fusion.7), channel_id=1, source_target_pairs={{0,4},{1,5},{2,6},{3,7},{4,0},{5,1},{6,2},{7,3},{8,12},{9,13},{10,... | collective-permute-start | bytes 7077896 | tf_op jit(solution)/shard_map/ppermute | solution.py:122
  1119.7 182.8 %collective-permute-start.71 = (bf16[8,288,512]{2,1,0:T(8,128)(2,1)}, bf16[8,288,512]{2,1,0:T(8,128)(2,1)}, u32[]{:S(2)}, u32[]{:S(2)}) collective-permute-start(bf16[8,288,512]{2,1,0:T(8,128)(2,1)} %add_convert_fusion.4), channel_id=1, source_target_pairs={{0,2},{1,3},{2,0},{3,1},{4,6},{5,7},{6,4},{7,5},{8,10},{9,11},{10,... | collective-permute-start | bytes 7077896 | tf_op jit(solution)/shard_map/ppermute | solution.py:122
  1133.5 224.1 %collective-permute-start.76 = (bf16[8,288,512]{2,1,0:T(8,128)(2,1)}, bf16[8,288,512]{2,1,0:T(8,128)(2,1)}, u32[]{:S(2)}, u32[]{:S(2)}) collective-permute-start(bf16[8,288,512]{2,1,0:T(8,128)(2,1)} %add_convert_fusion.1), channel_id=1, source_target_pairs={{0,2},{1,3},{2,0},{3,1},{4,6},{5,7},{6,4},{7,5},{8,10},{9,11},{10,... | collective-permute-start | bytes 7077896 | tf_op jit(solution)/shard_map/ppermute | solution.py:122
  1271.4 59.5 %all-to-all-start.6 = ((bf16[8,288,512]{2,1,0:T(8,128)(2,1)}), bf16[8,288,512]{2,1,0:T(8,128)(2,1)}, u32[]{:S(2)}, u32[]{:S(2)}) async-start(bf16[8,288,512]{2,1,0:T(8,128)(2,1)} %add_convert_fusion.6), calls=%async_computation.8 | async-start | bytes 4718592 | tf_op jit(solution)/shard_map/all_to_all | solution.py:233
  1330.9 85.1 %all-to-all-start.7 = ((bf16[8,288,512]{2,1,0:T(8,128)(2,1)}), bf16[8,288,512]{2,1,0:T(8,128)(2,1)S(1)}, u32[]{:S(2)}, u32[]{:S(2)}) async-start(bf16[8,288,512]{2,1,0:T(8,128)(2,1)} %add_convert_fusion.3), calls=%async_computation.9 | async-start | bytes 4718592 | tf_op jit(solution)/shard_map/all_to_all | solution.py:233
  1334.5 211.6 %reduce-scatter.3.cloned.1.call-start = ((), (), s32[]{:S(2)}) async-start(), calls=%async_computation.11 | async-start | bytes 4644864 | tf_op jit(solution)/shard_map/reduce_scatter | solution.py:557
  1355.1 69.2 %collective-permute-start.54 = (bf16[256,2048]{1,0:T(8,128)(2,1)}, bf16[256,2048]{1,0:T(8,128)(2,1)S(1)}, u32[]{:S(2)}, u32[]{:S(2)}) collective-permute-start(bf16[256,2048]{1,0:T(8,128)(2,1)} %fusion.162), channel_id=1, source_target_pairs={{0,2},{1,3},{2,0},{3,1},{4,6},{5,7},{6,4},{7,5},{8,10},{9,11},{10,... | collective-permute-start | bytes 3145736 | tf_op jit(solution)/shard_map/ppermute | solution.py:122
  1416.0 94.9 %all-to-all-start.8 = ((bf16[8,288,512]{2,1,0:T(8,128)(2,1)}), bf16[8,288,512]{2,1,0:T(8,128)(2,1)}, u32[]{:S(2)}, u32[]{:S(2)}) async-start(bf16[8,288,512]{2,1,0:T(8,128)(2,1)} %add_convert_fusion), calls=%async_computation.10 | async-start | bytes 4718592 | tf_op jit(solution)/shard_map/all_to_all | solution.py:233
  1433.1 18.7 %collective-permute-start.56 = (f32[3,2048]{1,0:T(4,128)S(1)}, f32[3,2048]{1,0:T(4,128)S(1)}, u32[]{:S(2)}, u32[]{:S(2)}) collective-permute-start(f32[3,2048]{1,0:T(4,128)S(1)} %fusion.232), channel_id=1, source_target_pairs={{0,4},{1,5},{2,6},{3,7},{4,0},{5,1},{6,2},{7,3},{8,12},{9,13},{10,... | collective-permute-start | bytes 73736 | tf_op jit(solution)/shard_map/ppermute | solution.py:122
  1463.6 31.7 %collective-permute-start.58 = (f32[3,2048]{1,0:T(4,128)S(1)}, f32[3,2048]{1,0:T(4,128)S(1)}, u32[]{:S(2)}, u32[]{:S(2)}) collective-permute-start(f32[3,2048]{1,0:T(4,128)S(1)} %add.389), channel_id=1, source_target_pairs={{0,16},{1,17},{2,18},{3,19},{4,20},{5,21},{6,22},{7,23},{8,24},{9,... | collective-permute-start | bytes 73736 | tf_op jit(solution)/shard_map/ppermute | solution.py:122
  1510.9 23.3 %all-to-all-start.5 = ((bf16[4,256,512]{2,1,0:T(8,128)(2,1)}), bf16[4,256,512]{2,1,0:T(8,128)(2,1)S(1)}, u32[]{:S(2)}, u32[]{:S(2)}) async-start(bf16[4,256,512]{2,1,0:T(8,128)(2,1)} %bitcast.461), calls=%async_computation.5 | async-start | bytes 2097152 | tf_op jit(solution)/shard_map/all_to_all | solution.py:233
  (173 other events, 3293.4 us)
Sparse Core Ops, SparseCore 0:
  10.8 115.0 all-gather.4
  135.8 158.2 all-gather.6
  1124.2 106.4 reduce-scatter.4
  1349.2 147.5 reduce-scatter.2

commit v2 on v1

v2 whole, which is shorter than its diff:
```python
import jax
import jax.numpy as jnp
from jax import lax
from jax.sharding import PartitionSpec as P

NORM_EPS = 1e-06
BF = jnp.bfloat16
F32 = jnp.float32


def product(former, latter):
    return jnp.dot(former, latter, preferred_element_type=F32)


def left_trans(former, latter):
    return lax.dot_general(
        former, latter, (((0,), (0,)), ((), ())), preferred_element_type=F32
    )


def right_trans(former, latter):
    return lax.dot_general(
        former, latter, (((1,), (1,)), ((), ())), preferred_element_type=F32
    )


def angles(length, head_size):
    half_size = head_size // 2
    inverse = 10000.0 ** (-(jnp.arange(half_size, dtype=F32) * 2.0 / head_size))
    theta = jnp.arange(length, dtype=F32)[:, None] * inverse[None, :]
    return (jnp.cos(theta), jnp.sin(theta))


def rotate(values_in, cosine_table, sine_table):
    half_size = values_in.shape[-1] // 2
    first_half = values_in[..., :half_size]
    second_half = values_in[..., half_size:]
    return jnp.concatenate(
        [
            first_half * cosine_table - second_half * sine_table,
            second_half * cosine_table + first_half * sine_table,
        ],
        axis=-1,
    )


def allowed_mask(key_count, length):
    row_place = jnp.arange(key_count)[:, None]
    col_place = jnp.arange(key_count)[None, :]
    return ((col_place <= row_place) & (col_place < length))[None]


def attend_forward(query_rows, key_rows, value_rows, length):
    allowed = allowed_mask(key_rows.shape[0], length)
    scores = jnp.einsum("hqd,kd->hqk", query_rows, key_rows, preferred_element_type=F32)
    masked = jnp.where(allowed, scores, -1e30)
    largest = jnp.max(masked, axis=-1, keepdims=True)
    exponent = jnp.exp(masked - largest)
    totals = jnp.sum(exponent, axis=-1, keepdims=True)
    probability = (exponent / totals).astype(BF)
    attended = jnp.einsum("hqk,kd->hqd", probability, value_rows, preferred_element_type=F32)
    return (attended.astype(BF), (largest + jnp.log(totals))[..., 0])


def attend_backward(query_rows, key_rows, value_rows, length, log_total, grad_out):
    allowed = allowed_mask(key_rows.shape[0], length)
    scores = jnp.einsum("hqd,kd->hqk", query_rows, key_rows, preferred_element_type=F32)
    probability = jnp.where(allowed, jnp.exp(scores - log_total[..., None]), 0.0)
    grad_prob = jnp.einsum("hqd,kd->hqk", grad_out, value_rows, preferred_element_type=F32)
    row_terms = jnp.sum(probability * grad_prob, axis=-1, keepdims=True)
    grad_scores = (probability * (grad_prob - row_terms)).astype(BF)
    grad_query = jnp.einsum("hqk,kd->hqd", grad_scores, key_rows, preferred_element_type=F32)
    grad_key = jnp.einsum("hqk,hqd->kd", grad_scores, query_rows, preferred_element_type=F32)
    grad_value = jnp.einsum(
        "hqk,hqd->kd", probability.astype(BF), grad_out, preferred_element_type=F32
    )
    return (grad_query, grad_key, grad_value)


def norm_scale(values_in):
    return lax.rsqrt(jnp.mean(values_in * values_in, axis=-1, keepdims=True) + NORM_EPS)


def norm_forward(values_in, gain_row):
    row_scale = norm_scale(values_in)
    return ((values_in * row_scale * (1.0 + gain_row)).astype(BF), row_scale)


def norm_backward(grad_rows, rows_in, gain_row, row_scale):
    factor = 1.0 + gain_row
    row_dots = jnp.sum(grad_rows * factor * rows_in, axis=-1, keepdims=True)
    grad_input = (
        row_scale * factor * grad_rows
        - rows_in * (row_scale * row_scale * row_scale) * row_dots / rows_in.shape[1]
    )
    return (grad_input, jnp.sum(grad_rows * rows_in * row_scale, axis=0))


def geglu(gate_lin, up_lin):
    return jax.nn.gelu(gate_lin, approximate=True) * up_lin


def solution(mesh):
    row_devices = mesh.shape["rows"]
    col_devices = mesh.shape["cols"]
    nk = 2
    nx = col_devices // nk
    nz = 4 if row_devices % 4 == 0 else row_devices
    ny = row_devices // nz
    BOTH = ("rows", "cols")

    def permute(value, move):
        pairs = []
        for z in range(nz):
            for y in range(ny):
                for x in range(nx):
                    for k in range(nk):
                        tz, ty, tx, tk = move(z, y, x, k)
                        source = (z * ny + y) * col_devices + x * nk + k
                        target = (tz * ny + ty) * col_devices + tx * nk + tk
                        pairs.append((source, target))
        return lax.ppermute(value, BOTH, pairs)

    def swap_z(value, mask):
        return permute(value, lambda z, y, x, k: (z ^ mask, y, x, k))

    def swap_y(value, mask):
        return permute(value, lambda z, y, x, k: (z, y ^ mask, x, k))

    def swap_x(value, mask):
        return permute(value, lambda z, y, x, k: (z, y, x ^ mask, k))

    def swap_k(value):
        return permute(value, lambda z, y, x, k: (z, y, x, k ^ 1))

    def ring(value):
        return permute(
            value, lambda z, y, x, k: ((z + 1) % nz if k == 0 else (z - 1) % nz, y, x, k)
        )

    def natural(parts, place):
        count = len(parts)
        arrays = list(parts)
        bit = 1
        while bit < count:
            hot = (place & bit) != 0
            arrays = [
                jnp.where(hot, arrays[slot ^ bit], arrays[slot]) for slot in range(count)
            ]
            bit *= 2
        return arrays

    def gather_cols(value, place):
        parts = [None] * col_devices
        for mask in range(nx):
            near = value if mask == 0 else swap_x(value, mask)
            parts[mask * nk] = near
            parts[mask * nk + 1] = swap_k(near)
        return natural(parts, place)

    def scatter_rest(kept, place_x):
        near = lax.dynamic_index_in_dim(kept, place_x, 0, keepdims=False)
        for mask in range(1, nx):
            away = lax.dynamic_index_in_dim(kept, place_x ^ mask, 0, keepdims=False)
            near = near + swap_x(away.astype(BF), mask).astype(F32)
        return near

    def scatter_cols(blocks, place_x, place_k, make):
        hot = place_k == 0
        away = jnp.where(hot, blocks[:, 1], blocks[:, 0])
        near = jnp.where(hot, blocks[:, 0], blocks[:, 1])
        got = swap_k(make(away).astype(BF))
        kept = make(near) + got.astype(F32)
        return scatter_rest(kept, place_x)

    def row_parts(value):
        parts = []
        for mask_z in range(nz):
            near = value if mask_z == 0 else swap_z(value, mask_z)
            parts.append(near)
            parts.extend(swap_y(near, mask) for mask in range(1, ny))
        return parts

    def scatter_y(blocks, place_y):
        blocks = blocks.reshape(nz, ny, *blocks.shape[1:])
        kept = lax.dynamic_index_in_dim(blocks, place_y, 1, keepdims=False)
        got = []
        for mask in range(1, ny):
            away = lax.dynamic_index_in_dim(blocks, place_y ^ mask, 1, keepdims=False)
            got.append(swap_y(away, mask))
        return [kept] + got

    def scatter_z(parts, place_z):
        kept = sum(part.astype(F32) for part in parts)
        got = [lax.dynamic_index_in_dim(kept, place_z, 0, keepdims=False)]
        for mask in range(1, nz):
            away = lax.dynamic_index_in_dim(kept, place_z ^ mask, 0, keepdims=False)
            got.append(swap_z(away.astype(BF), mask))
        return got

    def total(parts):
        return sum(part.astype(F32) for part in parts)

    def sum_all(value):
        for mask_count, swap in ((nz, swap_z), (ny, swap_y), (nx, swap_x)):
            bit = 1
            while bit < mask_count:
                value = value + swap(value, bit)
                bit *= 2
        return value + swap_k(value)

    def after(value, *others):
        return lax.optimization_barrier((value, *others))[0]

    def spread_x(own):
        return [own] + [swap_x(own, mask) for mask in range(1, nx)]

    def exchange(value, axis):
        return lax.all_to_all(value, axis, 0, 0, tiled=True)

    def shards(
        tokens,
        gain_attn,
        gain_mlp,
        w_q,
        w_kv,
        a_qkv,
        b_q,
        b_kv,
        w_o,
        a_o,
        b_o,
        w_gate,
        w_up,
        a_gu,
        b_gate,
        b_up,
        w_down,
        a_down,
        b_down,
        lengths,
        teacher,
        out_grad,
    ):
        row_place = lax.axis_index("rows")
        col_place = lax.axis_index("cols")
        place_x = col_place // nk
        place_z = row_place // ny
        place_y = row_place % ny
        place_k = col_place % nk
        row_count, local_features = tokens.shape
        features = local_features * col_devices
        seq_len = row_count * row_devices // lengths.shape[0]
        seqs_here = row_count // seq_len
        own_rows = row_count // col_devices
        rank = a_qkv.shape[1]
        block_d = w_q.shape[0]
        block_r = b_q.shape[0]
        block_e = block_d + block_r
        q_width = w_q.shape[1]
        kv_width = w_kv.shape[1]
        head_size = kv_width * col_devices // 2
        heads_here = q_width // head_size
        hidden_part = w_gate.shape[1] // row_devices
        lens_here = lax.dynamic_slice_in_dim(lengths, row_place * seqs_here, seqs_here)

        gain_rows = jnp.concatenate(
            [gain_attn[None], gain_mlp[None], jnp.zeros((14, local_features), BF)], axis=0
        )
        gain_full = jnp.concatenate(gather_cols(gain_rows, col_place), axis=1).astype(F32)
        gain_one = gain_full[0:1]
        gain_two = gain_full[1:2]
        full_x = jnp.concatenate(gather_cols(tokens, col_place), axis=1)

        pack_one = jnp.concatenate(
            [
                jnp.concatenate([w_q, w_kv, a_qkv], axis=1),
                jnp.concatenate([b_q, b_kv, jnp.zeros((block_r, rank), BF)], axis=1),
            ],
            axis=0,
        )
        got_one = jnp.stack(natural(row_parts(pack_one), row_place))
        slice_r = rank // col_devices
        own_a_gu = lax.dynamic_slice_in_dim(a_gu, col_place * slice_r, slice_r, 1)
        wide = lax.all_gather(
            jnp.concatenate([b_o, b_down, own_a_gu.reshape(-1, local_features)], axis=0),
            BOTH,
            axis=0,
            tiled=False,
        )

        def hidden_blocks(value):
            blocks = value.reshape(value.shape[0], row_devices, hidden_part)
            return blocks.transpose(1, 0, 2)

        def hidden_slice(value):
            return exchange(value, "rows").reshape(features, hidden_part)

        side_blocks = jnp.stack(
            [hidden_blocks(b_gate), hidden_blocks(b_up), hidden_blocks(a_down.T)], axis=1
        )
        normed, scale_one = norm_forward(full_x.astype(F32), gain_one)
        gate_own = hidden_slice(hidden_blocks(w_gate))
        pack_two = jnp.concatenate([w_o.T, a_o.T], axis=0)
        pack_two, side_blocks, gate_own, got_one = lax.optimization_barrier(
            (pack_two, side_blocks, gate_own, got_one)
        )
        parts_two = row_parts(pack_two)
        gate_parts = spread_x(gate_own)
        side_own = exchange(side_blocks, "rows")
        full_a_qkv = got_one[:, :block_d, q_width + kv_width :].reshape(features, rank)
        qkv_base = got_one[:, :block_d, : q_width + kv_width].reshape(
            features, q_width + kv_width
        )
        full_b_qkv = got_one[:, block_d:, : q_width + kv_width].reshape(rank, q_width + kv_width)
        w_qkv = (qkv_base.astype(F32) + product(full_a_qkv, full_b_qkv)).astype(BF)

        kv_piece = product(normed, w_qkv[:, q_width:])
        kv_parts = gather_cols(kv_piece, col_place)
        q_lin = product(normed, w_qkv[:, :q_width])
        kv_lin = jnp.concatenate(kv_parts, axis=1)
        up_blocks, side_own, q_lin = lax.optimization_barrier(
            (hidden_blocks(w_up), side_own, q_lin)
        )
        up_own = hidden_slice(up_blocks)
        side_parts = spread_x(side_own.transpose(1, 0, 2, 3).reshape(3, rank, hidden_part))
        query_scale = head_size ** (-0.5)
        cosine_table, sine_table = angles(seq_len, head_size)
        queries = q_lin.reshape(seqs_here, seq_len, heads_here, head_size).transpose(0, 2, 1, 3)
        queries = (rotate(queries, cosine_table, sine_table) * query_scale).astype(BF)
        keys = rotate(
            kv_lin[:, :head_size].reshape(seqs_here, seq_len, head_size),
            cosine_table,
            sine_table,
        ).astype(BF)
        values = kv_lin[:, head_size:].reshape(seqs_here, seq_len, head_size).astype(BF)
        forward_parts = [
            attend_forward(queries[s], keys[s], values[s], lens_here[s])
            for s in range(seqs_here)
        ]
        attn_rows = jnp.concatenate(
            [part[0].transpose(1, 0, 2).reshape(seq_len, q_width) for part in forward_parts],
            axis=0,
        )
        attn_rows, up_own, gate_parts, wide, *parts_two = lax.optimization_barrier(
            (attn_rows, up_own, gate_parts, wide, *parts_two)
        )
        up_parts = spread_x(up_own)
        down_blocks, up_own = lax.optimization_barrier((hidden_blocks(w_down.T), up_own))
        down_own = hidden_slice(down_blocks)
        got_two = jnp.stack(natural(parts_two, row_place))
        o_base = got_two[:, :block_d].reshape(features, q_width)
        full_a_o_t = got_two[:, block_d:block_e].reshape(rank, q_width)
        wide = wide.reshape(row_devices, col_devices, -1, local_features)

        def whole_b(start):
            value = wide[:, :, start : start + block_r]
            return value.transpose(0, 2, 1, 3).reshape(rank, features)

        full_b_o = whole_b(0)
        w_o_t = (o_base.astype(F32) + left_trans(full_b_o, full_a_o_t)).astype(BF)

        def scatter_tokens(rows, weight):
            blocks = rows.reshape(nx, nk, own_rows, rows.shape[1])
            hot = place_k == 0

            def partial_sum(first, second):
                block = jnp.where(hot, blocks[:, first], blocks[:, second])
                return right_trans(block.reshape(nx * own_rows, rows.shape[1]), weight)

            kept = swap_k(partial_sum(1, 0).astype(BF)).astype(F32) + partial_sum(0, 1)
            kept = kept.reshape(nx, own_rows, features)
            sent = [
                lax.dynamic_index_in_dim(kept, place_x ^ mask, 0, keepdims=False).astype(BF)
                for mask in range(1, nx)
            ]
            return (lax.dynamic_index_in_dim(kept, place_x, 0, keepdims=False), sent)

        def finish_tokens(near, sent):
            return near + total([swap_x(value, i + 1) for i, value in enumerate(sent)])

        near_one, sent_one = scatter_tokens(attn_rows, w_o_t)
        up_parts, side_parts, sent_one = lax.optimization_barrier(
            (up_parts, side_parts, sent_one)
        )
        branch_one = finish_tokens(near_one, sent_one)
        own_x = lax.dynamic_slice_in_dim(full_x, col_place * own_rows, own_rows, 0).astype(F32)
        own_scale = lax.dynamic_slice_in_dim(scale_one, col_place * own_rows, own_rows, 0)
        middle = own_x + branch_one
        down_own, middle = lax.optimization_barrier((down_own, middle))
        full_b_down = whole_b(block_r)
        full_b_down_t = full_b_down.T
        full_a_gu = wide[:, :, 2 * block_r :].reshape(row_devices, col_devices, block_d, slice_r)
        full_a_gu = full_a_gu.transpose(0, 2, 1, 3).reshape(features, rank)
        gate_sides = [part[0] for part in side_parts]
        up_sides = [part[1] for part in side_parts]
        down_sides = [part[2] for part in side_parts]

        def joined(bases, sides, factor):
            parts = [
                (base.astype(F32) + product(factor, side)).astype(BF)
                for base, side in zip(bases, sides)
            ]
            return jnp.concatenate(parts, axis=1)

        middle_low = middle.astype(BF).astype(F32)
        normed_two, scale_two = norm_forward(middle_low, gain_two)

        def gather_ring(value):
            chunks = []
            for step in range(nz):
                lines = [swap_y(value, mask) for mask in range(1, ny)]
                near = value
                if step + 1 < nz:
                    value = ring(value)
                    lines, value = lax.optimization_barrier((lines, value))
                for line in [near] + lines:
                    chunks.append(jnp.concatenate([line, swap_k(line)], axis=0))
            return chunks

        def scatter_ring(parts):
            totals = []
            for step in list(range(1, nz)) + [0]:
                mine = None
                for mask in reversed(range(ny)):
                    part = parts[step * ny + mask]
                    away = swap_k(part[own_rows:].astype(BF))
                    chip = part[:own_rows] + away.astype(F32)
                    if mask:
                        chip = swap_y(chip.astype(BF), mask).astype(F32)
                    mine = chip if mine is None else mine + chip
                if totals:
                    mine = mine + ring(totals[-1]).astype(F32)
                totals.append(mine.astype(BF) if step else mine)
            return totals

        normed_chunks = gather_ring(normed_two)
        gate_w = joined(gate_parts, gate_sides, full_a_gu)
        up_w = joined(up_parts, up_sides, full_a_gu)
        down_parts = spread_x(down_own)
        down_parts, normed_chunks[-ny] = lax.optimization_barrier(
            (down_parts, normed_chunks[-ny])
        )
        down_w = joined(down_parts, down_sides, full_b_down_t)
        pair = jnp.stack([teacher, out_grad]).reshape(
            2, col_devices, own_rows, local_features
        )
        pair = exchange(after(pair.transpose(1, 0, 2, 3), down_own), "cols")
        gates, ups, hiddens, parts = [], [], [], []
        for chunk in normed_chunks:
            gate_lin = product(chunk, gate_w)
            up_lin = product(chunk, up_w)
            hidden = geglu(gate_lin, up_lin).astype(BF)
            gates.append(gate_lin)
            ups.append(up_lin)
            hiddens.append(hidden)
            parts.append(right_trans(hidden, down_w))
        pair, parts[0] = lax.optimization_barrier((pair, parts[0]))
        pair = pair.transpose(1, 2, 0, 3).reshape(2, own_rows, features)
        teacher_own = pair[0].astype(F32)
        out_grad_own = pair[1].astype(F32)
        result = middle + scatter_ring(parts)[-1]

        spots = col_place * own_rows + jnp.arange(own_rows)
        limits = jnp.take(lens_here, spots // seq_len) if seqs_here > 1 else lens_here[0]
        valid_rows = ((spots % seq_len) < limits).astype(F32)[:, None]
        valid_count = jnp.sum(lengths).astype(F32)
        error_rows = result - teacher_own
        square = jnp.sum(error_rows * error_rows * valid_rows)
        total_tokens = row_count * row_devices
        seed_grad = out_grad_own + total_tokens / valid_count * error_rows * valid_rows
        grad_two = seed_grad.astype(BF)

        def to_columns(value):
            blocks = value.reshape(own_rows, col_devices, local_features).transpose(1, 0, 2)
            parts = []
            for mask in range(col_devices):
                block = lax.dynamic_index_in_dim(blocks, col_place ^ mask, 0, keepdims=False)
                if mask:
                    block = permute(
                        block,
                        lambda z, y, x, k, mask=mask: (z, y, x ^ (mask // nk), k ^ (mask % nk)),
                    )
                parts.append(block)
            return jnp.concatenate(natural(parts, col_place), axis=0)


        grad_chunks = gather_ring(grad_two)
        d_gates, d_ups, parts = [], [], []
        for chunk, gate_lin, up_lin in zip(grad_chunks, gates, ups):
            d_hidden = product(chunk, down_w)
            _, geglu_back = jax.vjp(geglu, gate_lin, up_lin)
            d_gate, d_up = geglu_back(d_hidden)
            d_gate = d_gate.astype(BF)
            d_up = d_up.astype(BF)
            d_gates.append(d_gate)
            d_ups.append(d_up)
            if len(d_gates) == 3:
                output = to_columns(after(result.astype(BF), d_gate))
            parts.append(right_trans(d_gate, gate_w) + right_trans(d_up, up_w))
        totals = scatter_ring(parts)
        d_normed_two = totals[-1]

        def weight_grad(left, right, factor, i):
            piece = right[:, i * hidden_part : (i + 1) * hidden_part]
            whole = left_trans(left, piece).astype(BF)
            side = left_trans(factor, whole).astype(BF)
            pack = jnp.concatenate(
                [
                    whole.reshape(row_devices, block_d, hidden_part),
                    side.reshape(row_devices, block_r, hidden_part),
                ],
                axis=1,
            )
            return (pack, whole)

        def weight_grads(left, right, factor):
            pairs = [weight_grad(left, right, factor, i) for i in range(nx)]
            return ([pair[0] for pair in pairs], [pair[1] for pair in pairs])

        def share_x(packs):
            return [swap_x(packs[mask], mask) for mask in range(1, nx)]

        def owned(kept, got):
            return exchange(total([kept] + got).astype(BF), "rows")

        def in_place(own):
            block = jnp.concatenate([own[r] for r in range(row_devices)], axis=1)
            return (block[:block_d].astype(F32), block[block_d:].astype(F32))

        def inner(sides, wholes):
            return sum(right_trans(side, whole) for side, whole in zip(sides, wholes))

        normed_all = jnp.concatenate(normed_chunks, axis=0)
        grad_all = after(jnp.concatenate(grad_chunks, axis=0), parts[-1])
        down_packs, down_all = weight_grads(
            grad_all, jnp.concatenate(hiddens, axis=0), full_b_down_t
        )
        down_got = share_x(down_packs)
        d_norm_two, gain_two_part = norm_backward(d_normed_two, middle_low, gain_two, scale_two)
        d_middle = seed_grad + d_norm_two

        grad_one = d_middle.astype(BF)
        near_parts = spread_x(grad_one)
        gates_all = jnp.concatenate(d_gates, axis=0)
        normed_all, near_parts[0] = lax.optimization_barrier((normed_all, near_parts[0]))
        gate_away = [
            weight_grad(normed_all, gates_all, full_a_gu, i) for i in range(1, nx)
        ]
        gate_away, near_parts, down_got, normed_all = lax.optimization_barrier(
            (gate_away, near_parts, down_got, normed_all)
        )
        gate_near = weight_grad(normed_all, gates_all, full_a_gu, 0)
        gate_packs = [pair[0] for pair in [gate_near] + gate_away]
        gate_all = [pair[1] for pair in [gate_near] + gate_away]
        gate_packs[0], normed_all = lax.optimization_barrier((gate_packs[0], normed_all))
        up_packs, up_all = weight_grads(normed_all, jnp.concatenate(d_ups, axis=0), full_a_gu)
        gate_got = share_x(gate_packs)
        down_g = owned(down_packs[0], down_got)
        grad_parts = []
        for near in near_parts:
            grad_parts.extend([near, swap_k(near)])
        grad_one_full = jnp.concatenate(natural(grad_parts, col_place), axis=0)
        d_attended = product(grad_one_full, w_o_t).astype(BF)
        gate_got, down_g, d_attended = lax.optimization_barrier((gate_got, down_g, d_attended))
        gate_g = owned(gate_packs[0], gate_got)
        up_got = share_x([None] + [after(pack, gate_got[0]) for pack in up_packs[1:]])
        d_heads = d_attended.reshape(seqs_here, seq_len, heads_here, head_size)
        d_heads = d_heads.transpose(0, 2, 1, 3)
        q_pieces, kv_pieces = [], []
        for s in range(seqs_here):
            d_query, d_key, d_value = attend_backward(
                queries[s], keys[s], values[s], lens_here[s], forward_parts[s][1], d_heads[s]
            )
            d_query = rotate(d_query * query_scale, cosine_table, -sine_table)
            q_pieces.append(d_query.transpose(1, 0, 2).reshape(seq_len, q_width).astype(BF))
            d_key = rotate(d_key, cosine_table, -sine_table)
            kv_pieces.append(jnp.concatenate([d_key, d_value], axis=1))
        d_q_lin = jnp.concatenate(q_pieces, axis=0)
        kv_blocks = jnp.concatenate(kv_pieces, axis=0).reshape(row_count, nx, nk, kv_width)
        d_kv_lin = scatter_cols(
            kv_blocks.transpose(1, 2, 0, 3), place_x, place_k, lambda block: block
        ).astype(BF)
        up_got, gate_g, d_kv_lin = lax.optimization_barrier((up_got, gate_g, d_kv_lin))
        up_g = owned(up_packs[0], up_got)
        d_qkv = jnp.concatenate([d_q_lin, d_kv_lin], axis=1)
        near_two, sent = scatter_tokens(d_qkv, w_qkv)
        d_normed = finish_tokens(near_two, sent)

        def blocks_of(value):
            return value.reshape(value.shape[0], nx, nk, -1).transpose(1, 2, 0, 3)

        def rank_blocks(value):
            blocks = value.reshape(nx, nk, slice_r, row_devices, block_d)
            blocks = blocks.transpose(0, 1, 3, 2, 4)
            return blocks.reshape(nx, nk, rank, local_features)

        o_rows = after(grad_one_full, d_q_lin)
        o_grad_t = left_trans(o_rows, attn_rows).astype(BF)
        a_o_grad_t = product(full_b_o, o_grad_t).astype(BF)
        shared = jnp.concatenate(
            [
                blocks_of(right_trans(full_a_o_t, o_grad_t)),
                blocks_of(inner(down_sides, down_all)),
                rank_blocks(
                    inner(gate_sides, gate_all) + inner(up_sides, up_all)
                ),
            ],
            axis=2,
        )
        shared = scatter_cols(shared, place_x, place_k, lambda block: block).astype(BF)
        shared = shared.reshape(3, row_devices, block_r, local_features).transpose(1, 0, 2, 3)
        o_parts = scatter_y(
            jnp.concatenate(
                [
                    o_grad_t.reshape(row_devices, block_d, q_width),
                    a_o_grad_t.reshape(row_devices, block_r, q_width),
                    shared.reshape(row_devices, 3 * block_r, local_features),
                ],
                axis=1,
            ),
            place_y,
        )
        qkv_grad = left_trans(after(normed, sent[0]), d_qkv).astype(BF)
        b_qkv_grad = left_trans(full_a_qkv, qkv_grad).astype(BF)
        a_qkv_part = rank_blocks(right_trans(full_b_qkv, qkv_grad))
        a_qkv_part = scatter_cols(a_qkv_part, place_x, place_k, lambda block: block).astype(BF)
        last_parts = scatter_y(
            jnp.concatenate(
                [
                    qkv_grad.reshape(row_devices, -1, kv_width),
                    b_qkv_grad.reshape(row_devices, -1, kv_width),
                    a_qkv_part.reshape(row_devices, -1, kv_width),
                ],
                axis=1,
            ),
            place_y,
        )
        d_norm_one, gain_one_part = norm_backward(d_normed, own_x, gain_one, own_scale)
        grad_low_x = (d_middle + d_norm_one).astype(BF)
        o_parts, up_g, grad_low_x = lax.optimization_barrier((o_parts, up_g, grad_low_x))
        o_parts = scatter_z(o_parts, place_z)
        grad_tokens = to_columns(grad_low_x).astype(F32)
        vectors = jnp.concatenate(
            [
                gain_one_part[None],
                gain_two_part[None],
                jnp.full((1, features), square, F32),
            ],
            axis=0,
        )
        last_parts, grad_low_x = lax.optimization_barrier((last_parts, grad_low_x))
        last_parts = scatter_z(last_parts, place_z)
        down_g, d_down_side = in_place(down_g)
        gate_g, d_gate_side = in_place(gate_g)
        up_g, d_up_side = in_place(up_g)

        def join_ranks(value):
            value = value.reshape(slice_r, block_d).astype(BF)
            return jnp.concatenate(gather_cols(value, col_place), axis=0).T.astype(F32)

        rows_sum = total(o_parts)
        grad_w_o = rows_sum[:block_d].T
        grad_a_o = rows_sum[block_d:block_e].T
        grad_b_o = rows_sum[block_e : block_e + block_r]
        grad_b_down = rows_sum[block_e + block_r : block_e + 2 * block_r]
        a_gu_own = rows_sum[block_e + 2 * block_r :]
        last_sum = total(last_parts)
        wide_q = q_width + kv_width
        first_cut = block_d * wide_q // kv_width
        second_cut = block_e * wide_q // kv_width
        grad_w_qkv = last_sum[:first_cut].reshape(block_d, wide_q)
        grad_b_qkv = last_sum[first_cut:second_cut].reshape(block_r, wide_q)
        a_qkv_own = last_sum[second_cut:]
        grad_a_gu = join_ranks(a_gu_own)
        grad_a_qkv = join_ranks(a_qkv_own)
        grad_w_q = grad_w_qkv[:, :q_width]
        grad_w_kv = grad_w_qkv[:, q_width:]
        grad_b_q = grad_b_qkv[:, :q_width]
        grad_b_kv = grad_b_qkv[:, q_width:]
        sums = sum_all(vectors)
        gains = lax.dynamic_slice_in_dim(sums, col_place * local_features, local_features, 1)
        loss_value = (sums[2, 0] / (2.0 * valid_count)).reshape(1)
        return (
            output,
            loss_value,
            grad_tokens,
            gains[0],
            gains[1],
            grad_w_q,
            grad_w_kv,
            grad_a_qkv,
            grad_b_q,
            grad_b_kv,
            grad_w_o,
            grad_a_o,
            grad_b_o,
            gate_g,
            up_g,
            grad_a_gu,
            d_gate_side,
            d_up_side,
            down_g.T,
            d_down_side.T,
            grad_b_down,
        )

    in_specs = (
        P("rows", "cols"),
        P("cols"),
        P("cols"),
        P("rows", "cols"),
        P("rows", "cols"),
        P("rows", None),
        P("rows", "cols"),
        P("rows", "cols"),
        P("cols", "rows"),
        P("cols", "rows"),
        P("rows", "cols"),
        P("rows", "cols"),
        P("rows", "cols"),
        P("rows", None),
        P("rows", "cols"),
        P("rows", "cols"),
        P("cols", "rows"),
        P("cols", "rows"),
        P("rows", "cols"),
        P(),
        P("rows", "cols"),
        P("rows", "cols"),
    )
    out_specs = (
        P("rows", "cols"),
        P(),
        P("rows", "cols"),
        P("cols"),
        P("cols"),
        P("rows", "cols"),
        P("rows", "cols"),
        P("rows", None),
        P("rows", "cols"),
        P("rows", "cols"),
        P("cols", "rows"),
        P("cols", "rows"),
        P("rows", "cols"),
        P("rows", "cols"),
        P("rows", "cols"),
        P("rows", None),
        P("rows", "cols"),
        P("rows", "cols"),
        P("cols", "rows"),
        P("cols", "rows"),
        P("rows", "cols"),
    )
    return jax.shard_map(shards, mesh=mesh, in_specs=in_specs, out_specs=out_specs, check_vma=False)
```

time: 1580 us -> 1430 us (0.905)
  waiting for transfers between devices: 708 us -> 411 us
  local copies, waits for them, and re-layouts: 196 us -> 259 us
  starting transfers between devices: 120 us -> 170 us
  matrix products: 370 us -> 398 us
    all_to_all x9 -> x8, waiting for transfers between devices: 256 us -> 24.5 us  [exchange(): return lax.all_to_all(value, axis, 0, 0, tiled=True)]
    unnamed x326 -> x479, local copies, waits for them, and re-layouts: 70.7 us -> 138 us
    ppermute x77 -> x128, waiting for transfers between devices: 452 us -> 387 us  [permute(): return lax.ppermute(value, BOTH, pairs)]
    ppermute x77 -> x128, starting transfers between devices: 72.8 us -> 123 us  [permute(): return lax.ppermute(value, BOTH, pairs)]
    dot_general x20 -> x35, matrix products: 141 us -> 180 us  [product(): return jnp.dot(former, latter, preferred_element_type=F32)]
    slice x21 -> x29, local copies, waits for them, and re-layouts: 54.3 us -> 26.4 us  [the longest x16 16.8 us: scatter_ring(): away = swap_k(part[own_rows:].astype(BF))]
    dot_general x21 -> x36, matrix products: 120 us -> 94.3 us  [right_trans(): lax.dot_general(former, latter, (((1,), (1,)), ((), ())), preferred_eleme...]
    dot_general x10 -> x16, matrix products: 86.3 us -> 102 us  [left_trans(): lax.dot_general(former, latter, (((0,), (0,)), ((), ())), preferred_eleme...]
  transfers between devices with their start and end apart: 90 -> 137, of which waited for: 31 -> 46; matrix products, arithmetic and copies ran while one was open for 44% -> 50% of each run, Pallas kernels for 0% -> 0%
where the time goes in v2:
time: 1430 us; the launch traced here: 1420 us
  waiting for transfers between devices  411 us (29%)
  matrix products  398 us (28%)
  local copies, waits for them, and re-layouts  259 us (18%)
  starting transfers between devices  170 us (12%)
  other arithmetic  165 us (12%)
  between operations  20.2 us (1%)
    ppermute x128, waiting for transfers between devices, permute(): return lax.ppermute(value, BOTH, pairs)  387 us
    dot_general x35, matrix products, product(): return jnp.dot(former, latter, preferred_element_type=F32)  180 us
    unnamed x479, local copies, waits for them, and re-layouts  138 us
    ppermute x128, starting transfers between devices, permute(): return lax.ppermute(value, BOTH, pairs)  123 us
    dot_general x16, matrix products, left_trans(): lax.dot_general(former, latter, (((0,), (0,)), ((), ())), preferred_eleme...  102 us
    dot_general x36, matrix products, right_trans(): lax.dot_general(former, latter, (((1,), (1,)), ((), ())), preferred_eleme...  94.3 us
    all_to_all x8, starting transfers between devices, exchange(): return lax.all_to_all(value, axis, 0, 0, tiled=True)  47 us
  transfers between devices with their start and end apart: 137, of which 46 were waited for; matrix products, arithmetic and copies ran while one was open for 50% of the time, Pallas kernels for 0%

profile of v2, /device:TPU:0, one launch (start us, length us, event | category | flops | bytes accessed | tf_op | source)
XLA Modules:
  0.0 1422.2 jit_solution(12319501573793590558)
XLA Ops:
  22.8 6.0 all-to-all-start
  37.4 14.0 collective-permute-done.2
  51.5 7.4 collective-permute-start.3
  62.5 7.4 collective-permute-done.5
  69.8 16.0 %collective-permute-done.3 = bf16[288,896]{1,0:T(8,128)(2,1)} collective-permute-done((bf16[288,896]{1,0:T(8,128)(2,1)}, bf16[288,896]{1,0:T(8,128)(2,1)}, u32[]{:S(2)}, u32[]{:S(2)}) %collective-permute-start.3) | collective-permute-done | bytes 516128 | tf_op jit(solution)/shard_map/ppermute | solution.py:122
  85.8 15.3 %collective-permute-done.1 = bf16[288,896]{1,0:T(8,128)(2,1)} collective-permute-done((bf16[288,896]{1,0:T(8,128)(2,1)}, bf16[288,896]{1,0:T(8,128)(2,1)}, u32[]{:S(2)}, u32[]{:S(2)}) %collective-permute-start.1) | collective-permute-done | bytes 516128 | tf_op jit(solution)/shard_map/ppermute | solution.py:122
  125.7 6.7 all-to-all-start.1
  153.5 6.5 fusion.146
  160.9 6.1 all-to-all-start.2
  171.0 10.2 collective-permute-done.20
  181.6 7.1 collective-permute-start.19
  213.5 20.3 %all-to-all-done.2 = bf16[8,256,512]{1,2,0:T(8,128)(2,1)S(1)} async-done(((bf16[8,256,512]{1,2,0:T(8,128)(2,1)}), bf16[8,256,512]{1,2,0:T(8,128)(2,1)S(1)}, u32[]{:S(2)}, u32[]{:S(2)}) %all-to-all-start.2) | async-done | bytes 2097184 | tf_op jit(solution)/shard_map/all_to_all | solution.py:219
  253.1 5.5 copy.213
  271.3 7.9 all-to-all-start.3
  295.3 40.9 %collective-permute-done.26 = bf16[3,256,512]{2,1,0:T(8,128)(2,1)} collective-permute-done((bf16[3,256,512]{2,1,0:T(8,128)(2,1)S(1)}, bf16[3,256,512]{2,1,0:T(8,128)(2,1)}, u32[]{:S(2)}, u32[]{:S(2)}) %collective-permute-start.26) | collective-permute-done | bytes 786464 | tf_op jit(solution)/shard_map/ppermute | solution.py:122
  347.7 13.2 collective-permute-done.27
  386.6 8.4 collective-permute-done.28
  395.0 5.4 collective-permute-done.29
  414.4 6.4 constant_dynamic-update-slice_fusion.58
  436.4 5.9 constant_dynamic-update-slice_fusion.57
  447.2 5.6 constant_dynamic-update-slice_fusion.56
  463.9 5.7 constant_dynamic-update-slice_fusion.55
  469.6 5.9 constant_dynamic-update-slice_fusion.54
  500.2 5.9 constant_dynamic-update-slice_fusion.53
  515.7 7.0 constant_dynamic-update-slice_fusion.52
  540.1 8.1 constant_dynamic-update-slice_fusion.51
  567.0 10.1 collective-permute-done.48
  599.1 10.4 collective-permute-done.57
  621.5 17.8 %collective-permute-done.58 = bf16[256,2048]{1,0:T(8,128)(2,1)} collective-permute-done((bf16[256,2048]{1,0:T(8,128)(2,1)}, bf16[256,2048]{1,0:T(8,128)(2,1)}, u32[]{:S(2)}, u32[]{:S(2)}) %collective-permute-start.58) | collective-permute-done | bytes 1048608 | tf_op jit(solution)/shard_map/ppermute | solution.py:122
  652.7 16.3 %collective-permute-done.59 = bf16[256,2048]{1,0:T(8,128)(2,1)} collective-permute-done((bf16[256,2048]{1,0:T(8,128)(2,1)}, bf16[256,2048]{1,0:T(8,128)(2,1)}, u32[]{:S(2)}, u32[]{:S(2)}) %collective-permute-start.59) | collective-permute-done | bytes 1048608 | tf_op jit(solution)/shard_map/ppermute | solution.py:122
  677.1 8.2 constant_dynamic-update-slice_fusion.66
  702.5 7.7 constant_dynamic-update-slice_fusion.65
  710.2 7.3 constant_dynamic-update-slice_fusion.64
  751.0 8.6 constant_dynamic-update-slice_fusion.63
  760.3 8.6 constant_dynamic-update-slice_fusion.62
  792.4 8.7 constant_dynamic-update-slice_fusion.61
  801.1 9.0 constant_dynamic-update-slice_fusion.60
  810.1 6.3 fusion.310
  849.9 9.2 constant_dynamic-update-slice_fusion.59
  866.1 13.8 fusion.30
  886.1 13.9 fusion.33
  900.8 9.8 collective-permute-done.90
  910.5 17.8 %collective-permute-done.77 = bf16[256,2048]{1,0:T(8,128)(2,1)S(1)} collective-permute-done((bf16[256,2048]{1,0:T(8,128)(2,1)S(1)}, bf16[256,2048]{1,0:T(8,128)(2,1)S(1)}, u32[]{:S(2)}, u32[]{:S(2)}) %collective-permute-start.77) | collective-permute-done | bytes 1048608 | tf_op jit(solution)/shard_map/ppermute | solution.py:122
  944.0 10.8 collective-permute-done.91
  962.1 13.8 fusion.20
  978.3 8.1 collective-permute-done.93
  986.5 20.9 %collective-permute-done.92 = bf16[256,2048]{1,0:T(8,128)(2,1)} collective-permute-done((bf16[256,2048]{1,0:T(8,128)(2,1)}, bf16[256,2048]{1,0:T(8,128)(2,1)}, u32[]{:S(2)}, u32[]{:S(2)}) %collective-permute-start.92) | collective-permute-done | bytes 1048608 | tf_op jit(solution)/shard_map/ppermute | solution.py:122
  1007.4 11.8 fusion.36
  1030.1 13.7 fusion.39
  1043.8 14.4 %fusion.42 = bf16[2048,512]{1,0:T(8,128)(2,1)S(1)} fusion(bf16[4096,2048]{1,0:T(8,128)(2,1)} %get-tuple-element.150, bf16[4096,1024]{1,0:T(8,128)(2,1)} %get-tuple-element.261), kind=kOutput, calls=%fused_computation.101 | convolution fusion | flops 8590983168 | bytes 23068672 | tf_op jit(solution)/shard_map/dot_general | solution.py:16
  1082.2 6.2 convolution_convert_fusion.4
  1088.4 21.9 %collective-permute-done.94 = bf16[8,288,512]{2,1,0:T(8,128)(2,1)} collective-permute-done((bf16[8,288,512]{2,1,0:T(8,128)(2,1)}, bf16[8,288,512]{2,1,0:T(8,128)(2,1)}, u32[]{:S(2)}, u32[]{:S(2)}) %collective-permute-start.94) | collective-permute-done | bytes 2359328 | tf_op jit(solution)/shard_map/ppermute | solution.py:122
  1112.6 6.8 fusion.184
  1119.4 6.7 multiply_reduce_fusion
  1130.6 6.0 all-to-all-start.6
  1136.6 7.2 multiply_convert_fusion
  1174.0 6.0 copy.258
  1187.5 22.4 %collective-permute-done.99 = bf16[1024,128]{0,1:T(8,128)(2,1)S(1)} collective-permute-done((bf16[1024,128]{0,1:T(8,128)(2,1)S(1)}, bf16[1024,128]{0,1:T(8,128)(2,1)S(1)}, u32[]{:S(2)}, u32[]{:S(2)}) %collective-permute-start.99) | collective-permute-done | bytes 262176 | tf_op jit(solution)/shard_map/ppermute | solution.py:122
  1270.4 5.6 concatenate.264
  1286.9 6.1 collective-permute-done.102
  1336.1 6.3 collective-permute-done.111
  1350.5 10.6 collective-permute-start.116
  1361.0 25.1 %collective-permute-done.123 = bf16[384,512]{1,0:T(8,128)(2,1)S(1)} collective-permute-done((bf16[384,512]{1,0:T(8,128)(2,1)S(1)}, bf16[384,512]{1,0:T(8,128)(2,1)S(1)}, u32[]{:S(2)}, u32[]{:S(2)}) %collective-permute-start.123) | collective-permute-done | bytes 393248 | tf_op jit(solution)/shard_map/ppermute | solution.py:122
  1394.0 8.9 collective-permute-done.117
  (1012 shorter events, 724.7 us)
Async XLA Ops:
  12.2 39.2 %collective-permute-start.2 = (bf16[288,896]{1,0:T(8,128)(2,1)}, bf16[288,896]{1,0:T(8,128)(2,1)}, u32[]{:S(2)}, u32[]{:S(2)}) collective-permute-start(bf16[288,896]{1,0:T(8,128)(2,1)} %maximum_maximum_fusion), channel_id=1, source_target_pairs={{0,16},{1,17},{2,18},{3,19},{4,20},{5,21},{6,22},{7,23},{8,24},{9,... | collective-permute-start | bytes 1548296 | tf_op jit(solution)/shard_map/ppermute | solution.py:122
  14.8 44.0 %collective-permute-start = (bf16[288,896]{1,0:T(8,128)(2,1)}, bf16[288,896]{1,0:T(8,128)(2,1)}, u32[]{:S(2)}, u32[]{:S(2)}) collective-permute-start(bf16[288,896]{1,0:T(8,128)(2,1)} %maximum_maximum_fusion), channel_id=1, source_target_pairs={{0,24},{1,25},{2,26},{3,27},{4,28},{5,29},{6,30},{7,31},{8,16},{9,... | collective-permute-start | bytes 1548296 | tf_op jit(solution)/shard_map/ppermute | solution.py:122
  22.8 96.7 %all-to-all-start = ((bf16[8,256,512]{1,2,0:T(8,128)(2,1)}), bf16[8,256,512]{1,2,0:T(8,128)(2,1)S(1)}, u32[]{:S(2)}, u32[]{:S(2)}) async-start(bf16[8,256,512]{1,2,0:T(8,128)(2,1)} %bitcast.599), calls=%async_computation | async-start | bytes 4194304 | tf_op jit(solution)/shard_map/all_to_all | solution.py:219
  28.8 206.6 %all-gather.3.cloned.1.call-start = ((), (), s32[]{:S(2)}) async-start(), calls=%async_computation.8 | async-start | bytes 3244032 | tf_op jit(solution)/shard_map/all_gather | solution.py:285
  33.1 29.2 %collective-permute-start.6 = (bf16[288,896]{1,0:T(8,128)(2,1)}, bf16[288,896]{1,0:T(8,128)(2,1)}, u32[]{:S(2)}, u32[]{:S(2)}) collective-permute-start(bf16[288,896]{1,0:T(8,128)(2,1)} %maximum_maximum_fusion), channel_id=1, source_target_pairs={{0,4},{1,5},{2,6},{3,7},{4,0},{5,1},{6,2},{7,3},{8,12},{9,13},{10,... | collective-permute-start | bytes 1548296 | tf_op jit(solution)/shard_map/ppermute | solution.py:122
  35.5 34.4 %collective-permute-start.5 = (bf16[288,896]{1,0:T(8,128)(2,1)}, bf16[288,896]{1,0:T(8,128)(2,1)}, u32[]{:S(2)}, u32[]{:S(2)}) collective-permute-start(bf16[288,896]{1,0:T(8,128)(2,1)} %collective-permute-done.4), channel_id=1, source_target_pairs={{0,4},{1,5},{2,6},{3,7},{4,0},{5,1},{6,2},{7,3},{8,12},{9,13},{10,... | collective-permute-start | bytes 1548296 | tf_op jit(solution)/shard_map/ppermute | solution.py:122
  51.5 34.4 %collective-permute-start.3 = (bf16[288,896]{1,0:T(8,128)(2,1)}, bf16[288,896]{1,0:T(8,128)(2,1)}, u32[]{:S(2)}, u32[]{:S(2)}) collective-permute-start(bf16[288,896]{1,0:T(8,128)(2,1)} %collective-permute-done.2), channel_id=1, source_target_pairs={{0,4},{1,5},{2,6},{3,7},{4,0},{5,1},{6,2},{7,3},{8,12},{9,13},{10,... | collective-permute-start | bytes 1548296 | tf_op jit(solution)/shard_map/ppermute | solution.py:122
  58.9 42.2 %collective-permute-start.1 = (bf16[288,896]{1,0:T(8,128)(2,1)}, bf16[288,896]{1,0:T(8,128)(2,1)}, u32[]{:S(2)}, u32[]{:S(2)}) collective-permute-start(bf16[288,896]{1,0:T(8,128)(2,1)} %collective-permute-done), channel_id=1, source_target_pairs={{0,4},{1,5},{2,6},{3,7},{4,0},{5,1},{6,2},{7,3},{8,12},{9,13},{10,... | collective-permute-start | bytes 1548296 | tf_op jit(solution)/shard_map/ppermute | solution.py:122
  59.4 46.5 %collective-permute-start.7 = (bf16[1024,512]{1,0:T(8,128)(2,1)}, bf16[1024,512]{1,0:T(8,128)(2,1)S(1)}, u32[]{:S(2)}, u32[]{:S(2)}) collective-permute-start(bf16[1024,512]{1,0:T(8,128)(2,1)} %param.22), channel_id=1, source_target_pairs={{0,2},{1,3},{2,0},{3,1},{4,6},{5,7},{6,4},{7,5},{8,10},{9,11},{10,... | collective-permute-start | bytes 3145736 | tf_op jit(solution)/shard_map/ppermute | solution.py:122
  62.4 44.9 %collective-permute-start.9 = (bf16[1024,512]{1,0:T(8,128)(2,1)}, bf16[1024,512]{1,0:T(8,128)(2,1)S(1)}, u32[]{:S(2)}, u32[]{:S(2)}) collective-permute-start(bf16[1024,512]{1,0:T(8,128)(2,1)} %param.22), channel_id=1, source_target_pairs={{0,1},{1,0},{2,3},{3,2},{4,5},{5,4},{6,7},{7,6},{8,9},{9,8},{10,11... | collective-permute-start | bytes 3145736 | tf_op jit(solution)/shard_map/ppermute | solution.py:122
  125.7 34.4 %all-to-all-start.1 = ((bf16[8,3,32,512]{3,2,1,0:T(8,128)(2,1)}), bf16[8,3,32,512]{3,2,1,0:T(8,128)(2,1)S(1)}, u32[]{:S(2)}, u32[]{:S(2)}) async-start(bf16[8,3,32,512]{3,2,1,0:T(8,128)(2,1)} %copy.203), calls=%async_computation.1 | async-start | bytes 1572864 | tf_op jit(solution)/shard_map/all_to_all | solution.py:219
  148.9 39.8 %collective-permute-start.15 = (f32[1024,128]{0,1:T(8,128)}, f32[1024,128]{0,1:T(8,128)}, u32[]{:S(2)}, u32[]{:S(2)}) collective-permute-start(f32[1024,128]{0,1:T(8,128)} %fusion.203), channel_id=1, source_target_pairs={{0,1},{1,0},{2,3},{3,2},{4,5},{5,4},{6,7},{7,6},{8,9},{9,8},{10,11... | collective-permute-start | bytes 1572872 | tf_op jit(solution)/shard_map/ppermute | solution.py:122
  151.1 30.1 %collective-permute-start.20 = (bf16[288,512]{0,1:T(8,128)(2,1)}, bf16[288,512]{0,1:T(8,128)(2,1)}, u32[]{:S(2)}, u32[]{:S(2)}) collective-permute-start(bf16[288,512]{0,1:T(8,128)(2,1)} %pad_maximum_fusion.19), channel_id=1, source_target_pairs={{0,16},{1,17},{2,18},{3,19},{4,20},{5,21},{6,22},{7,23},{8,24},{9,... | collective-permute-start | bytes 884744 | tf_op jit(solution)/shard_map/ppermute | solution.py:122
  153.5 35.2 %collective-permute-start.14 = (f32[1024,128]{0,1:T(8,128)}, f32[1024,128]{0,1:T(8,128)}, u32[]{:S(2)}, u32[]{:S(2)}) collective-permute-start(f32[1024,128]{0,1:T(8,128)} %collective-permute-done.13), channel_id=1, source_target_pairs={{0,1},{1,0},{2,3},{3,2},{4,5},{5,4},{6,7},{7,6},{8,9},{9,8},{10,11... | collective-permute-start | bytes 1572872 | tf_op jit(solution)/shard_map/ppermute | solution.py:122
  160.9 72.8 %all-to-all-start.2 = ((bf16[8,256,512]{1,2,0:T(8,128)(2,1)}), bf16[8,256,512]{1,2,0:T(8,128)(2,1)S(1)}, u32[]{:S(2)}, u32[]{:S(2)}) async-start(bf16[8,256,512]{1,2,0:T(8,128)(2,1)} %bitcast.5), calls=%async_computation.2 | async-start | bytes 4194304 | tf_op jit(solution)/shard_map/all_to_all | solution.py:219
  169.6 65.7 %collective-permute-start.17 = (bf16[288,512]{0,1:T(8,128)(2,1)}, bf16[288,512]{0,1:T(8,128)(2,1)}, u32[]{:S(2)}, u32[]{:S(2)}) collective-permute-start(bf16[288,512]{0,1:T(8,128)(2,1)} %pad_maximum_fusion.19), channel_id=1, source_target_pairs={{0,4},{1,5},{2,6},{3,7},{4,0},{5,1},{6,2},{7,3},{8,12},{9,13},{10,... | collective-permute-start | bytes 884744 | tf_op jit(solution)/shard_map/ppermute | solution.py:122
  181.2 54.1 %collective-permute-start.16 = (bf16[2048,512]{0,1:T(8,128)(2,1)}, bf16[2048,512]{0,1:T(8,128)(2,1)}, u32[]{:S(2)}, u32[]{:S(2)}) collective-permute-start(bf16[2048,512]{0,1:T(8,128)(2,1)} %bitcast.613), channel_id=1, source_target_pairs={{0,2},{1,3},{2,0},{3,1},{4,6},{5,7},{6,4},{7,5},{8,10},{9,11},{10,... | collective-permute-start | bytes 6291464 | tf_op jit(solution)/shard_map/ppermute | solution.py:122
  181.6 53.8 %collective-permute-start.19 = (bf16[288,512]{0,1:T(8,128)(2,1)}, bf16[288,512]{0,1:T(8,128)(2,1)}, u32[]{:S(2)}, u32[]{:S(2)}) collective-permute-start(bf16[288,512]{0,1:T(8,128)(2,1)} %collective-permute-done.18), channel_id=1, source_target_pairs={{0,4},{1,5},{2,6},{3,7},{4,0},{5,1},{6,2},{7,3},{8,12},{9,13},{10,... | collective-permute-start | bytes 884744 | tf_op jit(solution)/shard_map/ppermute | solution.py:122
  188.7 46.7 %collective-permute-start.21 = (bf16[288,512]{0,1:T(8,128)(2,1)}, bf16[288,512]{0,1:T(8,128)(2,1)}, u32[]{:S(2)}, u32[]{:S(2)}) collective-permute-start(bf16[288,512]{0,1:T(8,128)(2,1)} %collective-permute-done.20), channel_id=1, source_target_pairs={{0,4},{1,5},{2,6},{3,7},{4,0},{5,1},{6,2},{7,3},{8,12},{9,13},{10,... | collective-permute-start | bytes 884744 | tf_op jit(solution)/shard_map/ppermute | solution.py:122
  188.8 46.6 %collective-permute-start.23 = (bf16[288,512]{0,1:T(8,128)(2,1)}, bf16[288,512]{0,1:T(8,128)(2,1)}, u32[]{:S(2)}, u32[]{:S(2)}) collective-permute-start(bf16[288,512]{0,1:T(8,128)(2,1)} %collective-permute-done.22), channel_id=1, source_target_pairs={{0,4},{1,5},{2,6},{3,7},{4,0},{5,1},{6,2},{7,3},{8,12},{9,13},{10,... | collective-permute-start | bytes 884744 | tf_op jit(solution)/shard_map/ppermute | solution.py:122
  271.0 65.2 %collective-permute-start.25 = (bf16[2048,512]{0,1:T(8,128)(2,1)}, bf16[2048,512]{0,1:T(8,128)(2,1)}, u32[]{:S(2)}, u32[]{:S(2)}) collective-permute-start(bf16[2048,512]{0,1:T(8,128)(2,1)} %bitcast.222), channel_id=1, source_target_pairs={{0,2},{1,3},{2,0},{3,1},{4,6},{5,7},{6,4},{7,5},{8,10},{9,11},{10,... | collective-permute-start | bytes 6291464 | tf_op jit(solution)/shard_map/ppermute | solution.py:122
  271.3 91.3 %all-to-all-start.3 = ((bf16[8,256,512]{1,2,0:T(8,128)(2,1)}), bf16[8,256,512]{1,2,0:T(8,128)(2,1)}, u32[]{:S(2)}, u32[]{:S(2)}) async-start(bf16[8,256,512]{1,2,0:T(8,128)(2,1)} %bitcast.2), calls=%async_computation.3 | async-start | bytes 4194304 | tf_op jit(solution)/shard_map/all_to_all | solution.py:219
  279.3 56.9 %collective-permute-start.26 = (bf16[3,256,512]{2,1,0:T(8,128)(2,1)S(1)}, bf16[3,256,512]{2,1,0:T(8,128)(2,1)}, u32[]{:S(2)}, u32[]{:S(2)}) collective-permute-start(bf16[3,256,512]{2,1,0:T(8,128)(2,1)S(1)} %bitcast.615), channel_id=1, source_target_pairs={{0,2},{1,3},{2,0},{3,1},{4,6},{5,7},{6,4},{7,5},{8,10},{9,11},{10,... | collective-permute-start | bytes 2359304 | tf_op jit(solution)/shard_map/ppermute | solution.py:122
  369.1 34.3 %collective-permute-start.39 = (bf16[256,2048]{1,0:T(8,128)(2,1)}, bf16[256,2048]{1,0:T(8,128)(2,1)}, u32[]{:S(2)}, u32[]{:S(2)}) collective-permute-start(bf16[256,2048]{1,0:T(8,128)(2,1)} %get-tuple-element.315), channel_id=1, source_target_pairs={{0,1},{1,0},{2,3},{3,2},{4,5},{5,4},{6,7},{7,6},{8,9},{9,8},{10,11... | collective-permute-start | bytes 3145736 | tf_op jit(solution)/shard_map/ppermute | solution.py:122
  370.6 29.9 %collective-permute-start.29 = (bf16[256,2048]{1,0:T(8,128)(2,1)}, bf16[256,2048]{1,0:T(8,128)(2,1)}, u32[]{:S(2)}, u32[]{:S(2)}) collective-permute-start(bf16[256,2048]{1,0:T(8,128)(2,1)} %get-tuple-element.315), channel_id=1, source_target_pairs={{0,8},{1,25},{2,10},{3,27},{4,12},{5,29},{6,14},{7,31},{8,16},{9,1... | collective-permute-start | bytes 3145736 | tf_op jit(solution)/shard_map/ppermute | solution.py:122
  381.5 96.7 %collective-permute-start.31 = (bf16[2048,512]{0,1:T(8,128)(2,1)}, bf16[2048,512]{0,1:T(8,128)(2,1)}, u32[]{:S(2)}, u32[]{:S(2)}) collective-permute-start(bf16[2048,512]{0,1:T(8,128)(2,1)} %bitcast.224), channel_id=1, source_target_pairs={{0,2},{1,3},{2,0},{3,1},{4,6},{5,7},{6,4},{7,5},{8,10},{9,11},{10,... | collective-permute-start | bytes 6291464 | tf_op jit(solution)/shard_map/ppermute | solution.py:122
  381.8 206.3 %all-to-all-start.4 = ((bf16[4,2,256,512]{3,2,1,0:T(8,128)(2,1)}), bf16[4,2,256,512]{3,2,1,0:T(8,128)(2,1)S(1)}, u32[]{:S(2)}, u32[]{:S(2)}) async-start(bf16[4,2,256,512]{3,2,1,0:T(8,128)(2,1)} %maximum_bitcast_fusion), calls=%async_computation.4 | async-start | bytes 4194304 | tf_op jit(solution)/shard_map/all_to_all | solution.py:219
  402.2 40.2 %collective-permute-start.54 = (bf16[256,2048]{1,0:T(8,128)(2,1)}, bf16[256,2048]{1,0:T(8,128)(2,1)S(1)}, u32[]{:S(2)}, u32[]{:S(2)}) collective-permute-start(bf16[256,2048]{1,0:T(8,128)(2,1)} %collective-permute-done.29), channel_id=1, source_target_pairs={{0,1},{1,0},{2,3},{3,2},{4,5},{5,4},{6,7},{7,6},{8,9},{9,8},{10,11... | collective-permute-start | bytes 3145736 | tf_op jit(solution)/shard_map/ppermute | solution.py:122
  428.2 31.7 %collective-permute-start.49 = (bf16[256,2048]{1,0:T(8,128)(2,1)S(1)}, bf16[256,2048]{1,0:T(8,128)(2,1)S(1)}, u32[]{:S(2)}, u32[]{:S(2)}) collective-permute-start(bf16[256,2048]{1,0:T(8,128)(2,1)S(1)} %collective-permute-done.33), channel_id=1, source_target_pairs={{0,1},{1,0},{2,3},{3,2},{4,5},{5,4},{6,7},{7,6},{8,9},{9,8},{10,11... | collective-permute-start | bytes 3145736 | tf_op jit(solution)/shard_map/ppermute | solution.py:122
  453.5 62.0 %collective-permute-start.41 = (bf16[256,2048]{1,0:T(8,128)(2,1)}, bf16[256,2048]{1,0:T(8,128)(2,1)}, u32[]{:S(2)}, u32[]{:S(2)}) collective-permute-start(bf16[256,2048]{1,0:T(8,128)(2,1)} %collective-permute-done.35), channel_id=1, source_target_pairs={{0,4},{1,5},{2,6},{3,7},{4,0},{5,1},{6,2},{7,3},{8,12},{9,13},{10,... | collective-permute-start | bytes 3145736 | tf_op jit(solution)/shard_map/ppermute | solution.py:122
  494.8 56.1 %collective-permute-start.55 = (bf16[256,2048]{1,0:T(8,128)(2,1)}, bf16[256,2048]{1,0:T(8,128)(2,1)S(1)}, u32[]{:S(2)}, u32[]{:S(2)}) collective-permute-start(bf16[256,2048]{1,0:T(8,128)(2,1)} %slice.854), channel_id=1, source_target_pairs={{0,1},{1,0},{2,3},{3,2},{4,5},{5,4},{6,7},{7,6},{8,9},{9,8},{10,11... | collective-permute-start | bytes 3145736 | tf_op jit(solution)/shard_map/ppermute | solution.py:122
  500.0 65.7 %collective-permute-start.50 = (bf16[256,2048]{1,0:T(8,128)(2,1)}, bf16[256,2048]{1,0:T(8,128)(2,1)}, u32[]{:S(2)}, u32[]{:S(2)}) collective-permute-start(bf16[256,2048]{1,0:T(8,128)(2,1)} %slice.856), channel_id=1, source_target_pairs={{0,1},{1,0},{2,3},{3,2},{4,5},{5,4},{6,7},{7,6},{8,9},{9,8},{10,11... | collective-permute-start | bytes 3145736 | tf_op jit(solution)/shard_map/ppermute | solution.py:122
  531.5 45.6 %collective-permute-start.48 = (bf16[256,2048]{1,0:T(8,128)(2,1)}, bf16[256,2048]{1,0:T(8,128)(2,1)S(1)}, u32[]{:S(2)}, u32[]{:S(2)}) collective-permute-start(bf16[256,2048]{1,0:T(8,128)(2,1)} %fusion.140), channel_id=1, source_target_pairs={{0,4},{1,5},{2,6},{3,7},{4,0},{5,1},{6,2},{7,3},{8,12},{9,13},{10,... | collective-permute-start | bytes 3145736 | tf_op jit(solution)/shard_map/ppermute | solution.py:122
  558.7 37.4 %collective-permute-start.45 = (bf16[256,2048]{1,0:T(8,128)(2,1)}, bf16[256,2048]{1,0:T(8,128)(2,1)}, u32[]{:S(2)}, u32[]{:S(2)}) collective-permute-start(bf16[256,2048]{1,0:T(8,128)(2,1)} %slice.858), channel_id=1, source_target_pairs={{0,1},{1,0},{2,3},{3,2},{4,5},{5,4},{6,7},{7,6},{8,9},{9,8},{10,11... | collective-permute-start | bytes 3145736 | tf_op jit(solution)/shard_map/ppermute | solution.py:122
  565.7 33.4 %collective-permute-start.44 = (bf16[256,2048]{1,0:T(8,128)(2,1)}, bf16[256,2048]{1,0:T(8,128)(2,1)}, u32[]{:S(2)}, u32[]{:S(2)}) collective-permute-start(bf16[256,2048]{1,0:T(8,128)(2,1)} %fusion.144), channel_id=1, source_target_pairs={{0,4},{1,5},{2,6},{3,7},{4,0},{5,1},{6,2},{7,3},{8,12},{9,13},{10,... | collective-permute-start | bytes 3145736 | tf_op jit(solution)/shard_map/ppermute | solution.py:122
  590.8 29.7 %collective-permute-start.40 = (bf16[256,2048]{1,0:T(8,128)(2,1)}, bf16[256,2048]{1,0:T(8,128)(2,1)S(1)}, u32[]{:S(2)}, u32[]{:S(2)}) collective-permute-start(bf16[256,2048]{1,0:T(8,128)(2,1)} %slice.860), channel_id=1, source_target_pairs={{0,1},{1,0},{2,3},{3,2},{4,5},{5,4},{6,7},{7,6},{8,9},{9,8},{10,11... | collective-permute-start | bytes 3145736 | tf_op jit(solution)/shard_map/ppermute | solution.py:122
  647.0 30.1 %collective-permute-start.68 = (bf16[256,2048]{1,0:T(8,128)(2,1)}, bf16[256,2048]{1,0:T(8,128)(2,1)}, u32[]{:S(2)}, u32[]{:S(2)}) collective-permute-start(bf16[256,2048]{1,0:T(8,128)(2,1)} %get-tuple-element.294), channel_id=1, source_target_pairs={{0,1},{1,0},{2,3},{3,2},{4,5},{5,4},{6,7},{7,6},{8,9},{9,8},{10,11... | collective-permute-start | bytes 3145736 | tf_op jit(solution)/shard_map/ppermute | solution.py:122
  672.1 38.0 %collective-permute-start.61 = (bf16[256,2048]{1,0:T(8,128)(2,1)}, bf16[256,2048]{1,0:T(8,128)(2,1)S(1)}, u32[]{:S(2)}, u32[]{:S(2)}) collective-permute-start(bf16[256,2048]{1,0:T(8,128)(2,1)} %collective-permute-done.60), channel_id=1, source_target_pairs={{0,1},{1,0},{2,3},{3,2},{4,5},{5,4},{6,7},{7,6},{8,9},{9,8},{10,11... | collective-permute-start | bytes 3145736 | tf_op jit(solution)/shard_map/ppermute | solution.py:122
  701.0 48.4 %collective-permute-start.72 = (bf16[256,2048]{1,0:T(8,128)(2,1)}, bf16[256,2048]{1,0:T(8,128)(2,1)}, u32[]{:S(2)}, u32[]{:S(2)}) collective-permute-start(bf16[256,2048]{1,0:T(8,128)(2,1)} %collective-permute-done.71), channel_id=1, source_target_pairs={{0,4},{1,5},{2,6},{3,7},{4,0},{5,1},{6,2},{7,3},{8,12},{9,13},{10,... | collective-permute-start | bytes 3145736 | tf_op jit(solution)/shard_map/ppermute | solution.py:122
  702.2 47.3 %collective-permute-start.73 = (bf16[256,2048]{1,0:T(8,128)(2,1)}, bf16[256,2048]{1,0:T(8,128)(2,1)}, u32[]{:S(2)}, u32[]{:S(2)}) collective-permute-start(bf16[256,2048]{1,0:T(8,128)(2,1)} %collective-permute-done.71), channel_id=1, source_target_pairs={{0,8},{1,25},{2,10},{3,27},{4,12},{5,29},{6,14},{7,31},{8,16},{9,1... | collective-permute-start | bytes 3145736 | tf_op jit(solution)/shard_map/ppermute | solution.py:122
  747.7 196.3 %collective-permute-start.69 = (bf16[256,2048]{1,0:T(8,128)(2,1)}, bf16[256,2048]{1,0:T(8,128)(2,1)}, u32[]{:S(2)}, u32[]{:S(2)}) collective-permute-start(bf16[256,2048]{1,0:T(8,128)(2,1)} %slice.852), channel_id=1, source_target_pairs={{0,1},{1,0},{2,3},{3,2},{4,5},{5,4},{6,7},{7,6},{8,9},{9,8},{10,11... | collective-permute-start | bytes 3145736 | tf_op jit(solution)/shard_map/ppermute | solution.py:122
  749.4 91.0 %collective-permute-start.88 = (bf16[256,2048]{1,0:T(8,128)(2,1)}, bf16[256,2048]{1,0:T(8,128)(2,1)S(1)}, u32[]{:S(2)}, u32[]{:S(2)}) collective-permute-start(bf16[256,2048]{1,0:T(8,128)(2,1)} %slice.846), channel_id=1, source_target_pairs={{0,1},{1,0},{2,3},{3,2},{4,5},{5,4},{6,7},{7,6},{8,9},{9,8},{10,11... | collective-permute-start | bytes 3145736 | tf_op jit(solution)/shard_map/ppermute | solution.py:122
  749.5 31.2 %collective-permute-start.66 = (bf16[256,2048]{1,0:T(8,128)(2,1)}, bf16[256,2048]{1,0:T(8,128)(2,1)}, u32[]{:S(2)}, u32[]{:S(2)}) collective-permute-start(bf16[256,2048]{1,0:T(8,128)(2,1)} %slice.853), channel_id=1, source_target_pairs={{0,1},{1,0},{2,3},{3,2},{4,5},{5,4},{6,7},{7,6},{8,9},{9,8},{10,11... | collective-permute-start | bytes 3145736 | tf_op jit(solution)/shard_map/ppermute | solution.py:122
  750.9 50.2 %collective-permute-start.78 = (bf16[256,2048]{1,0:T(8,128)(2,1)}, bf16[256,2048]{1,0:T(8,128)(2,1)}, u32[]{:S(2)}, u32[]{:S(2)}) collective-permute-start(bf16[256,2048]{1,0:T(8,128)(2,1)} %collective-permute-done.73), channel_id=1, source_target_pairs={{0,1},{1,0},{2,3},{3,2},{4,5},{5,4},{6,7},{7,6},{8,9},{9,8},{10,11... | collective-permute-start | bytes 3145736 | tf_op jit(solution)/shard_map/ppermute | solution.py:122
  759.6 78.6 %collective-permute-start.74 = (bf16[256,2048]{1,0:T(8,128)(2,1)}, bf16[256,2048]{1,0:T(8,128)(2,1)}, u32[]{:S(2)}, u32[]{:S(2)}) collective-permute-start(bf16[256,2048]{1,0:T(8,128)(2,1)} %collective-permute-done.73), channel_id=1, source_target_pairs={{0,4},{1,5},{2,6},{3,7},{4,0},{5,1},{6,2},{7,3},{8,12},{9,13},{10,... | collective-permute-start | bytes 3145736 | tf_op jit(solution)/shard_map/ppermute | solution.py:122
  838.1 41.7 %collective-permute-start.84 = (bf16[256,2048]{1,0:T(8,128)(2,1)}, bf16[256,2048]{1,0:T(8,128)(2,1)}, u32[]{:S(2)}, u32[]{:S(2)}) collective-permute-start(bf16[256,2048]{1,0:T(8,128)(2,1)} %slice.848), channel_id=1, source_target_pairs={{0,1},{1,0},{2,3},{3,2},{4,5},{5,4},{6,7},{7,6},{8,9},{9,8},{10,11... | collective-permute-start | bytes 3145736 | tf_op jit(solution)/shard_map/ppermute | solution.py:122
  844.9 35.7 %collective-permute-start.89 = (bf16[256,2048]{1,0:T(8,128)(2,1)}, bf16[256,2048]{1,0:T(8,128)(2,1)S(1)}, u32[]{:S(2)}, u32[]{:S(2)}) collective-permute-start(bf16[256,2048]{1,0:T(8,128)(2,1)} %fusion.121), channel_id=1, source_target_pairs={{0,8},{1,25},{2,10},{3,27},{4,12},{5,29},{6,14},{7,31},{8,16},{9,1... | collective-permute-start | bytes 3145736 | tf_op jit(solution)/shard_map/ppermute | solution.py:122
  847.5 33.7 %collective-permute-start.82 = (bf16[256,2048]{1,0:T(8,128)(2,1)}, bf16[256,2048]{1,0:T(8,128)(2,1)}, u32[]{:S(2)}, u32[]{:S(2)}) collective-permute-start(bf16[256,2048]{1,0:T(8,128)(2,1)} %fusion.126), channel_id=1, source_target_pairs={{0,4},{1,5},{2,6},{3,7},{4,0},{5,1},{6,2},{7,3},{8,12},{9,13},{10,... | collective-permute-start | bytes 3145736 | tf_op jit(solution)/shard_map/ppermute | solution.py:122
  879.9 64.1 %collective-permute-start.67 = (bf16[256,2048]{1,0:T(8,128)(2,1)}, bf16[256,2048]{1,0:T(8,128)(2,1)}, u32[]{:S(2)}, u32[]{:S(2)}) collective-permute-start(bf16[256,2048]{1,0:T(8,128)(2,1)} %fusion.133), channel_id=1, source_target_pairs={{0,4},{1,5},{2,6},{3,7},{4,0},{5,1},{6,2},{7,3},{8,12},{9,13},{10,... | collective-permute-start | bytes 3145736 | tf_op jit(solution)/shard_map/ppermute | solution.py:122
  885.1 43.3 %collective-permute-start.77 = (bf16[256,2048]{1,0:T(8,128)(2,1)S(1)}, bf16[256,2048]{1,0:T(8,128)(2,1)S(1)}, u32[]{:S(2)}, u32[]{:S(2)}) collective-permute-start(bf16[256,2048]{1,0:T(8,128)(2,1)S(1)} %fusion.130), channel_id=1, source_target_pairs={{0,4},{1,5},{2,6},{3,7},{4,0},{5,1},{6,2},{7,3},{8,12},{9,13},{10,... | collective-permute-start | bytes 3145736 | tf_op jit(solution)/shard_map/ppermute | solution.py:122
  932.0 54.4 %collective-permute-start.93 = (bf16[8,288,512]{2,1,0:T(8,128)(2,1)}, bf16[8,288,512]{2,1,0:T(8,128)(2,1)}, u32[]{:S(2)}, u32[]{:S(2)}) collective-permute-start(bf16[8,288,512]{2,1,0:T(8,128)(2,1)} %pad_maximum_fusion.8), channel_id=1, source_target_pairs={{0,2},{1,3},{2,0},{3,1},{4,6},{5,7},{6,4},{7,5},{8,10},{9,11},{10,... | collective-permute-start | bytes 7077896 | tf_op jit(solution)/shard_map/ppermute | solution.py:122
  961.6 45.7 %collective-permute-start.92 = (bf16[256,2048]{1,0:T(8,128)(2,1)}, bf16[256,2048]{1,0:T(8,128)(2,1)}, u32[]{:S(2)}, u32[]{:S(2)}) collective-permute-start(bf16[256,2048]{1,0:T(8,128)(2,1)} %get-tuple-element.147), channel_id=1, source_target_pairs={{0,2},{1,3},{2,0},{3,1},{4,6},{5,7},{6,4},{7,5},{8,10},{9,11},{10,... | collective-permute-start | bytes 3145736 | tf_op jit(solution)/shard_map/ppermute | solution.py:122
  1025.3 85.0 %all-to-all-start.5 = ((bf16[8,288,512]{2,1,0:T(8,128)(2,1)}), bf16[8,288,512]{2,1,0:T(8,128)(2,1)}, u32[]{:S(2)}, u32[]{:S(2)}) async-start(bf16[8,288,512]{2,1,0:T(8,128)(2,1)} %add_convert_fusion.2), calls=%async_computation.5 | async-start | bytes 4718592 | tf_op jit(solution)/shard_map/all_to_all | solution.py:219
  1058.3 52.0 %collective-permute-start.94 = (bf16[8,288,512]{2,1,0:T(8,128)(2,1)}, bf16[8,288,512]{2,1,0:T(8,128)(2,1)}, u32[]{:S(2)}, u32[]{:S(2)}) collective-permute-start(bf16[8,288,512]{2,1,0:T(8,128)(2,1)} %pad_maximum_fusion.7), channel_id=1, source_target_pairs={{0,2},{1,3},{2,0},{3,1},{4,6},{5,7},{6,4},{7,5},{8,10},{9,11},{10,... | collective-permute-start | bytes 7077896 | tf_op jit(solution)/shard_map/ppermute | solution.py:122
  1126.1 88.6 %collective-permute-start.97 = (bf16[8,288,512]{2,1,0:T(8,128)(2,1)}, bf16[8,288,512]{2,1,0:T(8,128)(2,1)}, u32[]{:S(2)}, u32[]{:S(2)}) collective-permute-start(bf16[8,288,512]{2,1,0:T(8,128)(2,1)} %pad_maximum_fusion.10), channel_id=1, source_target_pairs={{0,2},{1,3},{2,0},{3,1},{4,6},{5,7},{6,4},{7,5},{8,10},{9,11},{10,... | collective-permute-start | bytes 7077896 | tf_op jit(solution)/shard_map/ppermute | solution.py:122
  1130.6 84.1 %all-to-all-start.6 = ((bf16[8,288,512]{2,1,0:T(8,128)(2,1)}), bf16[8,288,512]{2,1,0:T(8,128)(2,1)}, u32[]{:S(2)}, u32[]{:S(2)}) async-start(bf16[8,288,512]{2,1,0:T(8,128)(2,1)} %add_convert_fusion.1), calls=%async_computation.6 | async-start | bytes 4718592 | tf_op jit(solution)/shard_map/all_to_all | solution.py:219
  1212.7 100.7 %collective-permute-start.109 = (bf16[4,384,512]{2,1,0:T(8,128)(2,1)}, bf16[4,384,512]{2,1,0:T(8,128)(2,1)}, u32[]{:S(2)}, u32[]{:S(2)}) collective-permute-start(bf16[4,384,512]{2,1,0:T(8,128)(2,1)} %get-tuple-element.377), channel_id=1, source_target_pairs={{0,4},{1,5},{2,6},{3,7},{4,0},{5,1},{6,2},{7,3},{8,12},{9,13},{10,... | collective-permute-start | bytes 4718600 | tf_op jit(solution)/shard_map/ppermute | solution.py:122
  1233.1 80.4 %all-to-all-start.7 = ((bf16[8,288,512]{2,1,0:T(8,128)(2,1)}), bf16[8,288,512]{2,1,0:T(8,128)(2,1)}, u32[]{:S(2)}, u32[]{:S(2)}) async-start(bf16[8,288,512]{2,1,0:T(8,128)(2,1)} %add_convert_fusion), calls=%async_computation.7 | async-start | bytes 4718592 | tf_op jit(solution)/shard_map/all_to_all | solution.py:219
  1307.7 36.5 %collective-permute-start.115 = (bf16[4,1568,128]{2,1,0:T(8,128)(2,1)}, bf16[4,1568,128]{2,1,0:T(8,128)(2,1)}, u32[]{:S(2)}, u32[]{:S(2)}) collective-permute-start(bf16[4,1568,128]{2,1,0:T(8,128)(2,1)} %get-tuple-element.372), channel_id=1, source_target_pairs={{0,4},{1,5},{2,6},{3,7},{4,0},{5,1},{6,2},{7,3},{8,12},{9,13},{10,... | collective-permute-start | bytes 4816904 | tf_op jit(solution)/shard_map/ppermute | solution.py:122
  1336.1 50.1 %collective-permute-start.123 = (bf16[384,512]{1,0:T(8,128)(2,1)S(1)}, bf16[384,512]{1,0:T(8,128)(2,1)S(1)}, u32[]{:S(2)}, u32[]{:S(2)}) collective-permute-start(bf16[384,512]{1,0:T(8,128)(2,1)S(1)} %get-tuple-element.376), channel_id=1, source_target_pairs={{0,16},{1,17},{2,18},{3,19},{4,20},{5,21},{6,22},{7,23},{8,24},{9,... | collective-permute-start | bytes 1179656 | tf_op jit(solution)/shard_map/ppermute | solution.py:122
  1342.3 43.8 %collective-permute-start.122 = (bf16[384,512]{1,0:T(8,128)(2,1)S(1)}, bf16[384,512]{1,0:T(8,128)(2,1)S(1)}, u32[]{:S(2)}, u32[]{:S(2)}) collective-permute-start(bf16[384,512]{1,0:T(8,128)(2,1)S(1)} %get-tuple-element.374), channel_id=1, source_target_pairs={{0,8},{1,9},{2,10},{3,11},{4,12},{5,13},{6,14},{7,15},{8,0},{9,1},... | collective-permute-start | bytes 1179656 | tf_op jit(solution)/shard_map/ppermute | solution.py:122
  1347.0 47.0 %collective-permute-start.118 = (bf16[1568,128]{1,0:T(8,128)(2,1)}, bf16[1568,128]{1,0:T(8,128)(2,1)}, u32[]{:S(2)}, u32[]{:S(2)}) collective-permute-start(bf16[1568,128]{1,0:T(8,128)(2,1)} %get-tuple-element.370), channel_id=1, source_target_pairs={{0,24},{1,25},{2,26},{3,27},{4,28},{5,29},{6,30},{7,31},{8,16},{9,... | collective-permute-start | bytes 1204232 | tf_op jit(solution)/shard_map/ppermute | solution.py:122
  1348.5 54.5 %collective-permute-start.117 = (bf16[1568,128]{1,0:T(8,128)(2,1)}, bf16[1568,128]{1,0:T(8,128)(2,1)}, u32[]{:S(2)}, u32[]{:S(2)}) collective-permute-start(bf16[1568,128]{1,0:T(8,128)(2,1)} %get-tuple-element.371), channel_id=1, source_target_pairs={{0,16},{1,17},{2,18},{3,19},{4,20},{5,21},{6,22},{7,23},{8,24},{9,... | collective-permute-start | bytes 1204232 | tf_op jit(solution)/shard_map/ppermute | solution.py:122
  1350.5 52.5 %collective-permute-start.116 = (bf16[1568,128]{1,0:T(8,128)(2,1)}, bf16[1568,128]{1,0:T(8,128)(2,1)}, u32[]{:S(2)}, u32[]{:S(2)}) collective-permute-start(bf16[1568,128]{1,0:T(8,128)(2,1)} %get-tuple-element.369), channel_id=1, source_target_pairs={{0,8},{1,9},{2,10},{3,11},{4,12},{5,13},{6,14},{7,15},{8,0},{9,1},... | collective-permute-start | bytes 1204232 | tf_op jit(solution)/shard_map/ppermute | solution.py:122
  (277 other events, 3391.0 us)
Sparse Core Ops, SparseCore 0:
  32.4 89.6 all-gather.2

commit v3 on v2

--- a/solution.py
+++ b/solution.py
@@ -342,8 +342,8 @@
             [part[0].transpose(1, 0, 2).reshape(seq_len, q_width) for part in forward_parts],
             axis=0,
         )
-        attn_rows, up_own, gate_parts, wide, *parts_two = lax.optimization_barrier(
-            (attn_rows, up_own, gate_parts, wide, *parts_two)
+        attn_rows, up_own, gate_parts, side_parts, wide, *parts_two = lax.optimization_barrier(
+            (attn_rows, up_own, gate_parts, side_parts, wide, *parts_two)
         )
         up_parts = spread_x(up_own)
         down_blocks, up_own = lax.optimization_barrier((hidden_blocks(w_down.T), up_own))
@@ -380,9 +380,6 @@
             return near + total([swap_x(value, i + 1) for i, value in enumerate(sent)])
 
         near_one, sent_one = scatter_tokens(attn_rows, w_o_t)
-        up_parts, side_parts, sent_one = lax.optimization_barrier(
-            (up_parts, side_parts, sent_one)
-        )
         branch_one = finish_tokens(near_one, sent_one)
         own_x = lax.dynamic_slice_in_dim(full_x, col_place * own_rows, own_rows, 0).astype(F32)
         own_scale = lax.dynamic_slice_in_dim(scale_one, col_place * own_rows, own_rows, 0)
@@ -406,19 +403,25 @@
         middle_low = middle.astype(BF).astype(F32)
         normed_two, scale_two = norm_forward(middle_low, gain_two)
 
-        def gather_ring(value):
+        def gather_ring(value, work):
             chunks = []
             for step in range(nz):
                 lines = [swap_y(value, mask) for mask in range(1, ny)]
                 near = value
                 if step + 1 < nz:
                     value = ring(value)
-                    lines, value = lax.optimization_barrier((lines, value))
-                for line in [near] + lines:
+                    if step:
+                        lines, value = lax.optimization_barrier((lines, value))
+                    else:
+                        chunks.append(jnp.concatenate([near, swap_k(near)], axis=0))
+                        lines, value, done = lax.optimization_barrier(
+                            (lines, value, work(chunks[0]))
+                        )
+                for line in ([near] if step else []) + lines:
                     chunks.append(jnp.concatenate([line, swap_k(line)], axis=0))
-            return chunks
-
-        def scatter_ring(parts):
+            return (chunks, done)
+
+        def scatter_ring(parts, extra=None):
             totals = []
             for step in list(range(1, nz)) + [0]:
                 mine = None
@@ -429,12 +432,15 @@
                     if mask:
                         chip = swap_y(chip.astype(BF), mask).astype(F32)
                     mine = chip if mine is None else mine + chip
+                if step == 0 and extra is not None:
+                    totals[-1], extra = lax.optimization_barrier((totals[-1], extra))
                 if totals:
                     mine = mine + ring(totals[-1]).astype(F32)
                 totals.append(mine.astype(BF) if step else mine)
-            return totals
-
-        normed_chunks = gather_ring(normed_two)
+            return (totals, extra)
+
+        normed_chunks, normed_two = gather_ring(normed_two, lambda chunk: chunk)
+        up_parts, normed_chunks[1] = lax.optimization_barrier((up_parts, normed_chunks[1]))
         gate_w = joined(gate_parts, gate_sides, full_a_gu)
         up_w = joined(up_parts, up_sides, full_a_gu)
         down_parts = spread_x(down_own)
@@ -459,7 +465,7 @@
         pair = pair.transpose(1, 2, 0, 3).reshape(2, own_rows, features)
         teacher_own = pair[0].astype(F32)
         out_grad_own = pair[1].astype(F32)
-        result = middle + scatter_ring(parts)[-1]
+        result = middle + scatter_ring(parts)[0][-1]
 
         spots = col_place * own_rows + jnp.arange(own_rows)
         limits = jnp.take(lens_here, spots // seq_len) if seqs_here > 1 else lens_here[0]
@@ -485,20 +491,20 @@
             return jnp.concatenate(natural(parts, col_place), axis=0)
 
 
-        grad_chunks = gather_ring(grad_two)
+        grad_chunks, first_hidden = gather_ring(
+            grad_two, lambda chunk: product(chunk, down_w)
+        )
         d_gates, d_ups, parts = [], [], []
         for chunk, gate_lin, up_lin in zip(grad_chunks, gates, ups):
-            d_hidden = product(chunk, down_w)
+            d_hidden = product(chunk, down_w) if d_gates else first_hidden
             _, geglu_back = jax.vjp(geglu, gate_lin, up_lin)
             d_gate, d_up = geglu_back(d_hidden)
             d_gate = d_gate.astype(BF)
             d_up = d_up.astype(BF)
             d_gates.append(d_gate)
             d_ups.append(d_up)
-            if len(d_gates) == 3:
-                output = to_columns(after(result.astype(BF), d_gate))
             parts.append(right_trans(d_gate, gate_w) + right_trans(d_up, up_w))
-        totals = scatter_ring(parts)
+        totals, normed_all = scatter_ring(parts, jnp.concatenate(normed_chunks, axis=0))
         d_normed_two = totals[-1]
 
         def weight_grad(left, right, factor, i):
@@ -531,7 +537,6 @@
         def inner(sides, wholes):
             return sum(right_trans(side, whole) for side, whole in zip(sides, wholes))
 
-        normed_all = jnp.concatenate(normed_chunks, axis=0)
         grad_all = after(jnp.concatenate(grad_chunks, axis=0), parts[-1])
         down_packs, down_all = weight_grads(
             grad_all, jnp.concatenate(hiddens, axis=0), full_b_down_t
@@ -543,28 +548,30 @@
         grad_one = d_middle.astype(BF)
         near_parts = spread_x(grad_one)
         gates_all = jnp.concatenate(d_gates, axis=0)
-        normed_all, near_parts[0] = lax.optimization_barrier((normed_all, near_parts[0]))
         gate_away = [
             weight_grad(normed_all, gates_all, full_a_gu, i) for i in range(1, nx)
         ]
         gate_away, near_parts, down_got, normed_all = lax.optimization_barrier(
             (gate_away, near_parts, down_got, normed_all)
         )
+        gate_got = [swap_x(pair[0], i + 1) for i, pair in enumerate(gate_away)]
+        ups_all = jnp.concatenate(d_ups, axis=0)
+        up_away = [weight_grad(normed_all, ups_all, full_a_gu, i) for i in range(1, nx)]
+        up_away, gate_got, normed_all = lax.optimization_barrier((up_away, gate_got, normed_all))
+        up_got = [swap_x(pair[0], i + 1) for i, pair in enumerate(up_away)]
         gate_near = weight_grad(normed_all, gates_all, full_a_gu, 0)
-        gate_packs = [pair[0] for pair in [gate_near] + gate_away]
         gate_all = [pair[1] for pair in [gate_near] + gate_away]
-        gate_packs[0], normed_all = lax.optimization_barrier((gate_packs[0], normed_all))
-        up_packs, up_all = weight_grads(normed_all, jnp.concatenate(d_ups, axis=0), full_a_gu)
-        gate_got = share_x(gate_packs)
+        up_near = weight_grad(normed_all, ups_all, full_a_gu, 0)
+        up_all = [pair[1] for pair in [up_near] + up_away]
         down_g = owned(down_packs[0], down_got)
         grad_parts = []
         for near in near_parts:
             grad_parts.extend([near, swap_k(near)])
         grad_one_full = jnp.concatenate(natural(grad_parts, col_place), axis=0)
         d_attended = product(grad_one_full, w_o_t).astype(BF)
-        gate_got, down_g, d_attended = lax.optimization_barrier((gate_got, down_g, d_attended))
-        gate_g = owned(gate_packs[0], gate_got)
-        up_got = share_x([None] + [after(pack, gate_got[0]) for pack in up_packs[1:]])
+        down_g, d_attended = lax.optimization_barrier((down_g, d_attended))
+        gate_mine, down_g = lax.optimization_barrier((gate_near[0], down_g))
+        gate_g = owned(gate_mine, gate_got)
         d_heads = d_attended.reshape(seqs_here, seq_len, heads_here, head_size)
         d_heads = d_heads.transpose(0, 2, 1, 3)
         q_pieces, kv_pieces = [], []
@@ -577,14 +584,15 @@
             d_key = rotate(d_key, cosine_table, -sine_table)
             kv_pieces.append(jnp.concatenate([d_key, d_value], axis=1))
         d_q_lin = jnp.concatenate(q_pieces, axis=0)
+        up_got, gate_g, d_q_lin = lax.optimization_barrier((up_got, gate_g, d_q_lin))
+        up_g = owned(up_near[0], up_got)
         kv_blocks = jnp.concatenate(kv_pieces, axis=0).reshape(row_count, nx, nk, kv_width)
         d_kv_lin = scatter_cols(
             kv_blocks.transpose(1, 2, 0, 3), place_x, place_k, lambda block: block
         ).astype(BF)
-        up_got, gate_g, d_kv_lin = lax.optimization_barrier((up_got, gate_g, d_kv_lin))
-        up_g = owned(up_packs[0], up_got)
         d_qkv = jnp.concatenate([d_q_lin, d_kv_lin], axis=1)
         near_two, sent = scatter_tokens(d_qkv, w_qkv)
+        up_g, sent = lax.optimization_barrier((up_g, sent))
         d_normed = finish_tokens(near_two, sent)
 
         def blocks_of(value):
@@ -595,7 +603,7 @@
             blocks = blocks.transpose(0, 1, 3, 2, 4)
             return blocks.reshape(nx, nk, rank, local_features)
 
-        o_rows = after(grad_one_full, d_q_lin)
+        o_rows = after(grad_one_full, d_kv_lin)
         o_grad_t = left_trans(o_rows, attn_rows).astype(BF)
         a_o_grad_t = product(full_b_o, o_grad_t).astype(BF)
         shared = jnp.concatenate(
@@ -621,26 +629,31 @@
             ),
             place_y,
         )
-        qkv_grad = left_trans(after(normed, sent[0]), d_qkv).astype(BF)
+        qkv_grad = left_trans(normed, d_qkv).astype(BF)
         b_qkv_grad = left_trans(full_a_qkv, qkv_grad).astype(BF)
         a_qkv_part = rank_blocks(right_trans(full_b_qkv, qkv_grad))
         a_qkv_part = scatter_cols(a_qkv_part, place_x, place_k, lambda block: block).astype(BF)
+        rank_parts = scatter_y(a_qkv_part.reshape(row_devices, block_r, local_features), place_y)
         last_parts = scatter_y(
             jnp.concatenate(
                 [
                     qkv_grad.reshape(row_devices, -1, kv_width),
                     b_qkv_grad.reshape(row_devices, -1, kv_width),
-                    a_qkv_part.reshape(row_devices, -1, kv_width),
-                ],
+                    ],
                 axis=1,
             ),
             place_y,
         )
+        last_parts, d_normed = lax.optimization_barrier((last_parts, d_normed))
+        last_parts = scatter_z(last_parts, place_z)
+        rank_parts = scatter_z(rank_parts, place_z)
         d_norm_one, gain_one_part = norm_backward(d_normed, own_x, gain_one, own_scale)
         grad_low_x = (d_middle + d_norm_one).astype(BF)
-        o_parts, up_g, grad_low_x = lax.optimization_barrier((o_parts, up_g, grad_low_x))
         o_parts = scatter_z(o_parts, place_z)
+        o_parts, grad_low_x = lax.optimization_barrier((o_parts, grad_low_x))
+        result_low, grad_low_x = lax.optimization_barrier((result.astype(BF), grad_low_x))
         grad_tokens = to_columns(grad_low_x).astype(F32)
+        output = to_columns(result_low)
         vectors = jnp.concatenate(
             [
                 gain_one_part[None],
@@ -649,8 +662,8 @@
             ],
             axis=0,
         )
-        last_parts, grad_low_x = lax.optimization_barrier((last_parts, grad_low_x))
-        last_parts = scatter_z(last_parts, place_z)
+        sums = sum_all(vectors)
+        last_parts, rank_parts, sums = lax.optimization_barrier((last_parts, rank_parts, sums))
         down_g, d_down_side = in_place(down_g)
         gate_g, d_gate_side = in_place(gate_g)
         up_g, d_up_side = in_place(up_g)
@@ -668,17 +681,15 @@
         last_sum = total(last_parts)
         wide_q = q_width + kv_width
         first_cut = block_d * wide_q // kv_width
-        second_cut = block_e * wide_q // kv_width
         grad_w_qkv = last_sum[:first_cut].reshape(block_d, wide_q)
-        grad_b_qkv = last_sum[first_cut:second_cut].reshape(block_r, wide_q)
-        a_qkv_own = last_sum[second_cut:]
+        grad_b_qkv = last_sum[first_cut:].reshape(block_r, wide_q)
+        a_qkv_own = total(rank_parts)
         grad_a_gu = join_ranks(a_gu_own)
         grad_a_qkv = join_ranks(a_qkv_own)
         grad_w_q = grad_w_qkv[:, :q_width]
         grad_w_kv = grad_w_qkv[:, q_width:]
         grad_b_q = grad_b_qkv[:, :q_width]
         grad_b_kv = grad_b_qkv[:, q_width:]
-        sums = sum_all(vectors)
         gains = lax.dynamic_slice_in_dim(sums, col_place * local_features, local_features, 1)
         loss_value = (sums[2, 0] / (2.0 * valid_count)).reshape(1)
         return (

time: 1430 us -> 1410 us (0.986)
  matrix products: 398 us -> 381 us
  local copies, waits for them, and re-layouts: 259 us -> 243 us
    ppermute x128 -> x132, waiting for transfers between devices: 387 us -> 378 us  [permute(): return lax.ppermute(value, BOTH, pairs)]
    unnamed x479 -> x453, local copies, waits for them, and re-layouts: 138 us -> 132 us
    ppermute x128 -> x132, starting transfers between devices: 123 us -> 124 us  [permute(): return lax.ppermute(value, BOTH, pairs)]
  transfers between devices with their start and end apart: 137 -> 141, of which waited for: 46 -> 43; matrix products, arithmetic and copies ran while one was open for 50% -> 51% of each run, Pallas kernels for 0% -> 0%
where the time goes in v3:
time: 1410 us; the launch traced here: 1390 us
  waiting for transfers between devices  414 us (29%)
  matrix products  381 us (27%)
  local copies, waits for them, and re-layouts  243 us (17%)
  starting transfers between devices  176 us (12%)
  other arithmetic  160 us (11%)
  between operations  20.4 us (1%)
    ppermute x132, waiting for transfers between devices, permute(): return lax.ppermute(value, BOTH, pairs)  378 us
    dot_general x35, matrix products, product(): return jnp.dot(former, latter, preferred_element_type=F32)  171 us
    unnamed x453, local copies, waits for them, and re-layouts  132 us
    ppermute x132, starting transfers between devices, permute(): return lax.ppermute(value, BOTH, pairs)  124 us
    dot_general x16, matrix products, left_trans(): lax.dot_general(former, latter, (((0,), (0,)), ((), ())), preferred_eleme...  98.3 us
    dot_general x36, matrix products, right_trans(): lax.dot_general(former, latter, (((1,), (1,)), ((), ())), preferred_eleme...  92.9 us
    all_to_all x8, starting transfers between devices, exchange(): return lax.all_to_all(value, axis, 0, 0, tiled=True)  51.5 us
    all_to_all x8, waiting for transfers between devices, exchange(): return lax.all_to_all(value, axis, 0, 0, tiled=True)  36.2 us
  transfers between devices with their start and end apart: 141, of which 43 were waited for; matrix products, arithmetic and copies ran while one was open for 51% of the time, Pallas kernels for 0%

profile of v3, /device:TPU:0, one launch (start us, length us, event | category | flops | bytes accessed | tf_op | source)
XLA Modules:
  0.0 1394.7 jit_solution(8256788863350905255)
XLA Ops:
  22.8 6.0 all-to-all-start
  38.5 12.8 collective-permute-done.2
  51.3 7.4 collective-permute-start.3
  62.4 8.2 collective-permute-done.5
  70.6 17.3 %collective-permute-done.3 = bf16[288,896]{1,0:T(8,128)(2,1)} collective-permute-done((bf16[288,896]{1,0:T(8,128)(2,1)S(1)}, bf16[288,896]{1,0:T(8,128)(2,1)}, u32[]{:S(2)}, u32[]{:S(2)}) %collective-permute-start.3) | collective-permute-done | bytes 516128 | tf_op jit(solution)/shard_map/ppermute | solution.py:122
  87.9 17.7 %collective-permute-done.1 = bf16[288,896]{1,0:T(8,128)(2,1)} collective-permute-done((bf16[288,896]{1,0:T(8,128)(2,1)}, bf16[288,896]{1,0:T(8,128)(2,1)}, u32[]{:S(2)}, u32[]{:S(2)}) %collective-permute-start.1) | collective-permute-done | bytes 516128 | tf_op jit(solution)/shard_map/ppermute | solution.py:122
  152.9 6.6 fusion.145
  159.5 5.9 all-to-all-start.2
  170.4 13.6 collective-permute-done.21
  185.1 6.3 collective-permute-start.20
  218.5 16.9 %all-to-all-done.2 = bf16[8,256,512]{1,2,0:T(8,128)(2,1)} async-done(((bf16[8,256,512]{1,2,0:T(8,128)(2,1)}), bf16[8,256,512]{1,2,0:T(8,128)(2,1)}, u32[]{:S(2)}, u32[]{:S(2)}) %all-to-all-start.2) | async-done | bytes 2097184 | tf_op jit(solution)/shard_map/all_to_all | solution.py:219
  238.7 6.0 collective-permute-done.17
  253.9 5.7 copy.276
  272.3 16.2 %all-to-all-start.3 = ((bf16[8,256,512]{1,2,0:T(8,128)(2,1)}), bf16[8,256,512]{1,2,0:T(8,128)(2,1)}, u32[]{:S(2)}, u32[]{:S(2)}) async-start(bf16[8,256,512]{1,2,0:T(8,128)(2,1)} %bitcast.645), calls=%async_computation.3 | async-start | bytes 4194304 | tf_op jit(solution)/shard_map/all_to_all | solution.py:219
  295.6 23.7 %collective-permute-done.26 = bf16[256,2048]{1,0:T(8,128)(2,1)} collective-permute-done((bf16[256,2048]{1,0:T(8,128)(2,1)S(1)}, bf16[256,2048]{1,0:T(8,128)(2,1)}, u32[]{:S(2)}, u32[]{:S(2)}) %collective-permute-start.26) | collective-permute-done | bytes 1048608 | tf_op jit(solution)/shard_map/ppermute | solution.py:122
  321.9 15.7 %all-to-all-done.3 = bf16[8,256,512]{1,2,0:T(8,128)(2,1)} async-done(((bf16[8,256,512]{1,2,0:T(8,128)(2,1)}), bf16[8,256,512]{1,2,0:T(8,128)(2,1)}, u32[]{:S(2)}, u32[]{:S(2)}) %all-to-all-start.3) | async-done | bytes 2097184 | tf_op jit(solution)/shard_map/all_to_all | solution.py:219
  351.6 16.9 %collective-permute-done.28 = bf16[256,2048]{1,0:T(8,128)(2,1)} collective-permute-done((bf16[256,2048]{1,0:T(8,128)(2,1)}, bf16[256,2048]{1,0:T(8,128)(2,1)}, u32[]{:S(2)}, u32[]{:S(2)}) %collective-permute-start.28) | collective-permute-done | bytes 1048608 | tf_op jit(solution)/shard_map/ppermute | solution.py:122
  410.4 7.0 constant_dynamic-update-slice_fusion.55
  421.3 6.2 constant_dynamic-update-slice_fusion.54
  434.2 5.6 constant_dynamic-update-slice_fusion.53
  450.4 5.7 constant_dynamic-update-slice_fusion.52
  456.1 5.8 constant_dynamic-update-slice_fusion.51
  484.9 6.0 constant_dynamic-update-slice_fusion.50
  499.8 7.0 constant_dynamic-update-slice_fusion.49
  520.4 8.4 constant_dynamic-update-slice_fusion.48
  531.5 5.6 collective-permute-done.53
  550.1 9.5 collective-permute-done.48
  581.3 10.3 collective-permute-done.57
  605.8 16.3 %collective-permute-done.58 = bf16[256,2048]{1,0:T(8,128)(2,1)S(1)} collective-permute-done((bf16[256,2048]{1,0:T(8,128)(2,1)}, bf16[256,2048]{1,0:T(8,128)(2,1)S(1)}, u32[]{:S(2)}, u32[]{:S(2)}) %collective-permute-start.58) | collective-permute-done | bytes 1048608 | tf_op jit(solution)/shard_map/ppermute | solution.py:122
  641.7 13.3 collective-permute-done.59
  675.2 8.0 collective-permute-done.62
  686.1 6.7 constant_dynamic-update-slice_fusion.62
  695.1 6.9 constant_dynamic-update-slice_fusion.61
  719.9 8.5 constant_dynamic-update-slice_fusion.60
  728.8 8.0 constant_dynamic-update-slice_fusion.59
  759.0 8.7 constant_dynamic-update-slice_fusion.58
  767.8 9.0 constant_dynamic-update-slice_fusion.57
  776.8 5.6 fusion.318
  815.4 7.5 constant_dynamic-update-slice_fusion.56
  830.6 13.7 fusion.32
  850.9 13.6 fusion.35
  865.2 10.0 collective-permute-done.83
  875.2 17.1 %collective-permute-done.69 = bf16[256,2048]{1,0:T(8,128)(2,1)S(1)} collective-permute-done((bf16[256,2048]{1,0:T(8,128)(2,1)S(1)}, bf16[256,2048]{1,0:T(8,128)(2,1)S(1)}, u32[]{:S(2)}, u32[]{:S(2)}) %collective-permute-start.69) | collective-permute-done | bytes 1048608 | tf_op jit(solution)/shard_map/ppermute | solution.py:122
  910.1 10.9 collective-permute-done.88
  929.5 12.5 fusion.22
  944.4 6.3 collective-permute-done.90
  950.7 22.5 %collective-permute-done.89 = bf16[256,2048]{1,0:T(8,128)(2,1)} collective-permute-done((bf16[256,2048]{1,0:T(8,128)(2,1)}, bf16[256,2048]{1,0:T(8,128)(2,1)}, u32[]{:S(2)}, u32[]{:S(2)}) %collective-permute-start.89) | collective-permute-done | bytes 1048608 | tf_op jit(solution)/shard_map/ppermute | solution.py:122
  984.0 13.7 fusion.16
  1005.0 6.0 convolution_convert_fusion.4
  1011.1 16.2 %collective-permute-done.95 = bf16[8,288,512]{2,1,0:T(8,128)(2,1)} collective-permute-done((bf16[8,288,512]{2,1,0:T(8,128)(2,1)}, bf16[8,288,512]{2,1,0:T(8,128)(2,1)}, u32[]{:S(2)}, u32[]{:S(2)}) %collective-permute-start.95) | collective-permute-done | bytes 2359328 | tf_op jit(solution)/shard_map/ppermute | solution.py:122
  1027.2 12.4 fusion.38
  1041.4 12.6 fusion.41
  1072.5 5.6 fusion.183
  1106.7 17.6 %collective-permute-done.94 = bf16[1024,128]{0,1:T(8,128)(2,1)S(1)} collective-permute-done((bf16[1024,128]{0,1:T(8,128)(2,1)S(1)}, bf16[1024,128]{0,1:T(8,128)(2,1)S(1)}, u32[]{:S(2)}, u32[]{:S(2)}) %collective-permute-start.94) | collective-permute-done | bytes 262176 | tf_op jit(solution)/shard_map/ppermute | solution.py:122
  1145.5 5.6 copy.324
  1153.8 5.3 collective-permute-done.97
  1164.3 6.3 convolution_convert_fusion
  1231.4 28.4 %collective-permute-done.114 = bf16[4,32,512]{2,1,0:T(8,128)(2,1)S(1)} collective-permute-done((bf16[4,32,512]{2,1,0:T(8,128)(2,1)S(1)}, bf16[4,32,512]{2,1,0:T(8,128)(2,1)S(1)}, u32[]{:S(2)}, u32[]{:S(2)}) %collective-permute-start.114) | collective-permute-done | bytes 131104 | tf_op jit(solution)/shard_map/ppermute | solution.py:122
  1282.6 7.6 collective-permute-done.105
  1323.3 5.8 collective-permute-done.121
  1333.9 5.5 collective-permute-done.106
  1340.2 5.0 collective-permute-done.107
  1355.6 13.5 collective-permute-done.117
  1369.1 5.2 collective-permute-done.110
  (997 shorter events, 716.9 us)
Async XLA Ops:
  12.2 39.1 %collective-permute-start.2 = (bf16[288,896]{1,0:T(8,128)(2,1)}, bf16[288,896]{1,0:T(8,128)(2,1)S(1)}, u32[]{:S(2)}, u32[]{:S(2)}) collective-permute-start(bf16[288,896]{1,0:T(8,128)(2,1)} %maximum_maximum_fusion), channel_id=1, source_target_pairs={{0,16},{1,17},{2,18},{3,19},{4,20},{5,21},{6,22},{7,23},{8,24},{9,... | collective-permute-start | bytes 1548296 | tf_op jit(solution)/shard_map/ppermute | solution.py:122
  14.8 43.9 %collective-permute-start = (bf16[288,896]{1,0:T(8,128)(2,1)}, bf16[288,896]{1,0:T(8,128)(2,1)}, u32[]{:S(2)}, u32[]{:S(2)}) collective-permute-start(bf16[288,896]{1,0:T(8,128)(2,1)} %maximum_maximum_fusion), channel_id=1, source_target_pairs={{0,24},{1,25},{2,26},{3,27},{4,28},{5,29},{6,30},{7,31},{8,16},{9,... | collective-permute-start | bytes 1548296 | tf_op jit(solution)/shard_map/ppermute | solution.py:122
  22.8 96.8 %all-to-all-start = ((bf16[8,256,512]{1,2,0:T(8,128)(2,1)}), bf16[8,256,512]{1,2,0:T(8,128)(2,1)S(1)}, u32[]{:S(2)}, u32[]{:S(2)}) async-start(bf16[8,256,512]{1,2,0:T(8,128)(2,1)} %bitcast.609), calls=%async_computation | async-start | bytes 4194304 | tf_op jit(solution)/shard_map/all_to_all | solution.py:219
  28.7 215.9 %all-gather.3.cloned.1.call-start = ((), (), s32[]{:S(2)}) async-start(), calls=%async_computation.8 | async-start | bytes 3244032 | tf_op jit(solution)/shard_map/all_gather | solution.py:285
  38.3 32.2 %collective-permute-start.5 = (bf16[288,896]{1,0:T(8,128)(2,1)S(1)}, bf16[288,896]{1,0:T(8,128)(2,1)}, u32[]{:S(2)}, u32[]{:S(2)}) collective-permute-start(bf16[288,896]{1,0:T(8,128)(2,1)S(1)} %collective-permute-done.4), channel_id=1, source_target_pairs={{0,4},{1,5},{2,6},{3,7},{4,0},{5,1},{6,2},{7,3},{8,12},{9,13},{10,... | collective-permute-start | bytes 1548296 | tf_op jit(solution)/shard_map/ppermute | solution.py:122
  51.3 36.6 %collective-permute-start.3 = (bf16[288,896]{1,0:T(8,128)(2,1)S(1)}, bf16[288,896]{1,0:T(8,128)(2,1)}, u32[]{:S(2)}, u32[]{:S(2)}) collective-permute-start(bf16[288,896]{1,0:T(8,128)(2,1)S(1)} %collective-permute-done.2), channel_id=1, source_target_pairs={{0,4},{1,5},{2,6},{3,7},{4,0},{5,1},{6,2},{7,3},{8,12},{9,13},{10,... | collective-permute-start | bytes 1548296 | tf_op jit(solution)/shard_map/ppermute | solution.py:122
  58.8 46.9 %collective-permute-start.1 = (bf16[288,896]{1,0:T(8,128)(2,1)}, bf16[288,896]{1,0:T(8,128)(2,1)}, u32[]{:S(2)}, u32[]{:S(2)}) collective-permute-start(bf16[288,896]{1,0:T(8,128)(2,1)} %collective-permute-done), channel_id=1, source_target_pairs={{0,4},{1,5},{2,6},{3,7},{4,0},{5,1},{6,2},{7,3},{8,12},{9,13},{10,... | collective-permute-start | bytes 1548296 | tf_op jit(solution)/shard_map/ppermute | solution.py:122
  59.3 50.9 %collective-permute-start.7 = (bf16[1024,512]{1,0:T(8,128)(2,1)}, bf16[1024,512]{1,0:T(8,128)(2,1)S(1)}, u32[]{:S(2)}, u32[]{:S(2)}) collective-permute-start(bf16[1024,512]{1,0:T(8,128)(2,1)} %param.22), channel_id=1, source_target_pairs={{0,2},{1,3},{2,0},{3,1},{4,6},{5,7},{6,4},{7,5},{8,10},{9,11},{10,... | collective-permute-start | bytes 3145736 | tf_op jit(solution)/shard_map/ppermute | solution.py:122
  62.3 49.2 %collective-permute-start.9 = (bf16[1024,512]{1,0:T(8,128)(2,1)}, bf16[1024,512]{1,0:T(8,128)(2,1)S(1)}, u32[]{:S(2)}, u32[]{:S(2)}) collective-permute-start(bf16[1024,512]{1,0:T(8,128)(2,1)} %param.22), channel_id=1, source_target_pairs={{0,1},{1,0},{2,3},{3,2},{4,5},{5,4},{6,7},{7,6},{8,9},{9,8},{10,11... | collective-permute-start | bytes 3145736 | tf_op jit(solution)/shard_map/ppermute | solution.py:122
  148.3 43.0 %collective-permute-start.15 = (f32[1024,128]{0,1:T(8,128)}, f32[1024,128]{0,1:T(8,128)}, u32[]{:S(2)}, u32[]{:S(2)}) collective-permute-start(f32[1024,128]{0,1:T(8,128)} %fusion.199), channel_id=1, source_target_pairs={{0,1},{1,0},{2,3},{3,2},{4,5},{5,4},{6,7},{7,6},{8,9},{9,8},{10,11... | collective-permute-start | bytes 1572872 | tf_op jit(solution)/shard_map/ppermute | solution.py:122
  150.5 33.5 %collective-permute-start.21 = (bf16[288,512]{0,1:T(8,128)(2,1)}, bf16[288,512]{0,1:T(8,128)(2,1)}, u32[]{:S(2)}, u32[]{:S(2)}) collective-permute-start(bf16[288,512]{0,1:T(8,128)(2,1)} %pad_maximum_fusion.18), channel_id=1, source_target_pairs={{0,16},{1,17},{2,18},{3,19},{4,20},{5,21},{6,22},{7,23},{8,24},{9,... | collective-permute-start | bytes 884744 | tf_op jit(solution)/shard_map/ppermute | solution.py:122
  152.8 32.3 %collective-permute-start.23 = (bf16[288,512]{0,1:T(8,128)(2,1)}, bf16[288,512]{0,1:T(8,128)(2,1)}, u32[]{:S(2)}, u32[]{:S(2)}) collective-permute-start(bf16[288,512]{0,1:T(8,128)(2,1)} %pad_maximum_fusion.18), channel_id=1, source_target_pairs={{0,24},{1,25},{2,26},{3,27},{4,28},{5,29},{6,30},{7,31},{8,16},{9,... | collective-permute-start | bytes 884744 | tf_op jit(solution)/shard_map/ppermute | solution.py:122
  152.9 38.5 %collective-permute-start.14 = (f32[1024,128]{0,1:T(8,128)}, f32[1024,128]{0,1:T(8,128)}, u32[]{:S(2)}, u32[]{:S(2)}) collective-permute-start(f32[1024,128]{0,1:T(8,128)} %collective-permute-done.13), channel_id=1, source_target_pairs={{0,1},{1,0},{2,3},{3,2},{4,5},{5,4},{6,7},{7,6},{8,9},{9,8},{10,11... | collective-permute-start | bytes 1572872 | tf_op jit(solution)/shard_map/ppermute | solution.py:122
  159.5 75.9 %all-to-all-start.2 = ((bf16[8,256,512]{1,2,0:T(8,128)(2,1)}), bf16[8,256,512]{1,2,0:T(8,128)(2,1)}, u32[]{:S(2)}, u32[]{:S(2)}) async-start(bf16[8,256,512]{1,2,0:T(8,128)(2,1)} %bitcast.610), calls=%async_computation.2 | async-start | bytes 4194304 | tf_op jit(solution)/shard_map/all_to_all | solution.py:219
  169.5 43.9 %collective-permute-start.18 = (bf16[288,512]{0,1:T(8,128)(2,1)}, bf16[288,512]{0,1:T(8,128)(2,1)}, u32[]{:S(2)}, u32[]{:S(2)}) collective-permute-start(bf16[288,512]{0,1:T(8,128)(2,1)} %pad_maximum_fusion.18), channel_id=1, source_target_pairs={{0,4},{1,5},{2,6},{3,7},{4,0},{5,1},{6,2},{7,3},{8,12},{9,13},{10,... | collective-permute-start | bytes 884744 | tf_op jit(solution)/shard_map/ppermute | solution.py:122
  184.0 54.7 %collective-permute-start.16 = (bf16[2048,512]{0,1:T(8,128)(2,1)S(1)}, bf16[2048,512]{0,1:T(8,128)(2,1)}, u32[]{:S(2)}, u32[]{:S(2)}) collective-permute-start(bf16[2048,512]{0,1:T(8,128)(2,1)S(1)} %bitcast.604), channel_id=1, source_target_pairs={{0,2},{1,3},{2,0},{3,1},{4,6},{5,7},{6,4},{7,5},{8,10},{9,11},{10,... | collective-permute-start | bytes 6291464 | tf_op jit(solution)/shard_map/ppermute | solution.py:122
  185.1 53.6 %collective-permute-start.20 = (bf16[288,512]{0,1:T(8,128)(2,1)}, bf16[288,512]{0,1:T(8,128)(2,1)}, u32[]{:S(2)}, u32[]{:S(2)}) collective-permute-start(bf16[288,512]{0,1:T(8,128)(2,1)} %collective-permute-done.19), channel_id=1, source_target_pairs={{0,4},{1,5},{2,6},{3,7},{4,0},{5,1},{6,2},{7,3},{8,12},{9,13},{10,... | collective-permute-start | bytes 884744 | tf_op jit(solution)/shard_map/ppermute | solution.py:122
  191.4 47.3 %collective-permute-start.22 = (bf16[288,512]{0,1:T(8,128)(2,1)}, bf16[288,512]{0,1:T(8,128)(2,1)}, u32[]{:S(2)}, u32[]{:S(2)}) collective-permute-start(bf16[288,512]{0,1:T(8,128)(2,1)} %collective-permute-done.21), channel_id=1, source_target_pairs={{0,4},{1,5},{2,6},{3,7},{4,0},{5,1},{6,2},{7,3},{8,12},{9,13},{10,... | collective-permute-start | bytes 884744 | tf_op jit(solution)/shard_map/ppermute | solution.py:122
  191.4 47.2 %collective-permute-start.24 = (bf16[288,512]{0,1:T(8,128)(2,1)}, bf16[288,512]{0,1:T(8,128)(2,1)}, u32[]{:S(2)}, u32[]{:S(2)}) collective-permute-start(bf16[288,512]{0,1:T(8,128)(2,1)} %collective-permute-done.23), channel_id=1, source_target_pairs={{0,4},{1,5},{2,6},{3,7},{4,0},{5,1},{6,2},{7,3},{8,12},{9,13},{10,... | collective-permute-start | bytes 884744 | tf_op jit(solution)/shard_map/ppermute | solution.py:122
  213.4 31.2 %collective-permute-start.17 = (bf16[3,256,512]{2,1,0:T(8,128)(2,1)}, bf16[3,256,512]{2,1,0:T(8,128)(2,1)}, u32[]{:S(2)}, u32[]{:S(2)}) collective-permute-start(bf16[3,256,512]{2,1,0:T(8,128)(2,1)} %bitcast.40), channel_id=1, source_target_pairs={{0,2},{1,3},{2,0},{3,1},{4,6},{5,7},{6,4},{7,5},{8,10},{9,11},{10,... | collective-permute-start | bytes 2359304 | tf_op jit(solution)/shard_map/ppermute | solution.py:122
  272.3 65.3 %all-to-all-start.3 = ((bf16[8,256,512]{1,2,0:T(8,128)(2,1)}), bf16[8,256,512]{1,2,0:T(8,128)(2,1)}, u32[]{:S(2)}, u32[]{:S(2)}) async-start(bf16[8,256,512]{1,2,0:T(8,128)(2,1)} %bitcast.645), calls=%async_computation.3 | async-start | bytes 4194304 | tf_op jit(solution)/shard_map/all_to_all | solution.py:219
  345.2 55.4 %collective-permute-start.27 = (bf16[2048,512]{0,1:T(8,128)(2,1)}, bf16[2048,512]{0,1:T(8,128)(2,1)}, u32[]{:S(2)}, u32[]{:S(2)}) collective-permute-start(bf16[2048,512]{0,1:T(8,128)(2,1)} %bitcast.238), channel_id=1, source_target_pairs={{0,2},{1,3},{2,0},{3,1},{4,6},{5,7},{6,4},{7,5},{8,10},{9,11},{10,... | collective-permute-start | bytes 6291464 | tf_op jit(solution)/shard_map/ppermute | solution.py:122
  346.9 39.6 %collective-permute-start.30 = (bf16[256,2048]{1,0:T(8,128)(2,1)}, bf16[256,2048]{1,0:T(8,128)(2,1)}, u32[]{:S(2)}, u32[]{:S(2)}) collective-permute-start(bf16[256,2048]{1,0:T(8,128)(2,1)} %get-tuple-element.373), channel_id=1, source_target_pairs={{0,1},{1,0},{2,3},{3,2},{4,5},{5,4},{6,7},{7,6},{8,9},{9,8},{10,11... | collective-permute-start | bytes 3145736 | tf_op jit(solution)/shard_map/ppermute | solution.py:122
  381.9 189.8 %all-to-all-start.4 = ((bf16[4,2,256,512]{3,2,1,0:T(8,128)(2,1)}), bf16[4,2,256,512]{3,2,1,0:T(8,128)(2,1)}, u32[]{:S(2)}, u32[]{:S(2)}) async-start(bf16[4,2,256,512]{3,2,1,0:T(8,128)(2,1)} %maximum_bitcast_fusion), calls=%async_computation.4 | async-start | bytes 4194304 | tf_op jit(solution)/shard_map/all_to_all | solution.py:219
  386.6 77.9 %collective-permute-start.32 = (bf16[2048,512]{0,1:T(8,128)(2,1)}, bf16[2048,512]{0,1:T(8,128)(2,1)S(1)}, u32[]{:S(2)}, u32[]{:S(2)}) collective-permute-start(bf16[2048,512]{0,1:T(8,128)(2,1)} %bitcast.606), channel_id=1, source_target_pairs={{0,2},{1,3},{2,0},{3,1},{4,6},{5,7},{6,4},{7,5},{8,10},{9,11},{10,... | collective-permute-start | bytes 6291464 | tf_op jit(solution)/shard_map/ppermute | solution.py:122
  395.6 31.9 %collective-permute-start.54 = (bf16[256,2048]{1,0:T(8,128)(2,1)}, bf16[256,2048]{1,0:T(8,128)(2,1)S(1)}, u32[]{:S(2)}, u32[]{:S(2)}) collective-permute-start(bf16[256,2048]{1,0:T(8,128)(2,1)} %collective-permute-done.29), channel_id=1, source_target_pairs={{0,1},{1,0},{2,3},{3,2},{4,5},{5,4},{6,7},{7,6},{8,9},{9,8},{10,11... | collective-permute-start | bytes 3145736 | tf_op jit(solution)/shard_map/ppermute | solution.py:122
  397.1 42.7 %collective-permute-start.35 = (bf16[256,2048]{1,0:T(8,128)(2,1)}, bf16[256,2048]{1,0:T(8,128)(2,1)S(1)}, u32[]{:S(2)}, u32[]{:S(2)}) collective-permute-start(bf16[256,2048]{1,0:T(8,128)(2,1)} %collective-permute-done.34), channel_id=1, source_target_pairs={{0,4},{1,5},{2,6},{3,7},{4,0},{5,1},{6,2},{7,3},{8,12},{9,13},{10,... | collective-permute-start | bytes 3145736 | tf_op jit(solution)/shard_map/ppermute | solution.py:122
  398.6 41.2 %collective-permute-start.36 = (bf16[256,2048]{1,0:T(8,128)(2,1)}, bf16[256,2048]{1,0:T(8,128)(2,1)}, u32[]{:S(2)}, u32[]{:S(2)}) collective-permute-start(bf16[256,2048]{1,0:T(8,128)(2,1)} %collective-permute-done.34), channel_id=1, source_target_pairs={{0,8},{1,25},{2,10},{3,27},{4,12},{5,29},{6,14},{7,31},{8,16},{9,1... | collective-permute-start | bytes 3145736 | tf_op jit(solution)/shard_map/ppermute | solution.py:122
  400.5 46.1 %collective-permute-start.49 = (bf16[256,2048]{1,0:T(8,128)(2,1)}, bf16[256,2048]{1,0:T(8,128)(2,1)S(1)}, u32[]{:S(2)}, u32[]{:S(2)}) collective-permute-start(bf16[256,2048]{1,0:T(8,128)(2,1)} %collective-permute-done.34), channel_id=1, source_target_pairs={{0,1},{1,0},{2,3},{3,2},{4,5},{5,4},{6,7},{7,6},{8,9},{9,8},{10,11... | collective-permute-start | bytes 3145736 | tf_op jit(solution)/shard_map/ppermute | solution.py:122
  440.4 59.0 %collective-permute-start.41 = (bf16[256,2048]{1,0:T(8,128)(2,1)}, bf16[256,2048]{1,0:T(8,128)(2,1)S(1)}, u32[]{:S(2)}, u32[]{:S(2)}) collective-permute-start(bf16[256,2048]{1,0:T(8,128)(2,1)} %collective-permute-done.36), channel_id=1, source_target_pairs={{0,4},{1,5},{2,6},{3,7},{4,0},{5,1},{6,2},{7,3},{8,12},{9,13},{10,... | collective-permute-start | bytes 3145736 | tf_op jit(solution)/shard_map/ppermute | solution.py:122
  479.3 52.2 %collective-permute-start.55 = (bf16[256,2048]{1,0:T(8,128)(2,1)}, bf16[256,2048]{1,0:T(8,128)(2,1)}, u32[]{:S(2)}, u32[]{:S(2)}) collective-permute-start(bf16[256,2048]{1,0:T(8,128)(2,1)} %slice.848), channel_id=1, source_target_pairs={{0,1},{1,0},{2,3},{3,2},{4,5},{5,4},{6,7},{7,6},{8,9},{9,8},{10,11... | collective-permute-start | bytes 3145736 | tf_op jit(solution)/shard_map/ppermute | solution.py:122
  484.5 64.2 %collective-permute-start.50 = (bf16[256,2048]{1,0:T(8,128)(2,1)}, bf16[256,2048]{1,0:T(8,128)(2,1)}, u32[]{:S(2)}, u32[]{:S(2)}) collective-permute-start(bf16[256,2048]{1,0:T(8,128)(2,1)} %slice.850), channel_id=1, source_target_pairs={{0,1},{1,0},{2,3},{3,2},{4,5},{5,4},{6,7},{7,6},{8,9},{9,8},{10,11... | collective-permute-start | bytes 3145736 | tf_op jit(solution)/shard_map/ppermute | solution.py:122
  515.3 44.2 %collective-permute-start.48 = (bf16[256,2048]{1,0:T(8,128)(2,1)}, bf16[256,2048]{1,0:T(8,128)(2,1)S(1)}, u32[]{:S(2)}, u32[]{:S(2)}) collective-permute-start(bf16[256,2048]{1,0:T(8,128)(2,1)} %fusion.139), channel_id=1, source_target_pairs={{0,4},{1,5},{2,6},{3,7},{4,0},{5,1},{6,2},{7,3},{8,12},{9,13},{10,... | collective-permute-start | bytes 3145736 | tf_op jit(solution)/shard_map/ppermute | solution.py:122
  542.8 37.1 %collective-permute-start.45 = (bf16[256,2048]{1,0:T(8,128)(2,1)}, bf16[256,2048]{1,0:T(8,128)(2,1)}, u32[]{:S(2)}, u32[]{:S(2)}) collective-permute-start(bf16[256,2048]{1,0:T(8,128)(2,1)} %slice.852), channel_id=1, source_target_pairs={{0,1},{1,0},{2,3},{3,2},{4,5},{5,4},{6,7},{7,6},{8,9},{9,8},{10,11... | collective-permute-start | bytes 3145736 | tf_op jit(solution)/shard_map/ppermute | solution.py:122
  548.6 32.7 %collective-permute-start.44 = (bf16[256,2048]{1,0:T(8,128)(2,1)}, bf16[256,2048]{1,0:T(8,128)(2,1)}, u32[]{:S(2)}, u32[]{:S(2)}) collective-permute-start(bf16[256,2048]{1,0:T(8,128)(2,1)} %fusion.143), channel_id=1, source_target_pairs={{0,4},{1,5},{2,6},{3,7},{4,0},{5,1},{6,2},{7,3},{8,12},{9,13},{10,... | collective-permute-start | bytes 3145736 | tf_op jit(solution)/shard_map/ppermute | solution.py:122
  574.4 31.4 %collective-permute-start.40 = (bf16[256,2048]{1,0:T(8,128)(2,1)}, bf16[256,2048]{1,0:T(8,128)(2,1)S(1)}, u32[]{:S(2)}, u32[]{:S(2)}) collective-permute-start(bf16[256,2048]{1,0:T(8,128)(2,1)} %slice.854), channel_id=1, source_target_pairs={{0,1},{1,0},{2,3},{3,2},{4,5},{5,4},{6,7},{7,6},{8,9},{9,8},{10,11... | collective-permute-start | bytes 3145736 | tf_op jit(solution)/shard_map/ppermute | solution.py:122
  657.4 35.4 %collective-permute-start.80 = (bf16[256,2048]{1,0:T(8,128)(2,1)}, bf16[256,2048]{1,0:T(8,128)(2,1)S(1)}, u32[]{:S(2)}, u32[]{:S(2)}) collective-permute-start(bf16[256,2048]{1,0:T(8,128)(2,1)} %collective-permute-done.60), channel_id=1, source_target_pairs={{0,1},{1,0},{2,3},{3,2},{4,5},{5,4},{6,7},{7,6},{8,9},{9,8},{10,11... | collective-permute-start | bytes 3145736 | tf_op jit(solution)/shard_map/ppermute | solution.py:122
  669.1 241.0 %collective-permute-start.87 = (bf16[256,2048]{1,0:T(8,128)(2,1)}, bf16[256,2048]{1,0:T(8,128)(2,1)}, u32[]{:S(2)}, u32[]{:S(2)}) collective-permute-start(bf16[256,2048]{1,0:T(8,128)(2,1)} %slice.840), channel_id=1, source_target_pairs={{0,1},{1,0},{2,3},{3,2},{4,5},{5,4},{6,7},{7,6},{8,9},{9,8},{10,11... | collective-permute-start | bytes 3145736 | tf_op jit(solution)/shard_map/ppermute | solution.py:122
  684.9 43.5 %collective-permute-start.75 = (bf16[256,2048]{1,0:T(8,128)(2,1)S(1)}, bf16[256,2048]{1,0:T(8,128)(2,1)S(1)}, u32[]{:S(2)}, u32[]{:S(2)}) collective-permute-start(bf16[256,2048]{1,0:T(8,128)(2,1)S(1)} %collective-permute-done.63), channel_id=1, source_target_pairs={{0,1},{1,0},{2,3},{3,2},{4,5},{5,4},{6,7},{7,6},{8,9},{9,8},{10,11... | collective-permute-start | bytes 3145736 | tf_op jit(solution)/shard_map/ppermute | solution.py:122
  684.9 34.3 %collective-permute-start.64 = (bf16[256,2048]{1,0:T(8,128)(2,1)S(1)}, bf16[256,2048]{1,0:T(8,128)(2,1)}, u32[]{:S(2)}, u32[]{:S(2)}) collective-permute-start(bf16[256,2048]{1,0:T(8,128)(2,1)S(1)} %collective-permute-done.63), channel_id=1, source_target_pairs={{0,4},{1,5},{2,6},{3,7},{4,0},{5,1},{6,2},{7,3},{8,12},{9,13},{10,... | collective-permute-start | bytes 3145736 | tf_op jit(solution)/shard_map/ppermute | solution.py:122
  685.8 33.5 %collective-permute-start.65 = (bf16[256,2048]{1,0:T(8,128)(2,1)S(1)}, bf16[256,2048]{1,0:T(8,128)(2,1)}, u32[]{:S(2)}, u32[]{:S(2)}) collective-permute-start(bf16[256,2048]{1,0:T(8,128)(2,1)S(1)} %collective-permute-done.63), channel_id=1, source_target_pairs={{0,8},{1,25},{2,10},{3,27},{4,12},{5,29},{6,14},{7,31},{8,16},{9,1... | collective-permute-start | bytes 3145736 | tf_op jit(solution)/shard_map/ppermute | solution.py:122
  719.2 87.5 %collective-permute-start.81 = (bf16[256,2048]{1,0:T(8,128)(2,1)}, bf16[256,2048]{1,0:T(8,128)(2,1)}, u32[]{:S(2)}, u32[]{:S(2)}) collective-permute-start(bf16[256,2048]{1,0:T(8,128)(2,1)} %slice.842), channel_id=1, source_target_pairs={{0,1},{1,0},{2,3},{3,2},{4,5},{5,4},{6,7},{7,6},{8,9},{9,8},{10,11... | collective-permute-start | bytes 3145736 | tf_op jit(solution)/shard_map/ppermute | solution.py:122
  719.8 47.9 %collective-permute-start.70 = (bf16[256,2048]{1,0:T(8,128)(2,1)}, bf16[256,2048]{1,0:T(8,128)(2,1)}, u32[]{:S(2)}, u32[]{:S(2)}) collective-permute-start(bf16[256,2048]{1,0:T(8,128)(2,1)} %collective-permute-done.65), channel_id=1, source_target_pairs={{0,1},{1,0},{2,3},{3,2},{4,5},{5,4},{6,7},{7,6},{8,9},{9,8},{10,11... | collective-permute-start | bytes 3145736 | tf_op jit(solution)/shard_map/ppermute | solution.py:122
  728.4 76.0 %collective-permute-start.66 = (bf16[256,2048]{1,0:T(8,128)(2,1)}, bf16[256,2048]{1,0:T(8,128)(2,1)}, u32[]{:S(2)}, u32[]{:S(2)}) collective-permute-start(bf16[256,2048]{1,0:T(8,128)(2,1)} %collective-permute-done.65), channel_id=1, source_target_pairs={{0,4},{1,5},{2,6},{3,7},{4,0},{5,1},{6,2},{7,3},{8,12},{9,13},{10,... | collective-permute-start | bytes 3145736 | tf_op jit(solution)/shard_map/ppermute | solution.py:122
  804.4 39.9 %collective-permute-start.76 = (bf16[256,2048]{1,0:T(8,128)(2,1)}, bf16[256,2048]{1,0:T(8,128)(2,1)}, u32[]{:S(2)}, u32[]{:S(2)}) collective-permute-start(bf16[256,2048]{1,0:T(8,128)(2,1)} %slice.844), channel_id=1, source_target_pairs={{0,1},{1,0},{2,3},{3,2},{4,5},{5,4},{6,7},{7,6},{8,9},{9,8},{10,11... | collective-permute-start | bytes 3145736 | tf_op jit(solution)/shard_map/ppermute | solution.py:122
  812.0 33.6 %collective-permute-start.82 = (bf16[256,2048]{1,0:T(8,128)(2,1)}, bf16[256,2048]{1,0:T(8,128)(2,1)}, u32[]{:S(2)}, u32[]{:S(2)}) collective-permute-start(bf16[256,2048]{1,0:T(8,128)(2,1)} %fusion.123), channel_id=1, source_target_pairs={{0,8},{1,25},{2,10},{3,27},{4,12},{5,29},{6,14},{7,31},{8,16},{9,1... | collective-permute-start | bytes 3145736 | tf_op jit(solution)/shard_map/ppermute | solution.py:122
  814.3 31.3 %collective-permute-start.74 = (bf16[256,2048]{1,0:T(8,128)(2,1)}, bf16[256,2048]{1,0:T(8,128)(2,1)}, u32[]{:S(2)}, u32[]{:S(2)}) collective-permute-start(bf16[256,2048]{1,0:T(8,128)(2,1)} %fusion.128), channel_id=1, source_target_pairs={{0,4},{1,5},{2,6},{3,7},{4,0},{5,1},{6,2},{7,3},{8,12},{9,13},{10,... | collective-permute-start | bytes 3145736 | tf_op jit(solution)/shard_map/ppermute | solution.py:122
  844.3 65.8 %collective-permute-start.86 = (bf16[256,2048]{1,0:T(8,128)(2,1)}, bf16[256,2048]{1,0:T(8,128)(2,1)}, u32[]{:S(2)}, u32[]{:S(2)}) collective-permute-start(bf16[256,2048]{1,0:T(8,128)(2,1)} %fusion.121), channel_id=1, source_target_pairs={{0,4},{1,5},{2,6},{3,7},{4,0},{5,1},{6,2},{7,3},{8,12},{9,13},{10,... | collective-permute-start | bytes 3145736 | tf_op jit(solution)/shard_map/ppermute | solution.py:122
  849.2 43.1 %collective-permute-start.69 = (bf16[256,2048]{1,0:T(8,128)(2,1)S(1)}, bf16[256,2048]{1,0:T(8,128)(2,1)S(1)}, u32[]{:S(2)}, u32[]{:S(2)}) collective-permute-start(bf16[256,2048]{1,0:T(8,128)(2,1)S(1)} %fusion.132), channel_id=1, source_target_pairs={{0,4},{1,5},{2,6},{3,7},{4,0},{5,1},{6,2},{7,3},{8,12},{9,13},{10,... | collective-permute-start | bytes 3145736 | tf_op jit(solution)/shard_map/ppermute | solution.py:122
  897.0 53.7 %collective-permute-start.90 = (bf16[8,288,512]{2,1,0:T(8,128)(2,1)}, bf16[8,288,512]{2,1,0:T(8,128)(2,1)}, u32[]{:S(2)}, u32[]{:S(2)}) collective-permute-start(bf16[8,288,512]{2,1,0:T(8,128)(2,1)} %pad_maximum_fusion.8), channel_id=1, source_target_pairs={{0,2},{1,3},{2,0},{3,1},{4,6},{5,7},{6,4},{7,5},{8,10},{9,11},{10,... | collective-permute-start | bytes 7077896 | tf_op jit(solution)/shard_map/ppermute | solution.py:122
  927.7 45.5 %collective-permute-start.89 = (bf16[256,2048]{1,0:T(8,128)(2,1)}, bf16[256,2048]{1,0:T(8,128)(2,1)}, u32[]{:S(2)}, u32[]{:S(2)}) collective-permute-start(bf16[256,2048]{1,0:T(8,128)(2,1)} %get-tuple-element.161), channel_id=1, source_target_pairs={{0,2},{1,3},{2,0},{3,1},{4,6},{5,7},{6,4},{7,5},{8,10},{9,11},{10,... | collective-permute-start | bytes 3145736 | tf_op jit(solution)/shard_map/ppermute | solution.py:122
  973.2 54.0 %collective-permute-start.95 = (bf16[8,288,512]{2,1,0:T(8,128)(2,1)}, bf16[8,288,512]{2,1,0:T(8,128)(2,1)}, u32[]{:S(2)}, u32[]{:S(2)}) collective-permute-start(bf16[8,288,512]{2,1,0:T(8,128)(2,1)} %pad_maximum_fusion.7), channel_id=1, source_target_pairs={{0,2},{1,3},{2,0},{3,1},{4,6},{5,7},{6,4},{7,5},{8,10},{9,11},{10,... | collective-permute-start | bytes 7077896 | tf_op jit(solution)/shard_map/ppermute | solution.py:122
  979.2 92.7 %all-to-all-start.5 = ((bf16[8,288,512]{2,1,0:T(8,128)(2,1)}), bf16[8,288,512]{2,1,0:T(8,128)(2,1)}, u32[]{:S(2)}, u32[]{:S(2)}) async-start(bf16[8,288,512]{2,1,0:T(8,128)(2,1)} %add_convert_fusion.2), calls=%async_computation.5 | async-start | bytes 4718592 | tf_op jit(solution)/shard_map/all_to_all | solution.py:219
  1065.6 98.7 %collective-permute-start.102 = (bf16[8,288,512]{2,1,0:T(8,128)(2,1)}, bf16[8,288,512]{2,1,0:T(8,128)(2,1)}, u32[]{:S(2)}, u32[]{:S(2)}) collective-permute-start(bf16[8,288,512]{2,1,0:T(8,128)(2,1)} %pad_maximum_fusion.9), channel_id=1, source_target_pairs={{0,2},{1,3},{2,0},{3,1},{4,6},{5,7},{6,4},{7,5},{8,10},{9,11},{10,... | collective-permute-start | bytes 7077896 | tf_op jit(solution)/shard_map/ppermute | solution.py:122
  1096.3 68.0 %all-to-all-start.6 = ((bf16[8,288,512]{2,1,0:T(8,128)(2,1)}), bf16[8,288,512]{2,1,0:T(8,128)(2,1)}, u32[]{:S(2)}, u32[]{:S(2)}) async-start(bf16[8,288,512]{2,1,0:T(8,128)(2,1)} %add_convert_fusion.1), calls=%async_computation.6 | async-start | bytes 4718592 | tf_op jit(solution)/shard_map/all_to_all | solution.py:219
  1164.0 58.5 %collective-permute-start.98 = (bf16[4,384,512]{2,1,0:T(8,128)(2,1)}, bf16[4,384,512]{2,1,0:T(8,128)(2,1)}, u32[]{:S(2)}, u32[]{:S(2)}) collective-permute-start(bf16[4,384,512]{2,1,0:T(8,128)(2,1)} %dynamic-slice_bitcast_fusion), channel_id=1, source_target_pairs={{0,4},{1,5},{2,6},{3,7},{4,0},{5,1},{6,2},{7,3},{8,12},{9,13},{10,... | collective-permute-start | bytes 4718600 | tf_op jit(solution)/shard_map/ppermute | solution.py:122
  1182.6 107.9 %collective-permute-start.103 = (bf16[4,1440,128]{2,1,0:T(8,128)(2,1)}, bf16[4,1440,128]{2,1,0:T(8,128)(2,1)}, u32[]{:S(2)}, u32[]{:S(2)}) collective-permute-start(bf16[4,1440,128]{2,1,0:T(8,128)(2,1)} %get-tuple-element.435), channel_id=1, source_target_pairs={{0,4},{1,5},{2,6},{3,7},{4,0},{5,1},{6,2},{7,3},{8,12},{9,13},{10,... | collective-permute-start | bytes 4423688 | tf_op jit(solution)/shard_map/ppermute | solution.py:122
  1188.1 78.0 %all-to-all-start.7 = ((bf16[8,288,512]{2,1,0:T(8,128)(2,1)}), bf16[8,288,512]{2,1,0:T(8,128)(2,1)}, u32[]{:S(2)}, u32[]{:S(2)}) async-start(bf16[8,288,512]{2,1,0:T(8,128)(2,1)} %add_convert_fusion), calls=%async_computation.7 | async-start | bytes 4718592 | tf_op jit(solution)/shard_map/all_to_all | solution.py:219
  1205.7 54.8 %collective-permute-start.104 = (bf16[512,2048]{1,0:T(8,128)(2,1)}, bf16[512,2048]{1,0:T(8,128)(2,1)}, u32[]{:S(2)}, u32[]{:S(2)}) collective-permute-start(bf16[512,2048]{1,0:T(8,128)(2,1)} %convolution_convert_fusion.3), channel_id=1, source_target_pairs={{0,1},{1,0},{2,3},{3,2},{4,5},{5,4},{6,7},{7,6},{8,9},{9,8},{10,11... | collective-permute-start | bytes 6291464 | tf_op jit(solution)/shard_map/ppermute | solution.py:122
  1225.4 71.5 %collective-permute-start.99 = (bf16[384,512]{1,0:T(8,128)(2,1)}, bf16[384,512]{1,0:T(8,128)(2,1)}, u32[]{:S(2)}, u32[]{:S(2)}) collective-permute-start(bf16[384,512]{1,0:T(8,128)(2,1)} %get-tuple-element.426), channel_id=1, source_target_pairs={{0,8},{1,9},{2,10},{3,11},{4,12},{5,13},{6,14},{7,15},{8,0},{9,1},... | collective-permute-start | bytes 1179656 | tf_op jit(solution)/shard_map/ppermute | solution.py:122
  1227.3 69.6 %collective-permute-start.100 = (bf16[384,512]{1,0:T(8,128)(2,1)}, bf16[384,512]{1,0:T(8,128)(2,1)}, u32[]{:S(2)}, u32[]{:S(2)}) collective-permute-start(bf16[384,512]{1,0:T(8,128)(2,1)} %get-tuple-element.425), channel_id=1, source_target_pairs={{0,16},{1,17},{2,18},{3,19},{4,20},{5,21},{6,22},{7,23},{8,24},{9,... | collective-permute-start | bytes 1179656 | tf_op jit(solution)/shard_map/ppermute | solution.py:122
  1229.8 30.0 %collective-permute-start.114 = (bf16[4,32,512]{2,1,0:T(8,128)(2,1)S(1)}, bf16[4,32,512]{2,1,0:T(8,128)(2,1)S(1)}, u32[]{:S(2)}, u32[]{:S(2)}) collective-permute-start(bf16[4,32,512]{2,1,0:T(8,128)(2,1)S(1)} %dynamic-slice_bitcast_fusion.5), channel_id=1, source_target_pairs={{0,4},{1,5},{2,6},{3,7},{4,0},{5,1},{6,2},{7,3},{8,12},{9,13},{10,... | collective-permute-start | bytes 393224 | tf_op jit(solution)/shard_map/ppermute | solution.py:122
  1259.8 37.1 %collective-permute-start.101 = (bf16[384,512]{1,0:T(8,128)(2,1)S(1)}, bf16[384,512]{1,0:T(8,128)(2,1)}, u32[]{:S(2)}, u32[]{:S(2)}) collective-permute-start(bf16[384,512]{1,0:T(8,128)(2,1)S(1)} %get-tuple-element.424), channel_id=1, source_target_pairs={{0,24},{1,25},{2,26},{3,27},{4,28},{5,29},{6,30},{7,31},{8,16},{9,... | collective-permute-start | bytes 1179656 | tf_op jit(solution)/shard_map/ppermute | solution.py:122
  1290.2 61.1 %collective-permute-start.115 = (bf16[32,512]{1,0:T(8,128)(2,1)}, bf16[32,512]{1,0:T(8,128)(2,1)}, u32[]{:S(2)}, u32[]{:S(2)}) collective-permute-start(bf16[32,512]{1,0:T(8,128)(2,1)} %get-tuple-element.494), channel_id=1, source_target_pairs={{0,8},{1,9},{2,10},{3,11},{4,12},{5,13},{6,14},{7,15},{8,0},{9,1},... | collective-permute-start | bytes 98312 | tf_op jit(solution)/shard_map/ppermute | solution.py:122
  (268 other events, 3699.9 us)
Sparse Core Ops, SparseCore 0:
  32.4 86.4 all-gather.2

commit v4 on v3

--- a/solution.py
+++ b/solution.py
@@ -584,15 +584,16 @@
             d_key = rotate(d_key, cosine_table, -sine_table)
             kv_pieces.append(jnp.concatenate([d_key, d_value], axis=1))
         d_q_lin = jnp.concatenate(q_pieces, axis=0)
-        up_got, gate_g, d_q_lin = lax.optimization_barrier((up_got, gate_g, d_q_lin))
-        up_g = owned(up_near[0], up_got)
+        up_got, d_q_lin = lax.optimization_barrier((up_got, d_q_lin))
         kv_blocks = jnp.concatenate(kv_pieces, axis=0).reshape(row_count, nx, nk, kv_width)
         d_kv_lin = scatter_cols(
             kv_blocks.transpose(1, 2, 0, 3), place_x, place_k, lambda block: block
         ).astype(BF)
         d_qkv = jnp.concatenate([d_q_lin, d_kv_lin], axis=1)
         near_two, sent = scatter_tokens(d_qkv, w_qkv)
-        up_g, sent = lax.optimization_barrier((up_g, sent))
+        gate_g, sent = lax.optimization_barrier((gate_g, sent))
+        up_mine, gate_g = lax.optimization_barrier((up_near[0], gate_g))
+        up_g = owned(up_mine, up_got)
         d_normed = finish_tokens(near_two, sent)
 
         def blocks_of(value):
@@ -644,7 +645,9 @@
             ),
             place_y,
         )
-        last_parts, d_normed = lax.optimization_barrier((last_parts, d_normed))
+        last_parts, rank_parts, d_normed = lax.optimization_barrier(
+            (last_parts, rank_parts, d_normed)
+        )
         last_parts = scatter_z(last_parts, place_z)
         rank_parts = scatter_z(rank_parts, place_z)
         d_norm_one, gain_one_part = norm_backward(d_normed, own_x, gain_one, own_scale)

time: 1410 us -> 1460 us (1.035)
  local copies, waits for them, and re-layouts: 243 us -> 264 us
  waiting for transfers between devices: 414 us -> 432 us
    ppermute x132, waiting for transfers between devices: 378 us -> 396 us  [permute(): return lax.ppermute(value, BOTH, pairs)]
    unnamed x453 -> x459, local copies, waits for them, and re-layouts: 132 us -> 138 us
  transfers between devices with their start and end apart: 141 -> 141, of which waited for: 43 -> 44; matrix products, arithmetic and copies ran while one was open for 51% -> 50% of each run, Pallas kernels for 0% -> 0%
where the time goes in v4:
time: 1460 us; the launch traced here: 1450 us
  waiting for transfers between devices  432 us (30%)
  matrix products  380 us (26%)
  local copies, waits for them, and re-layouts  264 us (18%)
  starting transfers between devices  183 us (13%)
  other arithmetic  169 us (12%)
  between operations  20.5 us (1%)
    ppermute x132, waiting for transfers between devices, permute(): return lax.ppermute(value, BOTH, pairs)  396 us
    dot_general x35, matrix products, product(): return jnp.dot(former, latter, preferred_element_type=F32)  169 us
    unnamed x459, local copies, waits for them, and re-layouts  138 us
    ppermute x132, starting transfers between devices, permute(): return lax.ppermute(value, BOTH, pairs)  131 us
    dot_general x16, matrix products, left_trans(): lax.dot_general(former, latter, (((0,), (0,)), ((), ())), preferred_eleme...  98.5 us
    dot_general x36, matrix products, right_trans(): lax.dot_general(former, latter, (((1,), (1,)), ((), ())), preferred_eleme...  92.9 us
    all_to_all x8, starting transfers between devices, exchange(): return lax.all_to_all(value, axis, 0, 0, tiled=True)  51.8 us
    all_to_all x8, waiting for transfers between devices, exchange(): return lax.all_to_all(value, axis, 0, 0, tiled=True)  36.2 us
  transfers between devices with their start and end apart: 141, of which 44 were waited for; matrix products, arithmetic and copies ran while one was open for 50% of the time, Pallas kernels for 0%

profile of v4, /device:TPU:0, one launch (start us, length us, event | category | flops | bytes accessed | tf_op | source)
XLA Modules:
  0.0 1448.1 jit_solution(12533166716590345403)
XLA Ops:
  22.8 6.0 all-to-all-start
  38.5 12.8 collective-permute-done.2
  51.3 7.4 collective-permute-start.3
  62.4 8.2 collective-permute-done.5
  70.6 17.3 %collective-permute-done.3 = bf16[288,896]{1,0:T(8,128)(2,1)} collective-permute-done((bf16[288,896]{1,0:T(8,128)(2,1)S(1)}, bf16[288,896]{1,0:T(8,128)(2,1)}, u32[]{:S(2)}, u32[]{:S(2)}) %collective-permute-start.3) | collective-permute-done | bytes 516128 | tf_op jit(solution)/shard_map/ppermute | solution.py:122
  87.9 17.8 %collective-permute-done.1 = bf16[288,896]{1,0:T(8,128)(2,1)} collective-permute-done((bf16[288,896]{1,0:T(8,128)(2,1)}, bf16[288,896]{1,0:T(8,128)(2,1)}, u32[]{:S(2)}, u32[]{:S(2)}) %collective-permute-start.1) | collective-permute-done | bytes 516128 | tf_op jit(solution)/shard_map/ppermute | solution.py:122
  153.0 6.6 fusion.145
  159.5 5.9 all-to-all-start.2
  170.4 13.6 collective-permute-done.21
  185.1 6.3 collective-permute-start.20
  218.6 16.9 %all-to-all-done.2 = bf16[8,256,512]{1,2,0:T(8,128)(2,1)} async-done(((bf16[8,256,512]{1,2,0:T(8,128)(2,1)}), bf16[8,256,512]{1,2,0:T(8,128)(2,1)}, u32[]{:S(2)}, u32[]{:S(2)}) %all-to-all-start.2) | async-done | bytes 2097184 | tf_op jit(solution)/shard_map/all_to_all | solution.py:219
  238.7 6.0 collective-permute-done.17
  260.2 13.1 copy.225
  286.1 16.3 %all-to-all-start.3 = ((bf16[8,256,512]{1,2,0:T(8,128)(2,1)}), bf16[8,256,512]{1,2,0:T(8,128)(2,1)}, u32[]{:S(2)}, u32[]{:S(2)}) async-start(bf16[8,256,512]{1,2,0:T(8,128)(2,1)} %bitcast.666), calls=%async_computation.3 | async-start | bytes 4194304 | tf_op jit(solution)/shard_map/all_to_all | solution.py:219
  309.4 23.7 %collective-permute-done.26 = bf16[256,2048]{1,0:T(8,128)(2,1)} collective-permute-done((bf16[256,2048]{1,0:T(8,128)(2,1)S(1)}, bf16[256,2048]{1,0:T(8,128)(2,1)}, u32[]{:S(2)}, u32[]{:S(2)}) %collective-permute-start.26) | collective-permute-done | bytes 1048608 | tf_op jit(solution)/shard_map/ppermute | solution.py:122
  335.7 15.7 %all-to-all-done.3 = bf16[8,256,512]{1,2,0:T(8,128)(2,1)} async-done(((bf16[8,256,512]{1,2,0:T(8,128)(2,1)}), bf16[8,256,512]{1,2,0:T(8,128)(2,1)}, u32[]{:S(2)}, u32[]{:S(2)}) %all-to-all-start.3) | async-done | bytes 2097184 | tf_op jit(solution)/shard_map/all_to_all | solution.py:219
  365.4 16.9 %collective-permute-done.28 = bf16[256,2048]{1,0:T(8,128)(2,1)} collective-permute-done((bf16[256,2048]{1,0:T(8,128)(2,1)}, bf16[256,2048]{1,0:T(8,128)(2,1)}, u32[]{:S(2)}, u32[]{:S(2)}) %collective-permute-start.28) | collective-permute-done | bytes 1048608 | tf_op jit(solution)/shard_map/ppermute | solution.py:122
  424.2 7.0 constant_dynamic-update-slice_fusion.55
  435.1 6.2 constant_dynamic-update-slice_fusion.54
  448.2 5.6 constant_dynamic-update-slice_fusion.53
  464.4 5.7 constant_dynamic-update-slice_fusion.52
  470.1 5.7 constant_dynamic-update-slice_fusion.51
  498.7 6.0 constant_dynamic-update-slice_fusion.50
  513.7 7.0 constant_dynamic-update-slice_fusion.49
  534.3 8.4 constant_dynamic-update-slice_fusion.48
  545.4 5.6 collective-permute-done.53
  564.0 9.4 collective-permute-done.48
  595.2 10.4 collective-permute-done.57
  619.7 16.3 %collective-permute-done.58 = bf16[256,2048]{1,0:T(8,128)(2,1)S(1)} collective-permute-done((bf16[256,2048]{1,0:T(8,128)(2,1)}, bf16[256,2048]{1,0:T(8,128)(2,1)S(1)}, u32[]{:S(2)}, u32[]{:S(2)}) %collective-permute-start.58) | collective-permute-done | bytes 1048608 | tf_op jit(solution)/shard_map/ppermute | solution.py:122
  655.6 13.4 collective-permute-done.59
  689.1 8.0 collective-permute-done.62
  699.9 6.7 constant_dynamic-update-slice_fusion.62
  709.0 6.9 constant_dynamic-update-slice_fusion.61
  733.8 8.5 constant_dynamic-update-slice_fusion.60
  742.6 8.0 constant_dynamic-update-slice_fusion.59
  772.9 8.8 constant_dynamic-update-slice_fusion.58
  781.7 9.0 constant_dynamic-update-slice_fusion.57
  790.7 5.6 fusion.326
  829.4 7.6 constant_dynamic-update-slice_fusion.56
  844.6 13.7 fusion.32
  864.9 13.6 fusion.35
  879.2 10.0 collective-permute-done.83
  889.3 17.1 %collective-permute-done.69 = bf16[256,2048]{1,0:T(8,128)(2,1)S(1)} collective-permute-done((bf16[256,2048]{1,0:T(8,128)(2,1)S(1)}, bf16[256,2048]{1,0:T(8,128)(2,1)S(1)}, u32[]{:S(2)}, u32[]{:S(2)}) %collective-permute-start.69) | collective-permute-done | bytes 1048608 | tf_op jit(solution)/shard_map/ppermute | solution.py:122
  924.1 10.9 collective-permute-done.88
  943.4 12.5 fusion.22
  958.4 6.4 collective-permute-done.90
  964.7 22.5 %collective-permute-done.89 = bf16[256,2048]{1,0:T(8,128)(2,1)} collective-permute-done((bf16[256,2048]{1,0:T(8,128)(2,1)}, bf16[256,2048]{1,0:T(8,128)(2,1)}, u32[]{:S(2)}, u32[]{:S(2)}) %collective-permute-start.89) | collective-permute-done | bytes 1048608 | tf_op jit(solution)/shard_map/ppermute | solution.py:122
  997.3 13.7 fusion.16
  1018.4 6.2 convolution_convert_fusion.4
  1024.6 16.6 %collective-permute-done.95 = bf16[8,288,512]{2,1,0:T(8,128)(2,1)} collective-permute-done((bf16[8,288,512]{2,1,0:T(8,128)(2,1)}, bf16[8,288,512]{2,1,0:T(8,128)(2,1)}, u32[]{:S(2)}, u32[]{:S(2)}) %collective-permute-start.95) | collective-permute-done | bytes 2359328 | tf_op jit(solution)/shard_map/ppermute | solution.py:122
  1041.2 13.6 fusion.38
  1057.9 12.6 fusion.41
  1094.1 5.8 fusion.183
  1138.3 5.6 copy.274
  1144.0 6.4 convolution_convert_fusion
  1219.3 11.1 collective-permute-done.97
  1251.0 5.5 all-to-all-start.7
  1256.5 29.9 %collective-permute-done.98 = bf16[4,384,512]{2,1,0:T(8,128)(2,1)} collective-permute-done((bf16[4,384,512]{2,1,0:T(8,128)(2,1)}, bf16[4,384,512]{2,1,0:T(8,128)(2,1)}, u32[]{:S(2)}, u32[]{:S(2)}) %collective-permute-start.98) | collective-permute-done | bytes 1572896 | tf_op jit(solution)/shard_map/ppermute | solution.py:122
  1289.6 6.6 collective-permute-start.100
  1304.2 32.8 %collective-permute-done.100 = bf16[384,512]{1,0:T(8,128)(2,1)S(1)} collective-permute-done((bf16[384,512]{1,0:T(8,128)(2,1)S(1)}, bf16[384,512]{1,0:T(8,128)(2,1)S(1)}, u32[]{:S(2)}, u32[]{:S(2)}) %collective-permute-start.100) | collective-permute-done | bytes 393248 | tf_op jit(solution)/shard_map/ppermute | solution.py:122
  1339.3 5.2 collective-permute-start.118
  1369.9 6.6 collective-permute-done.121
  1392.1 12.4 collective-permute-done.115
  1407.9 9.0 collective-permute-done.116
  (1006 shorter events, 735.2 us)
Async XLA Ops:
  12.2 39.1 %collective-permute-start.2 = (bf16[288,896]{1,0:T(8,128)(2,1)}, bf16[288,896]{1,0:T(8,128)(2,1)S(1)}, u32[]{:S(2)}, u32[]{:S(2)}) collective-permute-start(bf16[288,896]{1,0:T(8,128)(2,1)} %maximum_maximum_fusion), channel_id=1, source_target_pairs={{0,16},{1,17},{2,18},{3,19},{4,20},{5,21},{6,22},{7,23},{8,24},{9,... | collective-permute-start | bytes 1548296 | tf_op jit(solution)/shard_map/ppermute | solution.py:122
  14.8 43.9 %collective-permute-start = (bf16[288,896]{1,0:T(8,128)(2,1)}, bf16[288,896]{1,0:T(8,128)(2,1)}, u32[]{:S(2)}, u32[]{:S(2)}) collective-permute-start(bf16[288,896]{1,0:T(8,128)(2,1)} %maximum_maximum_fusion), channel_id=1, source_target_pairs={{0,24},{1,25},{2,26},{3,27},{4,28},{5,29},{6,30},{7,31},{8,16},{9,... | collective-permute-start | bytes 1548296 | tf_op jit(solution)/shard_map/ppermute | solution.py:122
  22.8 96.8 %all-to-all-start = ((bf16[8,256,512]{1,2,0:T(8,128)(2,1)}), bf16[8,256,512]{1,2,0:T(8,128)(2,1)S(1)}, u32[]{:S(2)}, u32[]{:S(2)}) async-start(bf16[8,256,512]{1,2,0:T(8,128)(2,1)} %bitcast.630), calls=%async_computation | async-start | bytes 4194304 | tf_op jit(solution)/shard_map/all_to_all | solution.py:219
  28.7 215.9 %all-gather.3.cloned.1.call-start = ((), (), s32[]{:S(2)}) async-start(), calls=%async_computation.8 | async-start | bytes 3244032 | tf_op jit(solution)/shard_map/all_gather | solution.py:285
  38.4 32.2 %collective-permute-start.5 = (bf16[288,896]{1,0:T(8,128)(2,1)S(1)}, bf16[288,896]{1,0:T(8,128)(2,1)}, u32[]{:S(2)}, u32[]{:S(2)}) collective-permute-start(bf16[288,896]{1,0:T(8,128)(2,1)S(1)} %collective-permute-done.4), channel_id=1, source_target_pairs={{0,4},{1,5},{2,6},{3,7},{4,0},{5,1},{6,2},{7,3},{8,12},{9,13},{10,... | collective-permute-start | bytes 1548296 | tf_op jit(solution)/shard_map/ppermute | solution.py:122
  51.3 36.6 %collective-permute-start.3 = (bf16[288,896]{1,0:T(8,128)(2,1)S(1)}, bf16[288,896]{1,0:T(8,128)(2,1)}, u32[]{:S(2)}, u32[]{:S(2)}) collective-permute-start(bf16[288,896]{1,0:T(8,128)(2,1)S(1)} %collective-permute-done.2), channel_id=1, source_target_pairs={{0,4},{1,5},{2,6},{3,7},{4,0},{5,1},{6,2},{7,3},{8,12},{9,13},{10,... | collective-permute-start | bytes 1548296 | tf_op jit(solution)/shard_map/ppermute | solution.py:122
  58.8 46.9 %collective-permute-start.1 = (bf16[288,896]{1,0:T(8,128)(2,1)}, bf16[288,896]{1,0:T(8,128)(2,1)}, u32[]{:S(2)}, u32[]{:S(2)}) collective-permute-start(bf16[288,896]{1,0:T(8,128)(2,1)} %collective-permute-done), channel_id=1, source_target_pairs={{0,4},{1,5},{2,6},{3,7},{4,0},{5,1},{6,2},{7,3},{8,12},{9,13},{10,... | collective-permute-start | bytes 1548296 | tf_op jit(solution)/shard_map/ppermute | solution.py:122
  59.3 50.9 %collective-permute-start.7 = (bf16[1024,512]{1,0:T(8,128)(2,1)}, bf16[1024,512]{1,0:T(8,128)(2,1)S(1)}, u32[]{:S(2)}, u32[]{:S(2)}) collective-permute-start(bf16[1024,512]{1,0:T(8,128)(2,1)} %param.22), channel_id=1, source_target_pairs={{0,2},{1,3},{2,0},{3,1},{4,6},{5,7},{6,4},{7,5},{8,10},{9,11},{10,... | collective-permute-start | bytes 3145736 | tf_op jit(solution)/shard_map/ppermute | solution.py:122
  62.3 49.3 %collective-permute-start.9 = (bf16[1024,512]{1,0:T(8,128)(2,1)}, bf16[1024,512]{1,0:T(8,128)(2,1)S(1)}, u32[]{:S(2)}, u32[]{:S(2)}) collective-permute-start(bf16[1024,512]{1,0:T(8,128)(2,1)} %param.22), channel_id=1, source_target_pairs={{0,1},{1,0},{2,3},{3,2},{4,5},{5,4},{6,7},{7,6},{8,9},{9,8},{10,11... | collective-permute-start | bytes 3145736 | tf_op jit(solution)/shard_map/ppermute | solution.py:122
  148.3 43.1 %collective-permute-start.15 = (f32[1024,128]{0,1:T(8,128)}, f32[1024,128]{0,1:T(8,128)}, u32[]{:S(2)}, u32[]{:S(2)}) collective-permute-start(f32[1024,128]{0,1:T(8,128)} %fusion.199), channel_id=1, source_target_pairs={{0,1},{1,0},{2,3},{3,2},{4,5},{5,4},{6,7},{7,6},{8,9},{9,8},{10,11... | collective-permute-start | bytes 1572872 | tf_op jit(solution)/shard_map/ppermute | solution.py:122
  150.5 33.5 %collective-permute-start.21 = (bf16[288,512]{0,1:T(8,128)(2,1)}, bf16[288,512]{0,1:T(8,128)(2,1)}, u32[]{:S(2)}, u32[]{:S(2)}) collective-permute-start(bf16[288,512]{0,1:T(8,128)(2,1)} %pad_maximum_fusion.19), channel_id=1, source_target_pairs={{0,16},{1,17},{2,18},{3,19},{4,20},{5,21},{6,22},{7,23},{8,24},{9,... | collective-permute-start | bytes 884744 | tf_op jit(solution)/shard_map/ppermute | solution.py:122
  152.9 32.3 %collective-permute-start.23 = (bf16[288,512]{0,1:T(8,128)(2,1)}, bf16[288,512]{0,1:T(8,128)(2,1)}, u32[]{:S(2)}, u32[]{:S(2)}) collective-permute-start(bf16[288,512]{0,1:T(8,128)(2,1)} %pad_maximum_fusion.19), channel_id=1, source_target_pairs={{0,24},{1,25},{2,26},{3,27},{4,28},{5,29},{6,30},{7,31},{8,16},{9,... | collective-permute-start | bytes 884744 | tf_op jit(solution)/shard_map/ppermute | solution.py:122
  153.0 38.5 %collective-permute-start.14 = (f32[1024,128]{0,1:T(8,128)}, f32[1024,128]{0,1:T(8,128)}, u32[]{:S(2)}, u32[]{:S(2)}) collective-permute-start(f32[1024,128]{0,1:T(8,128)} %collective-permute-done.13), channel_id=1, source_target_pairs={{0,1},{1,0},{2,3},{3,2},{4,5},{5,4},{6,7},{7,6},{8,9},{9,8},{10,11... | collective-permute-start | bytes 1572872 | tf_op jit(solution)/shard_map/ppermute | solution.py:122
  159.5 75.9 %all-to-all-start.2 = ((bf16[8,256,512]{1,2,0:T(8,128)(2,1)}), bf16[8,256,512]{1,2,0:T(8,128)(2,1)}, u32[]{:S(2)}, u32[]{:S(2)}) async-start(bf16[8,256,512]{1,2,0:T(8,128)(2,1)} %bitcast.631), calls=%async_computation.2 | async-start | bytes 4194304 | tf_op jit(solution)/shard_map/all_to_all | solution.py:219
  169.6 43.9 %collective-permute-start.18 = (bf16[288,512]{0,1:T(8,128)(2,1)}, bf16[288,512]{0,1:T(8,128)(2,1)}, u32[]{:S(2)}, u32[]{:S(2)}) collective-permute-start(bf16[288,512]{0,1:T(8,128)(2,1)} %pad_maximum_fusion.19), channel_id=1, source_target_pairs={{0,4},{1,5},{2,6},{3,7},{4,0},{5,1},{6,2},{7,3},{8,12},{9,13},{10,... | collective-permute-start | bytes 884744 | tf_op jit(solution)/shard_map/ppermute | solution.py:122
  184.0 54.7 %collective-permute-start.16 = (bf16[2048,512]{0,1:T(8,128)(2,1)S(1)}, bf16[2048,512]{0,1:T(8,128)(2,1)}, u32[]{:S(2)}, u32[]{:S(2)}) collective-permute-start(bf16[2048,512]{0,1:T(8,128)(2,1)S(1)} %bitcast.625), channel_id=1, source_target_pairs={{0,2},{1,3},{2,0},{3,1},{4,6},{5,7},{6,4},{7,5},{8,10},{9,11},{10,... | collective-permute-start | bytes 6291464 | tf_op jit(solution)/shard_map/ppermute | solution.py:122
  185.1 53.6 %collective-permute-start.20 = (bf16[288,512]{0,1:T(8,128)(2,1)}, bf16[288,512]{0,1:T(8,128)(2,1)}, u32[]{:S(2)}, u32[]{:S(2)}) collective-permute-start(bf16[288,512]{0,1:T(8,128)(2,1)} %collective-permute-done.19), channel_id=1, source_target_pairs={{0,4},{1,5},{2,6},{3,7},{4,0},{5,1},{6,2},{7,3},{8,12},{9,13},{10,... | collective-permute-start | bytes 884744 | tf_op jit(solution)/shard_map/ppermute | solution.py:122
  191.4 47.3 %collective-permute-start.22 = (bf16[288,512]{0,1:T(8,128)(2,1)}, bf16[288,512]{0,1:T(8,128)(2,1)}, u32[]{:S(2)}, u32[]{:S(2)}) collective-permute-start(bf16[288,512]{0,1:T(8,128)(2,1)} %collective-permute-done.21), channel_id=1, source_target_pairs={{0,4},{1,5},{2,6},{3,7},{4,0},{5,1},{6,2},{7,3},{8,12},{9,13},{10,... | collective-permute-start | bytes 884744 | tf_op jit(solution)/shard_map/ppermute | solution.py:122
  191.5 47.2 %collective-permute-start.24 = (bf16[288,512]{0,1:T(8,128)(2,1)}, bf16[288,512]{0,1:T(8,128)(2,1)}, u32[]{:S(2)}, u32[]{:S(2)}) collective-permute-start(bf16[288,512]{0,1:T(8,128)(2,1)} %collective-permute-done.23), channel_id=1, source_target_pairs={{0,4},{1,5},{2,6},{3,7},{4,0},{5,1},{6,2},{7,3},{8,12},{9,13},{10,... | collective-permute-start | bytes 884744 | tf_op jit(solution)/shard_map/ppermute | solution.py:122
  286.1 65.3 %all-to-all-start.3 = ((bf16[8,256,512]{1,2,0:T(8,128)(2,1)}), bf16[8,256,512]{1,2,0:T(8,128)(2,1)}, u32[]{:S(2)}, u32[]{:S(2)}) async-start(bf16[8,256,512]{1,2,0:T(8,128)(2,1)} %bitcast.666), calls=%async_computation.3 | async-start | bytes 4194304 | tf_op jit(solution)/shard_map/all_to_all | solution.py:219
  359.0 55.4 %collective-permute-start.27 = (bf16[2048,512]{0,1:T(8,128)(2,1)}, bf16[2048,512]{0,1:T(8,128)(2,1)}, u32[]{:S(2)}, u32[]{:S(2)}) collective-permute-start(bf16[2048,512]{0,1:T(8,128)(2,1)} %bitcast.238), channel_id=1, source_target_pairs={{0,2},{1,3},{2,0},{3,1},{4,6},{5,7},{6,4},{7,5},{8,10},{9,11},{10,... | collective-permute-start | bytes 6291464 | tf_op jit(solution)/shard_map/ppermute | solution.py:122
  360.7 39.7 %collective-permute-start.30 = (bf16[256,2048]{1,0:T(8,128)(2,1)}, bf16[256,2048]{1,0:T(8,128)(2,1)}, u32[]{:S(2)}, u32[]{:S(2)}) collective-permute-start(bf16[256,2048]{1,0:T(8,128)(2,1)} %get-tuple-element.358), channel_id=1, source_target_pairs={{0,1},{1,0},{2,3},{3,2},{4,5},{5,4},{6,7},{7,6},{8,9},{9,8},{10,11... | collective-permute-start | bytes 3145736 | tf_op jit(solution)/shard_map/ppermute | solution.py:122
  395.7 189.9 %all-to-all-start.4 = ((bf16[4,2,256,512]{3,2,1,0:T(8,128)(2,1)}), bf16[4,2,256,512]{3,2,1,0:T(8,128)(2,1)}, u32[]{:S(2)}, u32[]{:S(2)}) async-start(bf16[4,2,256,512]{3,2,1,0:T(8,128)(2,1)} %maximum_bitcast_fusion), calls=%async_computation.4 | async-start | bytes 4194304 | tf_op jit(solution)/shard_map/all_to_all | solution.py:219
  400.4 78.0 %collective-permute-start.32 = (bf16[2048,512]{0,1:T(8,128)(2,1)}, bf16[2048,512]{0,1:T(8,128)(2,1)S(1)}, u32[]{:S(2)}, u32[]{:S(2)}) collective-permute-start(bf16[2048,512]{0,1:T(8,128)(2,1)} %bitcast.627), channel_id=1, source_target_pairs={{0,2},{1,3},{2,0},{3,1},{4,6},{5,7},{6,4},{7,5},{8,10},{9,11},{10,... | collective-permute-start | bytes 6291464 | tf_op jit(solution)/shard_map/ppermute | solution.py:122
  409.4 32.0 %collective-permute-start.54 = (bf16[256,2048]{1,0:T(8,128)(2,1)}, bf16[256,2048]{1,0:T(8,128)(2,1)S(1)}, u32[]{:S(2)}, u32[]{:S(2)}) collective-permute-start(bf16[256,2048]{1,0:T(8,128)(2,1)} %collective-permute-done.29), channel_id=1, source_target_pairs={{0,1},{1,0},{2,3},{3,2},{4,5},{5,4},{6,7},{7,6},{8,9},{9,8},{10,11... | collective-permute-start | bytes 3145736 | tf_op jit(solution)/shard_map/ppermute | solution.py:122
  410.9 42.8 %collective-permute-start.35 = (bf16[256,2048]{1,0:T(8,128)(2,1)}, bf16[256,2048]{1,0:T(8,128)(2,1)S(1)}, u32[]{:S(2)}, u32[]{:S(2)}) collective-permute-start(bf16[256,2048]{1,0:T(8,128)(2,1)} %collective-permute-done.34), channel_id=1, source_target_pairs={{0,4},{1,5},{2,6},{3,7},{4,0},{5,1},{6,2},{7,3},{8,12},{9,13},{10,... | collective-permute-start | bytes 3145736 | tf_op jit(solution)/shard_map/ppermute | solution.py:122
  412.4 41.4 %collective-permute-start.36 = (bf16[256,2048]{1,0:T(8,128)(2,1)}, bf16[256,2048]{1,0:T(8,128)(2,1)}, u32[]{:S(2)}, u32[]{:S(2)}) collective-permute-start(bf16[256,2048]{1,0:T(8,128)(2,1)} %collective-permute-done.34), channel_id=1, source_target_pairs={{0,8},{1,25},{2,10},{3,27},{4,12},{5,29},{6,14},{7,31},{8,16},{9,1... | collective-permute-start | bytes 3145736 | tf_op jit(solution)/shard_map/ppermute | solution.py:122
  414.3 46.2 %collective-permute-start.49 = (bf16[256,2048]{1,0:T(8,128)(2,1)}, bf16[256,2048]{1,0:T(8,128)(2,1)S(1)}, u32[]{:S(2)}, u32[]{:S(2)}) collective-permute-start(bf16[256,2048]{1,0:T(8,128)(2,1)} %collective-permute-done.34), channel_id=1, source_target_pairs={{0,1},{1,0},{2,3},{3,2},{4,5},{5,4},{6,7},{7,6},{8,9},{9,8},{10,11... | collective-permute-start | bytes 3145736 | tf_op jit(solution)/shard_map/ppermute | solution.py:122
  454.3 58.9 %collective-permute-start.41 = (bf16[256,2048]{1,0:T(8,128)(2,1)}, bf16[256,2048]{1,0:T(8,128)(2,1)S(1)}, u32[]{:S(2)}, u32[]{:S(2)}) collective-permute-start(bf16[256,2048]{1,0:T(8,128)(2,1)} %collective-permute-done.36), channel_id=1, source_target_pairs={{0,4},{1,5},{2,6},{3,7},{4,0},{5,1},{6,2},{7,3},{8,12},{9,13},{10,... | collective-permute-start | bytes 3145736 | tf_op jit(solution)/shard_map/ppermute | solution.py:122
  493.2 52.2 %collective-permute-start.55 = (bf16[256,2048]{1,0:T(8,128)(2,1)}, bf16[256,2048]{1,0:T(8,128)(2,1)}, u32[]{:S(2)}, u32[]{:S(2)}) collective-permute-start(bf16[256,2048]{1,0:T(8,128)(2,1)} %slice.868), channel_id=1, source_target_pairs={{0,1},{1,0},{2,3},{3,2},{4,5},{5,4},{6,7},{7,6},{8,9},{9,8},{10,11... | collective-permute-start | bytes 3145736 | tf_op jit(solution)/shard_map/ppermute | solution.py:122
  498.3 64.3 %collective-permute-start.50 = (bf16[256,2048]{1,0:T(8,128)(2,1)}, bf16[256,2048]{1,0:T(8,128)(2,1)}, u32[]{:S(2)}, u32[]{:S(2)}) collective-permute-start(bf16[256,2048]{1,0:T(8,128)(2,1)} %slice.870), channel_id=1, source_target_pairs={{0,1},{1,0},{2,3},{3,2},{4,5},{5,4},{6,7},{7,6},{8,9},{9,8},{10,11... | collective-permute-start | bytes 3145736 | tf_op jit(solution)/shard_map/ppermute | solution.py:122
  529.2 44.2 %collective-permute-start.48 = (bf16[256,2048]{1,0:T(8,128)(2,1)}, bf16[256,2048]{1,0:T(8,128)(2,1)S(1)}, u32[]{:S(2)}, u32[]{:S(2)}) collective-permute-start(bf16[256,2048]{1,0:T(8,128)(2,1)} %fusion.139), channel_id=1, source_target_pairs={{0,4},{1,5},{2,6},{3,7},{4,0},{5,1},{6,2},{7,3},{8,12},{9,13},{10,... | collective-permute-start | bytes 3145736 | tf_op jit(solution)/shard_map/ppermute | solution.py:122
  556.7 37.0 %collective-permute-start.45 = (bf16[256,2048]{1,0:T(8,128)(2,1)}, bf16[256,2048]{1,0:T(8,128)(2,1)}, u32[]{:S(2)}, u32[]{:S(2)}) collective-permute-start(bf16[256,2048]{1,0:T(8,128)(2,1)} %slice.872), channel_id=1, source_target_pairs={{0,1},{1,0},{2,3},{3,2},{4,5},{5,4},{6,7},{7,6},{8,9},{9,8},{10,11... | collective-permute-start | bytes 3145736 | tf_op jit(solution)/shard_map/ppermute | solution.py:122
  562.6 32.6 %collective-permute-start.44 = (bf16[256,2048]{1,0:T(8,128)(2,1)}, bf16[256,2048]{1,0:T(8,128)(2,1)}, u32[]{:S(2)}, u32[]{:S(2)}) collective-permute-start(bf16[256,2048]{1,0:T(8,128)(2,1)} %fusion.143), channel_id=1, source_target_pairs={{0,4},{1,5},{2,6},{3,7},{4,0},{5,1},{6,2},{7,3},{8,12},{9,13},{10,... | collective-permute-start | bytes 3145736 | tf_op jit(solution)/shard_map/ppermute | solution.py:122
  588.3 31.3 %collective-permute-start.40 = (bf16[256,2048]{1,0:T(8,128)(2,1)}, bf16[256,2048]{1,0:T(8,128)(2,1)S(1)}, u32[]{:S(2)}, u32[]{:S(2)}) collective-permute-start(bf16[256,2048]{1,0:T(8,128)(2,1)} %slice.874), channel_id=1, source_target_pairs={{0,1},{1,0},{2,3},{3,2},{4,5},{5,4},{6,7},{7,6},{8,9},{9,8},{10,11... | collective-permute-start | bytes 3145736 | tf_op jit(solution)/shard_map/ppermute | solution.py:122
  671.3 35.3 %collective-permute-start.80 = (bf16[256,2048]{1,0:T(8,128)(2,1)}, bf16[256,2048]{1,0:T(8,128)(2,1)S(1)}, u32[]{:S(2)}, u32[]{:S(2)}) collective-permute-start(bf16[256,2048]{1,0:T(8,128)(2,1)} %collective-permute-done.60), channel_id=1, source_target_pairs={{0,1},{1,0},{2,3},{3,2},{4,5},{5,4},{6,7},{7,6},{8,9},{9,8},{10,11... | collective-permute-start | bytes 3145736 | tf_op jit(solution)/shard_map/ppermute | solution.py:122
  683.1 241.0 %collective-permute-start.87 = (bf16[256,2048]{1,0:T(8,128)(2,1)}, bf16[256,2048]{1,0:T(8,128)(2,1)}, u32[]{:S(2)}, u32[]{:S(2)}) collective-permute-start(bf16[256,2048]{1,0:T(8,128)(2,1)} %slice.860), channel_id=1, source_target_pairs={{0,1},{1,0},{2,3},{3,2},{4,5},{5,4},{6,7},{7,6},{8,9},{9,8},{10,11... | collective-permute-start | bytes 3145736 | tf_op jit(solution)/shard_map/ppermute | solution.py:122
  698.9 43.4 %collective-permute-start.75 = (bf16[256,2048]{1,0:T(8,128)(2,1)S(1)}, bf16[256,2048]{1,0:T(8,128)(2,1)S(1)}, u32[]{:S(2)}, u32[]{:S(2)}) collective-permute-start(bf16[256,2048]{1,0:T(8,128)(2,1)S(1)} %collective-permute-done.63), channel_id=1, source_target_pairs={{0,1},{1,0},{2,3},{3,2},{4,5},{5,4},{6,7},{7,6},{8,9},{9,8},{10,11... | collective-permute-start | bytes 3145736 | tf_op jit(solution)/shard_map/ppermute | solution.py:122
  698.9 34.3 %collective-permute-start.64 = (bf16[256,2048]{1,0:T(8,128)(2,1)S(1)}, bf16[256,2048]{1,0:T(8,128)(2,1)}, u32[]{:S(2)}, u32[]{:S(2)}) collective-permute-start(bf16[256,2048]{1,0:T(8,128)(2,1)S(1)} %collective-permute-done.63), channel_id=1, source_target_pairs={{0,4},{1,5},{2,6},{3,7},{4,0},{5,1},{6,2},{7,3},{8,12},{9,13},{10,... | collective-permute-start | bytes 3145736 | tf_op jit(solution)/shard_map/ppermute | solution.py:122
  699.7 33.5 %collective-permute-start.65 = (bf16[256,2048]{1,0:T(8,128)(2,1)S(1)}, bf16[256,2048]{1,0:T(8,128)(2,1)}, u32[]{:S(2)}, u32[]{:S(2)}) collective-permute-start(bf16[256,2048]{1,0:T(8,128)(2,1)S(1)} %collective-permute-done.63), channel_id=1, source_target_pairs={{0,8},{1,25},{2,10},{3,27},{4,12},{5,29},{6,14},{7,31},{8,16},{9,1... | collective-permute-start | bytes 3145736 | tf_op jit(solution)/shard_map/ppermute | solution.py:122
  733.1 87.5 %collective-permute-start.81 = (bf16[256,2048]{1,0:T(8,128)(2,1)}, bf16[256,2048]{1,0:T(8,128)(2,1)}, u32[]{:S(2)}, u32[]{:S(2)}) collective-permute-start(bf16[256,2048]{1,0:T(8,128)(2,1)} %slice.862), channel_id=1, source_target_pairs={{0,1},{1,0},{2,3},{3,2},{4,5},{5,4},{6,7},{7,6},{8,9},{9,8},{10,11... | collective-permute-start | bytes 3145736 | tf_op jit(solution)/shard_map/ppermute | solution.py:122
  733.7 48.0 %collective-permute-start.70 = (bf16[256,2048]{1,0:T(8,128)(2,1)}, bf16[256,2048]{1,0:T(8,128)(2,1)}, u32[]{:S(2)}, u32[]{:S(2)}) collective-permute-start(bf16[256,2048]{1,0:T(8,128)(2,1)} %collective-permute-done.65), channel_id=1, source_target_pairs={{0,1},{1,0},{2,3},{3,2},{4,5},{5,4},{6,7},{7,6},{8,9},{9,8},{10,11... | collective-permute-start | bytes 3145736 | tf_op jit(solution)/shard_map/ppermute | solution.py:122
  742.3 76.0 %collective-permute-start.66 = (bf16[256,2048]{1,0:T(8,128)(2,1)}, bf16[256,2048]{1,0:T(8,128)(2,1)}, u32[]{:S(2)}, u32[]{:S(2)}) collective-permute-start(bf16[256,2048]{1,0:T(8,128)(2,1)} %collective-permute-done.65), channel_id=1, source_target_pairs={{0,4},{1,5},{2,6},{3,7},{4,0},{5,1},{6,2},{7,3},{8,12},{9,13},{10,... | collective-permute-start | bytes 3145736 | tf_op jit(solution)/shard_map/ppermute | solution.py:122
  818.3 39.9 %collective-permute-start.76 = (bf16[256,2048]{1,0:T(8,128)(2,1)}, bf16[256,2048]{1,0:T(8,128)(2,1)}, u32[]{:S(2)}, u32[]{:S(2)}) collective-permute-start(bf16[256,2048]{1,0:T(8,128)(2,1)} %slice.864), channel_id=1, source_target_pairs={{0,1},{1,0},{2,3},{3,2},{4,5},{5,4},{6,7},{7,6},{8,9},{9,8},{10,11... | collective-permute-start | bytes 3145736 | tf_op jit(solution)/shard_map/ppermute | solution.py:122
  825.9 33.7 %collective-permute-start.82 = (bf16[256,2048]{1,0:T(8,128)(2,1)}, bf16[256,2048]{1,0:T(8,128)(2,1)}, u32[]{:S(2)}, u32[]{:S(2)}) collective-permute-start(bf16[256,2048]{1,0:T(8,128)(2,1)} %fusion.123), channel_id=1, source_target_pairs={{0,8},{1,25},{2,10},{3,27},{4,12},{5,29},{6,14},{7,31},{8,16},{9,1... | collective-permute-start | bytes 3145736 | tf_op jit(solution)/shard_map/ppermute | solution.py:122
  858.3 65.8 %collective-permute-start.86 = (bf16[256,2048]{1,0:T(8,128)(2,1)}, bf16[256,2048]{1,0:T(8,128)(2,1)}, u32[]{:S(2)}, u32[]{:S(2)}) collective-permute-start(bf16[256,2048]{1,0:T(8,128)(2,1)} %fusion.121), channel_id=1, source_target_pairs={{0,4},{1,5},{2,6},{3,7},{4,0},{5,1},{6,2},{7,3},{8,12},{9,13},{10,... | collective-permute-start | bytes 3145736 | tf_op jit(solution)/shard_map/ppermute | solution.py:122
  863.2 43.1 %collective-permute-start.69 = (bf16[256,2048]{1,0:T(8,128)(2,1)S(1)}, bf16[256,2048]{1,0:T(8,128)(2,1)S(1)}, u32[]{:S(2)}, u32[]{:S(2)}) collective-permute-start(bf16[256,2048]{1,0:T(8,128)(2,1)S(1)} %fusion.132), channel_id=1, source_target_pairs={{0,4},{1,5},{2,6},{3,7},{4,0},{5,1},{6,2},{7,3},{8,12},{9,13},{10,... | collective-permute-start | bytes 3145736 | tf_op jit(solution)/shard_map/ppermute | solution.py:122
  911.0 53.7 %collective-permute-start.90 = (bf16[8,288,512]{2,1,0:T(8,128)(2,1)}, bf16[8,288,512]{2,1,0:T(8,128)(2,1)}, u32[]{:S(2)}, u32[]{:S(2)}) collective-permute-start(bf16[8,288,512]{2,1,0:T(8,128)(2,1)} %pad_maximum_fusion.8), channel_id=1, source_target_pairs={{0,2},{1,3},{2,0},{3,1},{4,6},{5,7},{6,4},{7,5},{8,10},{9,11},{10,... | collective-permute-start | bytes 7077896 | tf_op jit(solution)/shard_map/ppermute | solution.py:122
  941.7 45.5 %collective-permute-start.89 = (bf16[256,2048]{1,0:T(8,128)(2,1)}, bf16[256,2048]{1,0:T(8,128)(2,1)}, u32[]{:S(2)}, u32[]{:S(2)}) collective-permute-start(bf16[256,2048]{1,0:T(8,128)(2,1)} %get-tuple-element.164), channel_id=1, source_target_pairs={{0,2},{1,3},{2,0},{3,1},{4,6},{5,7},{6,4},{7,5},{8,10},{9,11},{10,... | collective-permute-start | bytes 3145736 | tf_op jit(solution)/shard_map/ppermute | solution.py:122
  987.2 54.0 %collective-permute-start.95 = (bf16[8,288,512]{2,1,0:T(8,128)(2,1)}, bf16[8,288,512]{2,1,0:T(8,128)(2,1)}, u32[]{:S(2)}, u32[]{:S(2)}) collective-permute-start(bf16[8,288,512]{2,1,0:T(8,128)(2,1)} %pad_maximum_fusion.7), channel_id=1, source_target_pairs={{0,2},{1,3},{2,0},{3,1},{4,6},{5,7},{6,4},{7,5},{8,10},{9,11},{10,... | collective-permute-start | bytes 7077896 | tf_op jit(solution)/shard_map/ppermute | solution.py:122
  993.3 97.7 %all-to-all-start.5 = ((bf16[8,288,512]{2,1,0:T(8,128)(2,1)}), bf16[8,288,512]{2,1,0:T(8,128)(2,1)S(1)}, u32[]{:S(2)}, u32[]{:S(2)}) async-start(bf16[8,288,512]{2,1,0:T(8,128)(2,1)} %add_convert_fusion.2), calls=%async_computation.5 | async-start | bytes 4718592 | tf_op jit(solution)/shard_map/all_to_all | solution.py:219
  1082.2 61.7 %collective-permute-start.102 = (bf16[8,288,512]{2,1,0:T(8,128)(2,1)}, bf16[8,288,512]{2,1,0:T(8,128)(2,1)}, u32[]{:S(2)}, u32[]{:S(2)}) collective-permute-start(bf16[8,288,512]{2,1,0:T(8,128)(2,1)} %pad_maximum_fusion.9), channel_id=1, source_target_pairs={{0,2},{1,3},{2,0},{3,1},{4,6},{5,7},{6,4},{7,5},{8,10},{9,11},{10,... | collective-permute-start | bytes 7077896 | tf_op jit(solution)/shard_map/ppermute | solution.py:122
  1121.0 112.1 %all-to-all-start.6 = ((bf16[8,288,512]{2,1,0:T(8,128)(2,1)}), bf16[8,288,512]{2,1,0:T(8,128)(2,1)}, u32[]{:S(2)}, u32[]{:S(2)}) async-start(bf16[8,288,512]{2,1,0:T(8,128)(2,1)} %add_convert_fusion.1), calls=%async_computation.6 | async-start | bytes 4718592 | tf_op jit(solution)/shard_map/all_to_all | solution.py:219
  1162.7 46.9 %collective-permute-start.96 = (bf16[2,768,512]{2,1,0:T(8,128)(2,1)}, bf16[2,768,512]{2,1,0:T(8,128)(2,1)}, u32[]{:S(2)}, u32[]{:S(2)}) collective-permute-start(bf16[2,768,512]{2,1,0:T(8,128)(2,1)} %fusion.180), channel_id=1, source_target_pairs={{0,1},{1,0},{2,3},{3,2},{4,5},{5,4},{6,7},{7,6},{8,9},{9,8},{10,11... | collective-permute-start | bytes 4718600 | tf_op jit(solution)/shard_map/ppermute | solution.py:122
  1198.8 99.4 %collective-permute-start.103 = (bf16[4,1440,128]{2,1,0:T(8,128)(2,1)}, bf16[4,1440,128]{2,1,0:T(8,128)(2,1)}, u32[]{:S(2)}, u32[]{:S(2)}) collective-permute-start(bf16[4,1440,128]{2,1,0:T(8,128)(2,1)} %get-tuple-element.420), channel_id=1, source_target_pairs={{0,4},{1,5},{2,6},{3,7},{4,0},{5,1},{6,2},{7,3},{8,12},{9,13},{10,... | collective-permute-start | bytes 4423688 | tf_op jit(solution)/shard_map/ppermute | solution.py:122
  1214.0 84.2 %collective-permute-start.106 = (bf16[4,32,512]{2,1,0:T(8,128)(2,1)S(1)}, bf16[4,32,512]{2,1,0:T(8,128)(2,1)S(1)}, u32[]{:S(2)}, u32[]{:S(2)}) collective-permute-start(bf16[4,32,512]{2,1,0:T(8,128)(2,1)S(1)} %get-tuple-element.482), channel_id=1, source_target_pairs={{0,4},{1,5},{2,6},{3,7},{4,0},{5,1},{6,2},{7,3},{8,12},{9,13},{10,... | collective-permute-start | bytes 393224 | tf_op jit(solution)/shard_map/ppermute | solution.py:122
  1232.5 53.9 %collective-permute-start.98 = (bf16[4,384,512]{2,1,0:T(8,128)(2,1)}, bf16[4,384,512]{2,1,0:T(8,128)(2,1)}, u32[]{:S(2)}, u32[]{:S(2)}) collective-permute-start(bf16[4,384,512]{2,1,0:T(8,128)(2,1)} %dynamic-slice_bitcast_fusion), channel_id=1, source_target_pairs={{0,4},{1,5},{2,6},{3,7},{4,0},{5,1},{6,2},{7,3},{8,12},{9,13},{10,... | collective-permute-start | bytes 4718600 | tf_op jit(solution)/shard_map/ppermute | solution.py:122
  1233.1 63.3 %collective-permute-start.108 = (bf16[256,2048]{1,0:T(8,128)(2,1)}, bf16[256,2048]{1,0:T(8,128)(2,1)}, u32[]{:S(2)}, u32[]{:S(2)}) collective-permute-start(bf16[256,2048]{1,0:T(8,128)(2,1)} %fusion.193), channel_id=1, source_target_pairs={{0,2},{1,3},{2,0},{3,1},{4,6},{5,7},{6,4},{7,5},{8,10},{9,11},{10,... | collective-permute-start | bytes 3145736 | tf_op jit(solution)/shard_map/ppermute | solution.py:122
  1251.0 177.3 %all-to-all-start.7 = ((bf16[8,288,512]{2,1,0:T(8,128)(2,1)}), bf16[8,288,512]{2,1,0:T(8,128)(2,1)}, u32[]{:S(2)}, u32[]{:S(2)}) async-start(bf16[8,288,512]{2,1,0:T(8,128)(2,1)} %add_convert_fusion), calls=%async_computation.7 | async-start | bytes 4718592 | tf_op jit(solution)/shard_map/all_to_all | solution.py:219
  1289.6 47.4 %collective-permute-start.100 = (bf16[384,512]{1,0:T(8,128)(2,1)S(1)}, bf16[384,512]{1,0:T(8,128)(2,1)S(1)}, u32[]{:S(2)}, u32[]{:S(2)}) collective-permute-start(bf16[384,512]{1,0:T(8,128)(2,1)S(1)} %get-tuple-element.410), channel_id=1, source_target_pairs={{0,16},{1,17},{2,18},{3,19},{4,20},{5,21},{6,22},{7,23},{8,24},{9,... | collective-permute-start | bytes 1179656 | tf_op jit(solution)/shard_map/ppermute | solution.py:122
  1296.4 40.6 %collective-permute-start.101 = (bf16[384,512]{1,0:T(8,128)(2,1)S(1)}, bf16[384,512]{1,0:T(8,128)(2,1)S(1)}, u32[]{:S(2)}, u32[]{:S(2)}) collective-permute-start(bf16[384,512]{1,0:T(8,128)(2,1)S(1)} %get-tuple-element.409), channel_id=1, source_target_pairs={{0,24},{1,25},{2,26},{3,27},{4,28},{5,29},{6,30},{7,31},{8,16},{9,... | collective-permute-start | bytes 1179656 | tf_op jit(solution)/shard_map/ppermute | solution.py:122
  1378.3 38.7 %collective-permute-start.112 = (bf16[1440,128]{1,0:T(8,128)(2,1)}, bf16[1440,128]{1,0:T(8,128)(2,1)S(1)}, u32[]{:S(2)}, u32[]{:S(2)}) collective-permute-start(bf16[1440,128]{1,0:T(8,128)(2,1)} %get-tuple-element.419), channel_id=1, source_target_pairs={{0,8},{1,9},{2,10},{3,11},{4,12},{5,13},{6,14},{7,15},{8,0},{9,1},... | collective-permute-start | bytes 1105928 | tf_op jit(solution)/shard_map/ppermute | solution.py:122
  1379.0 38.0 %collective-permute-start.113 = (bf16[1440,128]{1,0:T(8,128)(2,1)}, bf16[1440,128]{1,0:T(8,128)(2,1)S(1)}, u32[]{:S(2)}, u32[]{:S(2)}) collective-permute-start(bf16[1440,128]{1,0:T(8,128)(2,1)} %get-tuple-element.418), channel_id=1, source_target_pairs={{0,16},{1,17},{2,18},{3,19},{4,20},{5,21},{6,22},{7,23},{8,24},{9,... | collective-permute-start | bytes 1105928 | tf_op jit(solution)/shard_map/ppermute | solution.py:122
  1382.5 34.5 %collective-permute-start.114 = (bf16[1440,128]{1,0:T(8,128)(2,1)S(1)}, bf16[1440,128]{1,0:T(8,128)(2,1)S(1)}, u32[]{:S(2)}, u32[]{:S(2)}) collective-permute-start(bf16[1440,128]{1,0:T(8,128)(2,1)S(1)} %copy-done.116), channel_id=1, source_target_pairs={{0,24},{1,25},{2,26},{3,27},{4,28},{5,29},{6,30},{7,31},{8,16},{9,... | collective-permute-start | bytes 1105928 | tf_op jit(solution)/shard_map/ppermute | solution.py:122
  (270 other events, 3835.1 us)
Sparse Core Ops, SparseCore 0:
  32.4 86.4 all-gather.2
